TPU v7x, 1024 devices: a whole 8x8x8 slice. The times are simulated.
1024 devices in a mesh: ctx: 64 (over x, y_hi, core), fsdp: 8 (over z), batch: 2 (over y_lo).
Axes of the slice: x: 8, y: 8 (y_hi: 4, y_lo: 2; y = y_hi * 2 + y_lo), z: 8, core: 2. Of those that a mesh axis runs over, the one named last changes fastest.
Arguments:
- inputs: bfloat16 [2, 8192, 4096], P('batch', 'ctx'), may hold values from -6 to 6
- values: bfloat16 [2, 8192, 2048], P('batch', 'ctx', 'fsdp'), may hold values from -6 to 6
- w_qk: bfloat16 [4096, 256], P('fsdp'), may hold values from -0.09375 to 0.09375
- conv_qk: float32 [3, 256], P(None, 'fsdp'), may hold values from -3 to 3
- conv_v: float32 [3, 2048], P(None, 'fsdp'), may hold values from -3 to 3
- d_attn: bfloat16 [2, 8192, 2048], P('batch', 'ctx', 'fsdp'), may hold values from -6 to 6
Outputs:
- attended: bfloat16 [2, 8192, 2048], P('batch', 'ctx', 'fsdp')
- grad_v: bfloat16 [2, 8192, 2048], P('batch', 'ctx', 'fsdp')
- grad_w: float32 [4096, 256], P(('ctx', 'batch'), 'fsdp')
All inputs are finite; a program needn't handle non-finite values.
Results may differ from a plain program's by a relative error of at most 0.013.
Values may be sent and summed in bfloat16 or wider, within the bound.
No kernel may reach another device: no remote copies, remote signals or barrier semaphores. Data moves between devices by JAX's collectives and lax.ppermute only.
A program may use at most 32 MiB of HBM per device.

v0:
```python
import jax
import jax.numpy as jnp
import numpy as np
from jax import lax
from jax.sharding import Mesh
from jax.sharding import PartitionSpec as P

F = 16
E = 256
CONV = 3
CTX = ("ctx_0", "ctx_1", "ctx_2")
CTX_BATCH = ("ctx_0", "ctx_1", "ctx_2", "batch")


eps_norm = 1e-05


def from_behind(value, axis, by):
    size = lax.axis_size(axis)
    pairs = [(i, i + by) for i in range(size) if 0 <= i + by < size]
    return lax.ppermute(value, axis, pairs)


def neutral_like(value, identity):
    return jnp.broadcast_to(jnp.asarray(identity, value.dtype), value.shape)


def carried_in(value, axes, combine, identity, reverse):
    before = start = neutral_like(value, identity)
    running = value
    for axis in reversed(axes):
        size, here = (lax.axis_size(axis), lax.axis_index(axis))
        pieces = lax.all_gather(
            running.astype(jnp.bfloat16 if value.dtype == jnp.float32 else value.dtype), axis
        )
        inside, running = (start, start)
        for k in reversed(range(size)) if reverse else range(size):
            passed = k > here if reverse else k < here
            running = combine(running, pieces[k].astype(value.dtype))
            inside = jnp.where(passed, running, inside)
        before = combine(inside, before)
    return before


def in_blocks(value, dim, size):
    before, after = (value.shape[:dim], value.shape[dim + 1 :])
    return jnp.moveaxis(value.reshape(*before, size, -1, *after), dim, 0)


def summed_on_arrival(value, axis, dim):
    parts = in_blocks(value, dim, lax.axis_size(axis))
    arrived = lax.all_to_all(parts, axis, split_axis=0, concat_axis=0, tiled=True)
    return arrived.sum(axis=0)


def expand_tables():
    leading_table = np.zeros((F, F * F), np.float32)
    trailing_table = np.zeros((F, F * F), np.float32)
    for first_at in range(F):
        for second_at in range(F):
            leading_table[first_at, first_at * F + second_at] = 1.0
            trailing_table[second_at, first_at * F + second_at] = 1.0
    return (jnp.asarray(leading_table), jnp.asarray(trailing_table))


def features(vector, leading_table, trailing_table):
    leading = vector.shape[:-1]
    first_rep = jnp.einsum("htf,fk->htk", vector, leading_table)
    second_rep = jnp.einsum("htf,fk->htk", vector, trailing_table)
    constant = jnp.ones(leading + (1,), jnp.float32)
    return jnp.concatenate(
        [constant, vector * F ** (-0.25), first_rep * second_rep * (2.0 * F) ** (-0.5)], axis=-1
    )


def features_back(vector, upstream, leading_table, trailing_table):
    linear = upstream[..., 1 : 1 + F]
    square = upstream[..., 1 + F :]
    first_rep = jnp.einsum("htf,fk->htk", vector, leading_table)
    second_rep = jnp.einsum("htf,fk->htk", vector, trailing_table)
    paired = jnp.einsum("htk,fk->htf", square * second_rep, leading_table)
    paired = paired + jnp.einsum("htk,fk->htf", square * first_rep, trailing_table)
    return linear * F ** (-0.25) + paired * (2.0 * F) ** (-0.5)


def pack_tables():
    full_rows = 1 + F + F * F
    packed_rows = 1 + F + F * (F + 1) // 2
    gather_table = np.zeros((packed_rows, full_rows), np.float32)
    spread_table = np.zeros((full_rows, packed_rows), np.float32)
    for feature in range(1 + F):
        gather_table[feature, feature] = 1.0
        spread_table[feature, feature] = 1.0
    position = 1 + F
    for leading_at in range(F):
        for trailing_at in range(leading_at, F):
            upper_row = 1 + F + leading_at * F + trailing_at
            lower_row = 1 + F + trailing_at * F + leading_at
            gather_table[position, upper_row] = 1.0
            if leading_at == trailing_at:
                spread_table[upper_row, position] = 1.0
            else:
                gather_table[position, lower_row] = 1.0
                spread_table[upper_row, position] = 0.5
                spread_table[lower_row, position] = 0.5
            position += 1
    return (jnp.asarray(gather_table), jnp.asarray(spread_table))


def add_terms(earlier, later_term):
    return earlier + later_term


def shards(inputs, values, w_qk, conv_qk, conv_v, d_attn):
    weights = lax.all_to_all(w_qk, "fsdp", split_axis=1, concat_axis=0, tiled=True)
    tokens = inputs[0]
    positions = tokens.shape[0]
    width_qk = weights.shape[1]
    heads = width_qk // (2 * F)
    leading_table, trailing_table = expand_tables()
    conv_all = jnp.concatenate([conv_qk, conv_v], axis=1)
    qk_raw = jnp.dot(tokens, weights, preferred_element_type=jnp.float32).astype(jnp.bfloat16)
    joined = jnp.concatenate([qk_raw, values[0]], axis=1)
    rim_rows = from_behind(joined[positions - (CONV - 1) :], CTX, 1)
    extended = jnp.concatenate([rim_rows, joined], axis=0)
    running = jnp.zeros(joined.shape, jnp.float32)
    for offset in range(CONV):
        running = running + conv_all[offset] * extended[
            CONV - 1 - offset : CONV - 1 - offset + positions
        ].astype(jnp.float32)
    convolved = running.astype(jnp.bfloat16)
    paired = convolved[:, :width_qk].reshape(positions, heads, 2 * F).transpose(1, 0, 2)
    queries = paired[:, :, :F]
    key_rows = paired[:, :, F:]
    valued = convolved[:, width_qk:].reshape(positions, heads, E).transpose(1, 0, 2)
    query32 = queries.astype(jnp.float32)
    key32 = key_rows.astype(jnp.float32)
    value32 = valued.astype(jnp.float32)
    query_feat = features(query32, leading_table, trailing_table)
    key_feat = features(key32, leading_table, trailing_table)
    own_state = jnp.einsum("hpf,hpe->hfe", key_feat, value32)
    gather_table, spread_table = pack_tables()
    payload = jnp.einsum("gf,hfe->hge", gather_table, own_state)
    carried = carried_in(payload, CTX, add_terms, jnp.zeros(payload.shape, jnp.float32), False)
    prior = jnp.einsum("fg,hge->hfe", spread_table, carried)
    dotted = jnp.einsum(
        "htf,hpf->htp", queries, key_rows, preferred_element_type=jnp.float32
    ) * F ** (-0.5)
    rows_at = lax.broadcasted_iota(jnp.int32, (positions, positions), 0)
    cols_at = lax.broadcasted_iota(jnp.int32, (positions, positions), 1)
    causal = (cols_at <= rows_at)[None]
    kernel_b = jnp.where(causal, 1.0 + dotted + 0.5 * dotted * dotted, 0.0).astype(jnp.bfloat16)
    mixed_out = jnp.einsum("htp,hpe->hte", kernel_b, valued, preferred_element_type=jnp.float32)
    mixed_out = mixed_out + jnp.einsum("htf,hfe->hte", query_feat, prior)
    scale_inv = lax.rsqrt(jnp.mean(mixed_out * mixed_out, axis=-1, keepdims=True) + eps_norm)
    normed = mixed_out * scale_inv
    attended = normed.astype(jnp.bfloat16).transpose(1, 0, 2).reshape(1, positions, heads * E)
    grad_in = d_attn[0].reshape(positions, heads, E).transpose(1, 0, 2).astype(jnp.float32)
    d_mixed = (
        scale_inv * (grad_in - normed * jnp.mean(grad_in * normed, axis=-1, keepdims=True))
    ).astype(jnp.bfloat16)
    d_mixed32 = d_mixed.astype(jnp.float32)
    own_grad = jnp.einsum("htf,hte->hfe", query_feat, d_mixed32)
    grad_payload = jnp.einsum("gf,hfe->hge", gather_table, own_grad)
    grad_carried = carried_in(
        grad_payload, CTX, add_terms, jnp.zeros(grad_payload.shape, jnp.float32), True
    )
    later = jnp.einsum("fg,hge->hfe", spread_table, grad_carried)
    d_kernel = jnp.einsum("hte,hpe->htp", d_mixed, valued, preferred_element_type=jnp.float32)
    d_score = (jnp.where(causal, d_kernel * (1.0 + dotted), 0.0) * F ** (-0.5)).astype(jnp.bfloat16)
    d_query = jnp.einsum("htp,hpf->htf", d_score, key_rows, preferred_element_type=jnp.float32)
    d_query = d_query + features_back(
        query32, jnp.einsum("hte,hfe->htf", d_mixed32, prior), leading_table, trailing_table
    )
    d_key = jnp.einsum("htp,htf->hpf", d_score, queries, preferred_element_type=jnp.float32)
    d_key = d_key + features_back(
        key32, jnp.einsum("hpe,hfe->hpf", value32, later), leading_table, trailing_table
    )
    d_valued = jnp.einsum("htp,hte->hpe", kernel_b, d_mixed, preferred_element_type=jnp.float32)
    d_valued = d_valued + jnp.einsum("hpf,hfe->hpe", key_feat, later)
    d_paired = (
        jnp.concatenate([d_query, d_key], axis=2).transpose(1, 0, 2).reshape(positions, width_qk)
    )
    d_joined = jnp.concatenate(
        [d_paired, d_valued.transpose(1, 0, 2).reshape(positions, heads * E)], axis=1
    )
    next_rows = from_behind(d_joined[: CONV - 1], CTX, -1)
    grad_ext = jnp.concatenate([d_joined, next_rows], axis=0)
    running = jnp.zeros(d_joined.shape, jnp.float32)
    for offset in range(CONV):
        running = running + conv_all[offset] * grad_ext[offset : offset + positions]
    grad_v = running[:, width_qk:].astype(jnp.bfloat16).reshape(1, positions, heads * E)
    d_qk = running[:, :width_qk].astype(jnp.bfloat16)
    ctx_count = lax.axis_size(CTX)
    batch_count = lax.axis_size("batch")
    grad_scale = float(positions * ctx_count * batch_count) ** (-0.5)
    along_seq = summed_on_arrival(
        lax.dot_general(tokens, d_qk, (((0,), (0,)), ((), ())), preferred_element_type=jnp.float32),
        CTX,
        0,
    )
    grad_w = summed_on_arrival(along_seq, "batch", 0)
    return (attended, grad_v, grad_w * grad_scale)


def solution(mesh):
    split = Mesh(
        mesh.devices.reshape(8, 4, 2, mesh.shape["fsdp"], mesh.shape["batch"]),
        ("ctx_0", "ctx_1", "ctx_2", "fsdp", "batch"),
    )
    in_specs = (
        P("batch", CTX, None),
        P("batch", CTX, "fsdp"),
        P("fsdp", None),
        P(None, "fsdp"),
        P(None, "fsdp"),
        P("batch", CTX, "fsdp"),
    )
    out_specs = (P("batch", CTX, "fsdp"), P("batch", CTX, "fsdp"), P(CTX_BATCH, "fsdp"))
    return jax.shard_map(
        shards, mesh=split, in_specs=in_specs, out_specs=out_specs, check_vma=False
    )
```

profile of v0, /device:TPU:1, one launch (start us, length us, event | category | flops | bytes accessed | tf_op | source)
XLA Modules:
  0.0 189.8 jit_solution(10413459782520286756)
XLA Ops:
  0.6 1.9 copy.84
  2.5 17.2 %all-to-all-start = ((bf16[512,8,32]{0,2,1:T(8,128)(2,1)}), bf16[512,8,32]{0,2,1:T(8,128)(2,1)S(1)}, u32[]{:S(2)}, u32[]{:S(2)}) async-start(bf16[512,8,32]{0,2,1:T(8,128)(2,1)} %bitcast.1), calls=%async_computation | async-start | bytes 524288 | tf_op jit(solution)/shard_map/all_to_all | solution.py:115
  19.8 0.8 copy-done.4
  20.7 9.5 %all-to-all-done = bf16[512,8,32]{0,2,1:T(8,128)(2,1)S(1)} async-done(((bf16[512,8,32]{0,2,1:T(8,128)(2,1)}), bf16[512,8,32]{0,2,1:T(8,128)(2,1)S(1)}, u32[]{:S(2)}, u32[]{:S(2)}) %all-to-all-start) | async-done | bytes 262176 | tf_op jit(solution)/shard_map/all_to_all | solution.py:115
  30.9 6.7 %collective-permute-start = (bf16[2,288]{0,1:T(8,128)(2,1)S(1)}, bf16[2,288]{0,1:T(8,128)(2,1)S(1)}, u32[]{:S(2)}, u32[]{:S(2)}) collective-permute-start(bf16[2,288]{0,1:T(8,128)(2,1)S(1)} %fusion.173), channel_id=1, source_target_pairs={{0,16},{16,32},{32,48},{48,64},{64,80},{80,96},{96,112},{112,128},... | collective-permute-start | bytes 3464 | tf_op jit(solution)/shard_map/ppermute | solution.py:21
  37.7 1.3 collective-permute-done
  43.0 1.9 %all-gather = bf16[2,153,256]{2,1,0:T(8,128)(2,1)S(1)} all-gather(bf16[1,153,256]{2,1,0:T(8,128)(2,1)S(1)} %fusion.15), channel_id=2, replica_groups=mesh['ctx_0'=8,'ctx_1'=4,'ctx_2'=2,'fsdp'=8,'batch'=2] {'ctx_2'}, dimensions={0}, use_global_device_ids=true | all-gather | bytes 235008 | tf_op jit(solution)/shard_map/all_gather | solution.py:33
  45.1 16.0 %all_gather.30 = bf16[4,1,153,256]{3,2,1,0:T(8,128)(2,1)S(1)} all-gather(bf16[1,1,153,256]{3,2,1,0:T(8,128)(2,1)S(1)} %fusion.123), channel_id=1, replica_groups=mesh['ctx_0'=8,'ctx_1'=4,'ctx_2'=2,'fsdp'=8,'batch'=2] {'ctx_1'}, dimensions={0}, use_global_device_ids=true | all-gather | bytes 391680 | tf_op jit(solution)/shard_map/all_gather | solution.py:33
  61.2 21.0 %all_gather.31 = bf16[8,1,153,256]{3,2,1,0:T(8,128)(2,1)S(1)} all-gather(bf16[1,1,153,256]{3,2,1,0:T(8,128)(2,1)S(1)} %fusion.98), channel_id=1, replica_groups=mesh['ctx_0'=8,'ctx_1'=4,'ctx_2'=2,'fsdp'=8,'batch'=2] {'ctx_0'}, dimensions={0}, use_global_device_ids=true | all-gather | bytes 705024 | tf_op jit(solution)/shard_map/all_gather | solution.py:33
  85.0 12.7 %all-gather.1 = bf16[2,153,256]{2,1,0:T(8,128)(2,1)S(1)} all-gather(bf16[1,153,256]{2,1,0:T(8,128)(2,1)S(1)} %fusion.12), channel_id=3, replica_groups=mesh['ctx_0'=8,'ctx_1'=4,'ctx_2'=2,'fsdp'=8,'batch'=2] {'ctx_2'}, dimensions={0}, use_global_device_ids=true | all-gather | bytes 235008 | tf_op jit(solution)/shard_map/all_gather | solution.py:33
  97.7 12.3 %all_gather.34 = bf16[4,1,153,256]{3,2,1,0:T(8,128)(2,1)S(1)} all-gather(bf16[1,1,153,256]{3,2,1,0:T(8,128)(2,1)S(1)} %fusion.124), channel_id=1, replica_groups=mesh['ctx_0'=8,'ctx_1'=4,'ctx_2'=2,'fsdp'=8,'batch'=2] {'ctx_1'}, dimensions={0}, use_global_device_ids=true | all-gather | bytes 391680 | tf_op jit(solution)/shard_map/all_gather | solution.py:33
  110.0 21.3 %all_gather.35 = bf16[8,1,153,256]{3,2,1,0:T(8,128)(2,1)S(1)} all-gather(bf16[1,1,153,256]{3,2,1,0:T(8,128)(2,1)S(1)} %fusion.94), channel_id=1, replica_groups=mesh['ctx_0'=8,'ctx_1'=4,'ctx_2'=2,'fsdp'=8,'batch'=2] {'ctx_0'}, dimensions={0}, use_global_device_ids=true | all-gather | bytes 705024 | tf_op jit(solution)/shard_map/all_gather | solution.py:33
  132.9 9.4 %collective-permute-start.1 = (f32[2,288]{0,1:T(8,128)S(1)}, f32[2,288]{0,1:T(8,128)S(1)}, u32[]{:S(2)}, u32[]{:S(2)}) collective-permute-start(f32[2,288]{0,1:T(8,128)S(1)} %fusion.103), channel_id=1, source_target_pairs={{16,0},{32,16},{48,32},{64,48},{80,64},{96,80},{112,96},{128,112},... | collective-permute-start | bytes 6920 | tf_op jit(solution)/shard_map/ppermute | solution.py:21
  142.3 1.6 collective-permute-done.1
  145.5 1.4 reshape.514
  146.9 10.7 %all-to-all-start.1 = ((f32[64,1,2048]{2,1,0:T(1,128)}), f32[64,1,2048]{2,1,0:T(1,128)S(1)}, u32[]{:S(2)}, u32[]{:S(2)}) async-start(f32[64,1,2048]{2,1,0:T(1,128)} %reshape.514), calls=%async_computation.1 | async-start | bytes 1048576 | tf_op jit(solution)/shard_map/all_to_all | solution.py:52
  157.6 0.7 fusion.186
  158.4 18.9 %all-to-all-done.1 = f32[64,1,2048]{2,1,0:T(1,128)S(1)} async-done(((f32[64,1,2048]{2,1,0:T(1,128)}), f32[64,1,2048]{2,1,0:T(1,128)S(1)}, u32[]{:S(2)}, u32[]{:S(2)}) %all-to-all-start.1) | async-done | bytes 524320 | tf_op jit(solution)/shard_map/all_to_all | solution.py:52
  177.9 1.9 %reduce.9 = f32[64,2048]{1,0:T(8,128)S(1)} reduce(f32[64,1,2048]{2,1,0:T(1,128)S(1)} %all-to-all-done.1, f32[]{:T(128)} %broadcast.362), dimensions={1}, to_apply=%all_to_all.24.reduce_sub_computation | reduce | bytes 1048580 | tf_op jit(solution)/shard_map/all_to_all | solution.py:52
  180.5 0.7 reshape.516
  181.1 4.0 %all-to-all-start.2 = ((f32[2,1,1024]{2,1,0:T(1,128)}), f32[2,1,1024]{2,1,0:T(1,128)S(1)}, u32[]{:S(2)}, u32[]{:S(2)}) async-start(f32[2,1,1024]{2,1,0:T(1,128)} %reshape.516), calls=%async_computation.2 | async-start | bytes 16384 | tf_op jit(solution)/shard_map/all_to_all | solution.py:52
  185.1 0.7 copy.99
  185.9 2.4 %all-to-all-done.2 = f32[2,1,1024]{2,1,0:T(1,128)S(1)} async-done(((f32[2,1,1024]{2,1,0:T(1,128)}), f32[2,1,1024]{2,1,0:T(1,128)S(1)}, u32[]{:S(2)}, u32[]{:S(2)}) %all-to-all-start.2) | async-done | bytes 8224 | tf_op jit(solution)/shard_map/all_to_all | solution.py:52
  188.3 0.7 reduce.10
  (82 shorter events, 13.0 us)
Async XLA Ops:
  0.6 29.6 %copy-start = (bf16[1,128,4096]{2,1,0:T(8,128)(2,1)S(1)}, bf16[1,128,4096]{2,1,0:T(8,128)(2,1)}, u32[]{:S(2)}) copy-start(bf16[1,128,4096]{2,1,0:T(8,128)(2,1)} %param.10) | copy-start | bytes 3145732
  2.5 27.7 %all-to-all-start = ((bf16[512,8,32]{0,2,1:T(8,128)(2,1)}), bf16[512,8,32]{0,2,1:T(8,128)(2,1)S(1)}, u32[]{:S(2)}, u32[]{:S(2)}) async-start(bf16[512,8,32]{0,2,1:T(8,128)(2,1)} %bitcast.1), calls=%async_computation | async-start | bytes 524288 | tf_op jit(solution)/shard_map/all_to_all | solution.py:115
  19.7 0.8 copy-start.4
  30.7 6.8 %copy-start.5 = (f32[3,256]{1,0:T(4,128)S(1)}, f32[3,256]{1,0:T(4,128)}, u32[]{:S(2)}) copy-start(f32[3,256]{1,0:T(4,128)} %param.14) | copy-start | bytes 9220
  30.8 6.7 %copy-start.6 = (f32[3,32]{1,0:T(4,128)S(1)}, f32[3,32]{1,0:T(4,128)}, u32[]{:S(2)}) copy-start(f32[3,32]{1,0:T(4,128)} %param.13) | copy-start | bytes 1156
  30.9 8.1 %collective-permute-start = (bf16[2,288]{0,1:T(8,128)(2,1)S(1)}, bf16[2,288]{0,1:T(8,128)(2,1)S(1)}, u32[]{:S(2)}, u32[]{:S(2)}) collective-permute-start(bf16[2,288]{0,1:T(8,128)(2,1)S(1)} %fusion.173), channel_id=1, source_target_pairs={{0,16},{16,32},{32,48},{48,64},{64,80},{80,96},{96,112},{112,128},... | collective-permute-start | bytes 3464 | tf_op jit(solution)/shard_map/ppermute | solution.py:21
  39.3 0.7 copy-start.2
  40.0 0.7 copy-start.3
  41.6 0.9 copy-start.8
  61.2 21.0 %copy-start.7 = (bf16[273,153]{1,0:T(8,128)(2,1)S(1)}, bf16[273,153]{1,0:T(8,128)(2,1)}, u32[]{:S(2)}) copy-start(bf16[273,153]{1,0:T(8,128)(2,1)} %constant.314) | copy-start | bytes 250618
  82.6 0.8 copy-start.1
  132.9 11.0 %collective-permute-start.1 = (f32[2,288]{0,1:T(8,128)S(1)}, f32[2,288]{0,1:T(8,128)S(1)}, u32[]{:S(2)}, u32[]{:S(2)}) collective-permute-start(f32[2,288]{0,1:T(8,128)S(1)} %fusion.103), channel_id=1, source_target_pairs={{16,0},{32,16},{48,32},{64,48},{80,64},{96,80},{112,96},{128,112},... | collective-permute-start | bytes 6920 | tf_op jit(solution)/shard_map/ppermute | solution.py:21
  146.9 30.4 %all-to-all-start.1 = ((f32[64,1,2048]{2,1,0:T(1,128)}), f32[64,1,2048]{2,1,0:T(1,128)S(1)}, u32[]{:S(2)}, u32[]{:S(2)}) async-start(f32[64,1,2048]{2,1,0:T(1,128)} %reshape.514), calls=%async_computation.1 | async-start | bytes 1048576 | tf_op jit(solution)/shard_map/all_to_all | solution.py:52
  181.1 7.1 %all-to-all-start.2 = ((f32[2,1,1024]{2,1,0:T(1,128)}), f32[2,1,1024]{2,1,0:T(1,128)S(1)}, u32[]{:S(2)}, u32[]{:S(2)}) async-start(f32[2,1,1024]{2,1,0:T(1,128)} %reshape.516), calls=%async_computation.2 | async-start | bytes 16384 | tf_op jit(solution)/shard_map/all_to_all | solution.py:52
where the time goes:
time: 191 us; the launch traced here: 190 us
  blocking collectives  85.1 us (45%)
  starting transfers between devices  48 us (25%)
  waiting for transfers between devices  33.7 us (18%)
  local copies, waits for them, and re-layouts  11.3 us (6%)
  matrix products  5.87 us (3%)
  other arithmetic  4.76 us (2%)
    all_gather x6, blocking collectives, carried_in(): lax.all_gather(running.astype(jnp.bfloat16 if value.dtype == jnp.float32...  85.1 us
    all_to_all x2, waiting for transfers between devices, summed_on_arrival(): lax.all_to_all(parts, axis, split_axis=0, concat_axis=0, tiled=True)  21.3 us
    all_to_all x1, starting transfers between devices, shards(): lax.all_to_all(w_qk, 'fsdp', split_axis=1, concat_axis=0, tiled=True)  17.2 us
    ppermute x2, starting transfers between devices, from_behind(): return lax.ppermute(value, axis, pairs)  16 us
    all_to_all x2, starting transfers between devices, summed_on_arrival(): lax.all_to_all(parts, axis, split_axis=0, concat_axis=0, tiled=True)  14.7 us
    all_to_all x1, waiting for transfers between devices, shards(): lax.all_to_all(w_qk, 'fsdp', split_axis=1, concat_axis=0, tiled=True)  9.54 us
    unnamed x26, local copies, waits for them, and re-layouts  8.92 us
  transfers between devices with their start and end apart: 5, of which 5 were waited for; matrix products, arithmetic and copies ran while one was open for 1% of the time, Pallas kernels for 0%

commit v1 on v0

v1 whole, which is shorter than its diff:
```python
import jax
import jax.numpy as jnp
from jax import lax
from jax.experimental import pallas as pl
from jax.experimental.pallas import tpu as pltpu
from jax.sharding import Mesh
from jax.sharding import PartitionSpec as P

F = 16
E = 256
CONV = 3
POS = 128
ROWS = 160
TILES = ROWS // 8 * (E // 128)
CTX = ("ctx_0", "ctx_1", "ctx_2")
CTX_BATCH = ("ctx_0", "ctx_1", "ctx_2", "batch")
BF = jnp.bfloat16
F32 = jnp.float32
eps_norm = 1e-05


def nn(a, b):
    return lax.dot_general(a, b, (((1,), (0,)), ((), ())), preferred_element_type=F32)


def nt(a, b):
    return lax.dot_general(a, b, (((1,), (1,)), ((), ())), preferred_element_type=F32)


def call(body, outs, *args, flops=0, name=None):
    moved = sum(a.size * a.dtype.itemsize for a in (*args, *outs))
    return pl.pallas_call(
        body,
        out_shape=outs,
        in_specs=[pl.BlockSpec(memory_space=pltpu.VMEM)] * len(args),
        out_specs=[pl.BlockSpec(memory_space=pltpu.VMEM)] * len(outs),
        cost_estimate=pl.CostEstimate(flops=flops, bytes_accessed=moved, transcendentals=0),
        compiler_params=pltpu.CompilerParams(vmem_limit_bytes=16 << 20),
        name=name,
    )(*args)


def struct(shape, dtype):
    return jax.ShapeDtypeStruct(shape, dtype)


def shifted(w, s):
    return w if s % F == 0 else jnp.concatenate([w[s % F :], w[: s % F]], axis=0)


def rows_of(w):
    parts = [w]
    for s in range(8):
        parts.append(w * shifted(w, s))
    parts.append(w[:8] * w[8:])
    at = lax.broadcasted_iota(jnp.int32, (8, w.shape[1]), 0)
    parts.append(jnp.where(at == 0, 1.0, 0.0).astype(F32))
    return jnp.concatenate(parts, axis=0)


def gains(rows, width):
    at = lax.broadcasted_iota(jnp.int32, (rows, width), 0)
    quad = jnp.where(at < 2 * F, 1.0 / 32.0, 1.0 / 16.0)
    return jnp.where(at < F, 0.25, jnp.where(at < 152, quad, 1.0)).astype(F32)


def rows_back(w, y):
    total = 0.25 * y[:F] + (1.0 / 16.0) * w * y[F : 2 * F]
    for s in range(1, 8):
        y_s = y[F * (s + 1) : F * (s + 2)]
        total = total + (1.0 / 16.0) * (
            shifted(w, s) * y_s + shifted(w, F - s) * shifted(y_s, F - s)
        )
    y_8 = y[144:152]
    half = jnp.concatenate([w[8:] * y_8, w[:8] * y_8], axis=0)
    return total + (1.0 / 16.0) * half


def to_tiles(state, tiles_ref):
    for tile in range(TILES):
        r, c = divmod(tile, 2)
        tiles_ref[tile] = state[8 * r : 8 * r + 8, 128 * c : 128 * c + 128].astype(BF)
    count = tiles_ref.shape[0]
    for tile in range(TILES, count):
        tiles_ref[tile] = jnp.zeros((8, 128), BF)


def from_tiles(tiles_ref):
    halves = [
        jnp.concatenate([tiles_ref[2 * r + c].astype(F32) for r in range(ROWS // 8)], axis=0)
        for c in range(2)
    ]
    return jnp.concatenate(halves, axis=1)


def turn_body(w_ref, out_ref):
    width = w_ref.shape[1]
    row = lax.broadcasted_iota(jnp.int32, (width, width), 0)
    col = lax.broadcasted_iota(jnp.int32, (width, width), 1)
    eye = jnp.where(row == col, 1.0, 0.0).astype(BF)
    turned = nt(eye, w_ref[...]).astype(BF)
    for part in range(out_ref.shape[0]):
        out_ref[part] = turned[32 * part : 32 * part + 32]


def state_body(w_ref, tok_ref, htok_ref, val_ref, hval_ref, cqk_ref, cv_ref, conv_ref, valued_ref, tiles_ref):
    parts, _, deep = w_ref.shape
    own = jnp.zeros((2 * F, POS), F32)
    rim = jnp.zeros((2 * F, htok_ref.shape[0]), F32)
    for part in range(parts):
        w = w_ref[part]
        own = own + nt(w, tok_ref[:, deep * part : deep * part + deep])
        rim = rim + nt(w, htok_ref[:, deep * part : deep * part + deep])
    x0 = own.astype(BF).astype(F32)
    h = rim.astype(BF).astype(F32)
    lane = lax.broadcasted_iota(jnp.int32, x0.shape, 1)
    last, before = (jnp.broadcast_to(h[:, k : k + 1], x0.shape) for k in (7, 6))
    x1 = jnp.where(lane == 0, last, pltpu.roll(x0, 1, 1))
    x2 = jnp.where(lane == 0, before, jnp.where(lane == 1, last, pltpu.roll(x0, 2, 1)))
    conv = cqk_ref[0] * x0 + cqk_ref[1] * x1 + cqk_ref[2] * x2
    conv = conv.astype(BF).astype(F32)
    conv_ref[...] = conv
    v0 = val_ref[...].astype(F32)
    hv = hval_ref[...].astype(F32)
    at = lax.broadcasted_iota(jnp.int32, v0.shape, 0)
    last, before = (jnp.broadcast_to(hv[k : k + 1], v0.shape) for k in (7, 6))
    v1 = jnp.where(at == 0, last, pltpu.roll(v0, 1, 0))
    v2 = jnp.where(at == 0, before, jnp.where(at == 1, last, pltpu.roll(v0, 2, 0)))
    valued = (cv_ref[0:1] * v0 + cv_ref[1:2] * v1 + cv_ref[2:3] * v2).astype(BF)
    valued_ref[...] = valued
    to_tiles(nn(rows_of(conv[F:]).astype(BF), valued), tiles_ref)


def local_body(conv_ref, valued_ref, mixed_ref, kernel_ref, slope_ref, qrows_ref, krows_ref, qturn_ref):
    conv = conv_ref[...]
    queries, keys = conv[:F], conv[F:]
    dotted = nn(queries.T.astype(BF), keys.astype(BF)) * 0.25
    row = lax.broadcasted_iota(jnp.int32, dotted.shape, 0)
    col = lax.broadcasted_iota(jnp.int32, dotted.shape, 1)
    causal = col <= row
    kernel = jnp.where(causal, 1.0 + dotted + 0.5 * dotted * dotted, 0.0)
    slope_ref[...] = jnp.where(causal, (1.0 + dotted) * 0.25, 0.0)
    mixed_ref[...] = nn(kernel.astype(BF), valued_ref[...])
    kernel_ref[...] = kernel.T.astype(BF)
    q_rows, k_rows = rows_of(queries), rows_of(keys)
    gain = gains(ROWS, POS)
    qturn_ref[...] = q_rows.astype(BF)
    qrows_ref[...] = (q_rows * gain).T.astype(BF)
    krows_ref[...] = (k_rows * gain).T.astype(BF)


def before_body(in_ref, out_ref):
    count = in_ref.shape[0]
    total = jnp.zeros(in_ref.shape[1:], F32)
    for k in range(count):
        out_ref[k] = total.astype(BF)
        total = total + in_ref[k].astype(F32)


def after_body(in_ref, out_ref):
    count = in_ref.shape[0]
    total = jnp.zeros(in_ref.shape[1:], F32)
    for k in reversed(range(count)):
        out_ref[k] = total.astype(BF)
        total = total + in_ref[k].astype(F32)


def mix_body(prior_ref, mixed_ref, qrows_ref, qturn_ref, grad_ref, att_ref, dmix_ref, rows_ref, tiles_ref):
    prior = from_tiles(prior_ref).astype(BF)
    rows_ref[...] = prior
    mixed = mixed_ref[...] + nn(qrows_ref[...], prior)
    inv = lax.rsqrt(jnp.mean(mixed * mixed, axis=-1, keepdims=True) + eps_norm)
    normed = mixed * inv
    att_ref[...] = normed.astype(BF)
    grad = grad_ref[...].astype(F32)
    d_mixed = (inv * (grad - normed * jnp.mean(grad * normed, axis=-1, keepdims=True))).astype(BF)
    dmix_ref[...] = d_mixed
    to_tiles(nn(qturn_ref[...], d_mixed), tiles_ref)


def back_body(conv_ref, valued_ref, kernel_ref, slope_ref, dmix_ref, rows_ref, dqk_ref, dval_ref):
    conv = conv_ref[...]
    queries, keys = conv[:F], conv[F:]
    d_mixed = dmix_ref[...]
    d_score = (nt(d_mixed, valued_ref[...]) * slope_ref[...]).astype(BF)
    d_query = nt(keys.astype(BF), d_score) + rows_back(queries, nt(rows_ref[...], d_mixed))
    dqk_ref[:F] = d_query
    dqk_ref[F:] = nn(queries.astype(BF), d_score)
    dval_ref[...] = nn(kernel_ref[...], d_mixed)


def grad_body(later_ref, conv_ref, valued_ref, krows_ref, dqk_ref, dval_ref, tok_ref, htok_ref, cqk_ref, cv_ref, gval_ref, head_ref, out_ref):
    later = from_tiles(later_ref).astype(BF)
    keys = conv_ref[F:]
    d_key = dqk_ref[F:] + rows_back(keys, nt(later, valued_ref[...]))
    d = jnp.concatenate([dqk_ref[:F], d_key], axis=0)
    lane = lax.broadcasted_iota(jnp.int32, d.shape, 1)
    d1, d2 = cqk_ref[1] * d, cqk_ref[2] * d
    own = cqk_ref[0] * d
    own = own + jnp.where(lane < POS - 1, pltpu.roll(d1, POS - 1, 1), 0.0)
    own = own + jnp.where(lane < POS - 2, pltpu.roll(d2, POS - 2, 1), 0.0)
    to_last = pltpu.roll(d2, 6, 1)
    rim = jnp.where(lane == 6, to_last, jnp.where(lane == 7, pltpu.roll(d1, 7, 1) + to_last, 0.0))
    own_b, rim_b = own.astype(BF), rim[:, :8].astype(BF)

    dv = dval_ref[...] + nn(krows_ref[...], later)
    head_ref[...] = dv[:8]
    at = lax.broadcasted_iota(jnp.int32, dv.shape, 0)
    gval = cv_ref[0:1] * dv
    gval = gval + cv_ref[1:2] * jnp.where(at < POS - 1, pltpu.roll(dv, POS - 1, 0), 0.0)
    gval = gval + cv_ref[2:3] * jnp.where(at < POS - 2, pltpu.roll(dv, POS - 2, 0), 0.0)
    gval_ref[...] = gval

    group = lax.broadcasted_iota(jnp.int32, (8, 128), 1) // 32
    chunk = 512
    for start in range(0, tok_ref.shape[1], chunk):
        part = nn(own_b, tok_ref[:, start : start + chunk]) + nn(rim_b, htok_ref[:, start : start + chunk])
        for at_lane in range(0, chunk, 128):
            blocks = [part[8 * i : 8 * i + 8, at_lane : at_lane + 128] for i in range(4)]
            for q in range(4):
                moved = [pltpu.roll(b, 32 * ((i - q) % 4), 1) if i != q else b for i, b in enumerate(blocks)]
                packed = jnp.where(
                    group == 0, moved[0], jnp.where(group == 1, moved[1], jnp.where(group == 2, moved[2], moved[3]))
                )
                out_ref[(start + at_lane) // 32 + q] = packed.astype(out_ref.dtype)


def rim_body(gval_ref, next_ref, cv_ref, out_ref):
    out_ref[...] = gval_ref[...].astype(BF)
    nxt = next_ref[...]
    at = lax.broadcasted_iota(jnp.int32, nxt.shape, 0)
    c1, c2 = cv_ref[1:2], cv_ref[2:3]
    first, second = (jnp.broadcast_to(nxt[k : k + 1], nxt.shape) for k in (0, 1))
    more = jnp.where(at == 6, c2 * first, jnp.where(at == 7, c1 * first + c2 * second, 0.0))
    out_ref[POS - 8 :] = (gval_ref[POS - 8 :] + more).astype(BF)


def sum_body(parts_ref, out_ref, *, scale):
    totals = [parts_ref[k].astype(F32) for k in range(8)]
    for k in range(8, parts_ref.shape[0]):
        totals[k % 8] = totals[k % 8] + parts_ref[k].astype(F32)
    while len(totals) > 1:
        totals = [a + b for a, b in zip(totals[::2], totals[1::2])]
    total = totals[0] * scale
    stacked = jnp.concatenate([total] + [pltpu.roll(total, 128 - 32 * i, 1) for i in (1, 2, 3)], axis=0)
    square = jnp.concatenate([stacked, jnp.zeros((96, 128), F32)], axis=0).T
    out_ref[...] = square[:32, :32]


def to_next(value, by):
    size = lax.axis_size(CTX)
    pairs = [(i, i + by) for i in range(size) if 0 <= i + by < size]
    return lax.ppermute(value, CTX, pairs)


def exchange(value, axes):
    return lax.all_to_all(value, axes, split_axis=0, concat_axis=0, tiled=True)


def shards(inputs, values, w_qk, conv_qk, conv_v, d_attn):
    tokens, own_values = inputs[0], values[0]
    depth = tokens.shape[1]
    splits = lax.axis_size("fsdp")
    blocks = lax.axis_size(CTX)
    peers = blocks * lax.axis_size("batch")
    deep = w_qk.shape[0]

    (turned,) = call(turn_body, [struct((splits, 2 * F, deep), BF)], w_qk, name="turn")
    weights = exchange(turned, "fsdp")
    rim = to_next(jnp.concatenate([tokens[POS - 8 :], own_values[POS - 8 :]], axis=1), 1)
    rim_tokens, rim_values = rim[:, :depth], rim[:, depth:]
    taps = jnp.broadcast_to(conv_qk[:, :, None], (CONV, 2 * F, POS))

    conv, valued, state = call(
        state_body,
        [struct((2 * F, POS), F32), struct((POS, E), BF), struct((blocks, 8, 128), BF)],
        weights, tokens, rim_tokens, own_values, rim_values, taps, conv_v,
        name="state",
    )
    states = exchange(state, CTX)
    mixed_own, kernel, slope, q_rows, k_rows, q_turn = call(
        local_body,
        [
            struct((POS, E), F32), struct((POS, POS), BF), struct((POS, POS), F32),
            struct((POS, ROWS), BF), struct((POS, ROWS), BF), struct((ROWS, POS), BF),
        ],
        conv, valued,
        flops=2 * POS * POS * (E + F), name="local",
    )
    (sums,) = call(before_body, [struct(states.shape, BF)], states, name="before")
    prior = exchange(sums, CTX)
    attended, d_mixed, prior_rows, grad_state = call(
        mix_body,
        [struct((POS, E), BF), struct((POS, E), BF), struct((ROWS, E), BF), struct((blocks, 8, 128), BF)],
        prior, mixed_own, q_rows, q_turn, d_attn[0],
        name="mix",
    )
    grad_states = exchange(grad_state, CTX)
    d_qk, d_val = call(
        back_body,
        [struct((2 * F, POS), F32), struct((POS, E), F32)],
        conv, valued, kernel, slope, d_mixed, prior_rows,
        flops=2 * POS * POS * (2 * E + 2 * F), name="back",
    )
    (grad_sums,) = call(after_body, [struct(grad_states.shape, BF)], grad_states, name="after")
    later = exchange(grad_sums, CTX)
    g_val, head, grad_parts = call(
        grad_body,
        [struct((POS, E), F32), struct((8, E), F32), struct((peers, 8, 128), BF)],
        later, conv, valued, k_rows, d_qk, d_val, tokens, rim_tokens, taps, conv_v,
        flops=2 * POS * depth * 2 * F, name="grad",
    )
    next_rows = to_next(head, -1)
    arrived = exchange(grad_parts, CTX_BATCH)
    (grad_v,) = call(rim_body, [struct((POS, E), BF)], g_val, next_rows, conv_v, name="rim")
    scale = float(POS * peers) ** (-0.5)
    (grad_w,) = call(
        lambda a, b: sum_body(a, b, scale=scale), [struct((2 * F, 2 * F), F32)], arrived, name="sum"
    )
    return (attended[None], grad_v[None], grad_w)


def solution(mesh):
    split = Mesh(
        mesh.devices.reshape(8, 4, 2, mesh.shape["fsdp"], mesh.shape["batch"]),
        ("ctx_0", "ctx_1", "ctx_2", "fsdp", "batch"),
    )
    in_specs = (
        P("batch", CTX, None),
        P("batch", CTX, "fsdp"),
        P("fsdp", None),
        P(None, "fsdp"),
        P(None, "fsdp"),
        P("batch", CTX, "fsdp"),
    )
    out_specs = (P("batch", CTX, "fsdp"), P("batch", CTX, "fsdp"), P(CTX_BATCH, "fsdp"))
    return jax.shard_map(
        shards, mesh=split, in_specs=in_specs, out_specs=out_specs, check_vma=False
    )
```

time: 191 us -> 140 us (0.73)
  blocking collectives: 85.1 us -> 46 us
  local copies, waits for them, and re-layouts: 11.3 us -> 2.43 us
  waiting for transfers between devices: 33.7 us -> 42.4 us
  starting transfers between devices: 48 us -> 39.9 us
  Pallas kernels: 0 us -> 7.57 us
  matrix products: 5.87 us -> 0 us
  other arithmetic: 4.76 us -> 0.01 us
    all_gather x6 -> x0, blocking collectives: 85.1 us -> none  [carried_in(): lax.all_gather(running.astype(jnp.bfloat16 if value.dtype == jnp.float32...]
    all_to_all x0 -> x2, blocking collectives: none -> 46 us  [exchange(): return lax.all_to_all(value, axes, split_axis=0, concat_axis=0, tiled=True)]
    ppermute x2, starting transfers between devices: 16 us -> 8.19 us  [to_next(): return lax.ppermute(value, CTX, pairs)]
    pallas_call x0 -> x10, Pallas kernels: none -> 7.57 us  [call(): pl.pallas_call(body, out_shape=outs, in_specs=[pl.BlockSpec(memory_space=...]
    unnamed x26 -> x12, local copies, waits for them, and re-layouts: 8.92 us -> 1.66 us
    all_to_all x3 -> x4, waiting for transfers between devices: 30.9 us -> 37.8 us  [exchange(): return lax.all_to_all(value, axes, split_axis=0, concat_axis=0, tiled=True)]
    dot_general x24 -> x0, matrix products: 5.87 us -> none  [the longest x1 0.51 us: shards(): grad_payload = jnp.einsum('gf,hfe->hge', gather_table, own_grad)]
    all_to_all x2 -> x0, other arithmetic: 2.64 us -> none  [summed_on_arrival(): lax.all_to_all(parts, axis, split_axis=0, concat_axis=0, tiled=True)]
  transfers between devices with their start and end apart: 5 -> 6, of which waited for: 5 -> 6; matrix products, arithmetic and copies ran while one was open for 1% -> 1% of each run, Pallas kernels for 0% -> 1%
where the time goes in v1:
time: 140 us; the launch traced here: 139 us
  blocking collectives  46 us (33%)
  waiting for transfers between devices  42.4 us (30%)
  starting transfers between devices  39.9 us (28%)
  Pallas kernels  7.57 us (5%)
  local copies, waits for them, and re-layouts  2.43 us (2%)
    all_to_all x2, blocking collectives, exchange(): return lax.all_to_all(value, axes, split_axis=0, concat_axis=0, tiled=True)  46 us
    all_to_all x4, waiting for transfers between devices, exchange(): return lax.all_to_all(value, axes, split_axis=0, concat_axis=0, tiled=True)  37.8 us
    all_to_all x4, starting transfers between devices, exchange(): return lax.all_to_all(value, axes, split_axis=0, concat_axis=0, tiled=True)  31.7 us
    ppermute x2, starting transfers between devices, to_next(): return lax.ppermute(value, CTX, pairs)  8.19 us
    pallas_call x10, Pallas kernels, call(): pl.pallas_call(body, out_shape=outs, in_specs=[pl.BlockSpec(memory_space=...  7.57 us
    ppermute x2, waiting for transfers between devices, to_next(): return lax.ppermute(value, CTX, pairs)  4.6 us
  transfers between devices with their start and end apart: 6, of which 6 were waited for; matrix products, arithmetic and copies ran while one was open for 1% of the time, Pallas kernels for 1%

profile of v1, /device:TPU:1, one launch (start us, length us, event | category | flops | bytes accessed | tf_op | source)
XLA Modules:
  0.0 139.1 jit_solution(4548700894519538791)
XLA Ops:
  0.6 1.0 copy-done.1
  1.7 1.0 turn.1
  2.6 17.2 %all-to-all-start = ((bf16[8,32,512]{2,1,0:T(8,128)(2,1)}), bf16[8,32,512]{2,1,0:T(8,128)(2,1)S(1)}, u32[]{:S(2)}, u32[]{:S(2)}) async-start(bf16[8,32,512]{2,1,0:T(8,128)(2,1)} %turn.1), calls=%async_computation | async-start | bytes 524288 | tf_op jit(solution)/shard_map/all_to_all | solution.py:257
  19.9 0.7 slice_bitcast_fusion.1
  20.6 5.3 %collective-permute-start = (bf16[8,4352]{1,0:T(8,128)(2,1)S(1)}, bf16[8,4352]{1,0:T(8,128)(2,1)S(1)}, u32[]{:S(2)}, u32[]{:S(2)}) collective-permute-start(bf16[8,4352]{1,0:T(8,128)(2,1)S(1)} %pad_maximum_fusion), channel_id=1, source_target_pairs={{0,16},{16,32},{32,48},{48,64},{64,80},{80,96},{96,112},{112,128},... | collective-permute-start | bytes 208904 | tf_op jit(solution)/shard_map/ppermute | solution.py:253
  25.9 1.3 collective-permute-done
  27.2 3.1 %all-to-all-done.w_ref = bf16[8,32,512]{2,1,0:T(8,128)(2,1)S(1)} async-done(((bf16[8,32,512]{2,1,0:T(8,128)(2,1)}), bf16[8,32,512]{2,1,0:T(8,128)(2,1)S(1)}, u32[]{:S(2)}, u32[]{:S(2)}) %all-to-all-start) | async-done | bytes 262176 | tf_op jit(solution)/shard_map/all_to_all | solution.py:257
  31.1 0.8 state.1
  31.8 28.7 %all_to_all.30.in_ref = bf16[64,8,128]{2,1,0:T(8,128)(2,1)S(1)} all-to-all(bf16[64,8,128]{2,1,0:T(8,128)(2,1)S(1)} %get-tuple-element.21), channel_id=1, replica_groups=mesh['ctx_0'=8,'ctx_1'=4,'ctx_2'=2,'fsdp'=8,'batch'=2] {'ctx_0','ctx_1',..., dimensions={0} | all-to-all | bytes 262144 | tf_op jit(solution)/shard_map/all_to_all | solution.py:257
  60.5 0.7 before.1
  61.2 4.4 %all-to-all-start.2 = ((bf16[64,8,128]{2,1,0:T(8,128)(2,1)}), bf16[64,8,128]{2,1,0:T(8,128)(2,1)S(1)}, u32[]{:S(2)}, u32[]{:S(2)}) async-start(bf16[64,8,128]{2,1,0:T(8,128)(2,1)} %before.1), calls=%async_computation.2 | async-start | bytes 262144 | tf_op jit(solution)/shard_map/all_to_all | solution.py:257
  66.0 13.4 %all-to-all-done.2.prior_ref = bf16[64,8,128]{2,1,0:T(8,128)(2,1)S(1)} async-done(((bf16[64,8,128]{2,1,0:T(8,128)(2,1)}), bf16[64,8,128]{2,1,0:T(8,128)(2,1)S(1)}, u32[]{:S(2)}, u32[]{:S(2)}) %all-to-all-start.2) | async-done | bytes 131104 | tf_op jit(solution)/shard_map/all_to_all | solution.py:257
  79.4 0.9 mix.1
  80.3 17.3 %all_to_all.31.in_ref = bf16[64,8,128]{2,1,0:T(8,128)(2,1)S(1)} all-to-all(bf16[64,8,128]{2,1,0:T(8,128)(2,1)S(1)} %get-tuple-element.28), channel_id=1, replica_groups=mesh['ctx_0'=8,'ctx_1'=4,'ctx_2'=2,'fsdp'=8,'batch'=2] {'ctx_0','ctx_1',..., dimensions={0} | all-to-all | bytes 262144 | tf_op jit(solution)/shard_map/all_to_all | solution.py:257
  97.6 0.7 after.1
  98.3 4.4 %all-to-all-start.4 = ((bf16[64,8,128]{2,1,0:T(8,128)(2,1)}), bf16[64,8,128]{2,1,0:T(8,128)(2,1)S(1)}, u32[]{:S(2)}, u32[]{:S(2)}) async-start(bf16[64,8,128]{2,1,0:T(8,128)(2,1)} %after.1), calls=%async_computation.4 | async-start | bytes 262144 | tf_op jit(solution)/shard_map/all_to_all | solution.py:257
  103.1 13.4 %all-to-all-done.4.later_ref = bf16[64,8,128]{2,1,0:T(8,128)(2,1)S(1)} async-done(((bf16[64,8,128]{2,1,0:T(8,128)(2,1)}), bf16[64,8,128]{2,1,0:T(8,128)(2,1)S(1)}, u32[]{:S(2)}, u32[]{:S(2)}) %all-to-all-start.4) | async-done | bytes 131104 | tf_op jit(solution)/shard_map/all_to_all | solution.py:257
  116.5 1.4 %grad.1 = (f32[128,256]{1,0:T(8,128)S(1)}, f32[8,256]{1,0:T(8,128)S(1)}, bf16[128,8,128]{2,1,0:T(8,128)(2,1)}) custom-call(bf16[64,8,128]{2,1,0:T(8,128)(2,1)S(1)} %all-to-all-done.4.later_ref, f32[32,128]{1,0:T(8,128)S(1)} %get-tuple-element.22.conv_ref, bf16[128,256]{1,0:T(8,128)(2,1)S(1)} %get-tuple-element.23.valued_ref, ...), custom_call_target="tpu_custom_call" | custom-call | flops 33554432 | bytes 1969152 | tf_op jit(solution)/shard_map/grad/pallas_call | solution.py:32
  117.9 5.6 %all-to-all-start.5 = ((bf16[128,8,128]{2,1,0:T(8,128)(2,1)}), bf16[128,8,128]{2,1,0:T(8,128)(2,1)S(1)}, u32[]{:S(2)}, u32[]{:S(2)}) async-start(bf16[128,8,128]{2,1,0:T(8,128)(2,1)} %get-tuple-element.38), calls=%async_computation.5 | async-start | bytes 524288 | tf_op jit(solution)/shard_map/all_to_all | solution.py:257
  123.5 2.9 %collective-permute-start.1 = (f32[8,256]{1,0:T(8,128)S(1)}, f32[8,256]{1,0:T(8,128)S(1)}, u32[]{:S(2)}, u32[]{:S(2)}) collective-permute-start(f32[8,256]{1,0:T(8,128)S(1)} %get-tuple-element.37), channel_id=1, source_target_pairs={{16,0},{32,16},{48,32},{64,48},{80,64},{96,80},{112,96},{128,112},... | collective-permute-start | bytes 24584 | tf_op jit(solution)/shard_map/ppermute | solution.py:253
  126.4 3.2 %collective-permute-done.1.next_ref = f32[8,256]{1,0:T(8,128)S(1)} collective-permute-done((f32[8,256]{1,0:T(8,128)S(1)}, f32[8,256]{1,0:T(8,128)S(1)}, u32[]{:S(2)}, u32[]{:S(2)}) %collective-permute-start.1) | collective-permute-done | bytes 8224 | tf_op jit(solution)/shard_map/ppermute | solution.py:253
  129.7 0.6 rim.1
  130.3 8.0 %all-to-all-done.5.a = bf16[128,8,128]{2,1,0:T(8,128)(2,1)S(1)} async-done(((bf16[128,8,128]{2,1,0:T(8,128)(2,1)}), bf16[128,8,128]{2,1,0:T(8,128)(2,1)S(1)}, u32[]{:S(2)}, u32[]{:S(2)}) %all-to-all-start.5) | async-done | bytes 262176 | tf_op jit(solution)/shard_map/all_to_all | solution.py:257
  138.3 0.8 sum.1
  (18 shorter events, 1.4 us)
Async XLA Ops:
  0.6 19.9 %copy-start = (bf16[1,128,4096]{2,1,0:T(8,128)(2,1)S(1)}, bf16[1,128,4096]{2,1,0:T(8,128)(2,1)}, u32[]{:S(2)}) copy-start(bf16[1,128,4096]{2,1,0:T(8,128)(2,1)} %param.6) | copy-start | bytes 3145732
  0.6 1.0 copy-start.1
  2.6 27.7 %all-to-all-start = ((bf16[8,32,512]{2,1,0:T(8,128)(2,1)}), bf16[8,32,512]{2,1,0:T(8,128)(2,1)S(1)}, u32[]{:S(2)}, u32[]{:S(2)}) async-start(bf16[8,32,512]{2,1,0:T(8,128)(2,1)} %turn.1), calls=%async_computation | async-start | bytes 524288 | tf_op jit(solution)/shard_map/all_to_all | solution.py:257
  20.6 6.6 %collective-permute-start = (bf16[8,4352]{1,0:T(8,128)(2,1)S(1)}, bf16[8,4352]{1,0:T(8,128)(2,1)S(1)}, u32[]{:S(2)}, u32[]{:S(2)}) collective-permute-start(bf16[8,4352]{1,0:T(8,128)(2,1)S(1)} %pad_maximum_fusion), channel_id=1, source_target_pairs={{0,16},{16,32},{32,48},{48,64},{64,80},{80,96},{96,112},{112,128},... | collective-permute-start | bytes 208904 | tf_op jit(solution)/shard_map/ppermute | solution.py:253
  27.2 3.2 %copy-start.2 = (bf16[1,128,256]{2,1,0:T(8,128)(2,1)S(1)}, bf16[1,128,256]{2,1,0:T(8,128)(2,1)}, u32[]{:S(2)}) copy-start(bf16[1,128,256]{2,1,0:T(8,128)(2,1)} %param.7) | copy-start | bytes 196612
  27.2 3.1 %copy-start.5 = (f32[3,32]{1,0:T(4,128)S(1)}, f32[3,32]{1,0:T(4,128)}, u32[]{:S(2)}) copy-start(f32[3,32]{1,0:T(4,128)} %param.9) | copy-start | bytes 1156
  30.4 0.7 copy-start.4
  61.2 18.2 %all-to-all-start.2 = ((bf16[64,8,128]{2,1,0:T(8,128)(2,1)}), bf16[64,8,128]{2,1,0:T(8,128)(2,1)S(1)}, u32[]{:S(2)}, u32[]{:S(2)}) async-start(bf16[64,8,128]{2,1,0:T(8,128)(2,1)} %before.1), calls=%async_computation.2 | async-start | bytes 262144 | tf_op jit(solution)/shard_map/all_to_all | solution.py:257
  65.7 13.7 %copy-start.3 = (bf16[1,128,256]{2,1,0:T(8,128)(2,1)S(1)}, bf16[1,128,256]{2,1,0:T(8,128)(2,1)}, u32[]{:S(2)}) copy-start(bf16[1,128,256]{2,1,0:T(8,128)(2,1)} %param.11) | copy-start | bytes 196612
  98.3 18.2 %all-to-all-start.4 = ((bf16[64,8,128]{2,1,0:T(8,128)(2,1)}), bf16[64,8,128]{2,1,0:T(8,128)(2,1)S(1)}, u32[]{:S(2)}, u32[]{:S(2)}) async-start(bf16[64,8,128]{2,1,0:T(8,128)(2,1)} %after.1), calls=%async_computation.4 | async-start | bytes 262144 | tf_op jit(solution)/shard_map/all_to_all | solution.py:257
  117.9 20.4 %all-to-all-start.5 = ((bf16[128,8,128]{2,1,0:T(8,128)(2,1)}), bf16[128,8,128]{2,1,0:T(8,128)(2,1)S(1)}, u32[]{:S(2)}, u32[]{:S(2)}) async-start(bf16[128,8,128]{2,1,0:T(8,128)(2,1)} %get-tuple-element.38), calls=%async_computation.5 | async-start | bytes 524288 | tf_op jit(solution)/shard_map/all_to_all | solution.py:257
  123.5 6.2 %collective-permute-start.1 = (f32[8,256]{1,0:T(8,128)S(1)}, f32[8,256]{1,0:T(8,128)S(1)}, u32[]{:S(2)}, u32[]{:S(2)}) collective-permute-start(f32[8,256]{1,0:T(8,128)S(1)} %get-tuple-element.37), channel_id=1, source_target_pairs={{16,0},{32,16},{48,32},{64,48},{80,64},{96,80},{112,96},{128,112},... | collective-permute-start | bytes 24584 | tf_op jit(solution)/shard_map/ppermute | solution.py:253

commit v2 on v1

v2 whole, which is shorter than its diff:
```python
import jax
import jax.numpy as jnp
from jax import lax
from jax.experimental import pallas as pl
from jax.experimental.pallas import tpu as pltpu
from jax.sharding import Mesh
from jax.sharding import PartitionSpec as P

F = 16
E = 256
CONV = 3
POS = 128
ROWS = 160
SLAB = ("ctx_1", "ctx_2")
CTX = ("ctx_0", "ctx_1", "ctx_2")
CTX_BATCH = ("ctx_0", "ctx_1", "ctx_2", "batch")
BF = jnp.bfloat16
F32 = jnp.float32
eps_norm = 1e-05


def nn(a, b):
    return lax.dot_general(a, b, (((1,), (0,)), ((), ())), preferred_element_type=F32)


def nt(a, b):
    return lax.dot_general(a, b, (((1,), (1,)), ((), ())), preferred_element_type=F32)


def tn(a, b):
    return lax.dot_general(a, b, (((0,), (0,)), ((), ())), preferred_element_type=F32)


def call(body, outs, *args, flops=0, name=None):
    moved = sum(a.size * a.dtype.itemsize for a in (*args, *outs))
    return pl.pallas_call(
        body,
        out_shape=outs,
        in_specs=[
            pl.BlockSpec(memory_space=pltpu.SMEM if a.dtype == jnp.int32 else pltpu.VMEM) for a in args
        ],
        out_specs=[pl.BlockSpec(memory_space=pltpu.VMEM)] * len(outs),
        cost_estimate=pl.CostEstimate(flops=flops, bytes_accessed=moved, transcendentals=0),
        compiler_params=pltpu.CompilerParams(vmem_limit_bytes=16 << 20),
        name=name,
    )(*args)


def struct(shape, dtype):
    return jax.ShapeDtypeStruct(shape, dtype)


def shifted(w, s):
    return w if s % F == 0 else jnp.concatenate([w[s % F :], w[: s % F]], axis=0)


def rows_of(w):
    parts = [w]
    for s in range(8):
        parts.append(w * shifted(w, s))
    parts.append(w[:8] * w[8:])
    at = lax.broadcasted_iota(jnp.int32, (8, w.shape[1]), 0)
    parts.append(jnp.where(at == 0, 1.0, 0.0).astype(F32))
    return jnp.concatenate(parts, axis=0)


def gains():
    at = lax.broadcasted_iota(jnp.int32, (1, ROWS), 1)
    quad = jnp.where(at < 2 * F, 1.0 / 32.0, 1.0 / 16.0)
    return jnp.where(at < F, 0.25, jnp.where(at < 152, quad, 1.0)).astype(F32)


def eye(size):
    row = lax.broadcasted_iota(jnp.int32, (size, size), 0)
    col = lax.broadcasted_iota(jnp.int32, (size, size), 1)
    return jnp.where(row == col, 1.0, 0.0).astype(BF)


def rows_back(w, y):
    total = 0.25 * y[:F] + (1.0 / 16.0) * w * y[F : 2 * F]
    for s in range(1, 8):
        y_s = y[F * (s + 1) : F * (s + 2)]
        total = total + (1.0 / 16.0) * (
            shifted(w, s) * y_s + shifted(w, F - s) * shifted(y_s, F - s)
        )
    y_8 = y[144:152]
    half = jnp.concatenate([w[8:] * y_8, w[:8] * y_8], axis=0)
    return total + (1.0 / 16.0) * half


def turn_body(w_ref, out_ref):
    turned = nt(eye(w_ref.shape[1]), w_ref[...]).astype(BF)
    for part in range(out_ref.shape[0]):
        out_ref[part] = turned[32 * part : 32 * part + 32]


def values_body(val_ref, hval_ref, grad_ref, cv_ref, out_ref):
    v0 = val_ref[...].astype(F32)
    hv = hval_ref[...].astype(F32)
    at = lax.broadcasted_iota(jnp.int32, v0.shape, 0)
    last, before = (jnp.broadcast_to(hv[k : k + 1], v0.shape) for k in (7, 6))
    v1 = jnp.where(at == 0, last, pltpu.roll(v0, 1, 0))
    v2 = jnp.where(at == 0, before, jnp.where(at == 1, last, pltpu.roll(v0, 2, 0)))
    valued = (cv_ref[0:1] * v0 + cv_ref[1:2] * v1 + cv_ref[2:3] * v2).astype(BF)
    square = eye(E)
    out_ref[0] = nt(square, valued).astype(BF)
    out_ref[1] = nt(square, grad_ref[...]).astype(BF)


def spread_body(w_ref, tok_ref, htok_ref, turned_ref, cqk_ref, out_ref):
    parts, _, deep = w_ref.shape
    own = jnp.zeros((2 * F, POS), F32)
    rim = jnp.zeros((2 * F, htok_ref.shape[0]), F32)
    for part in range(parts):
        w = w_ref[part]
        own = own + nt(w, tok_ref[:, deep * part : deep * part + deep])
        rim = rim + nt(w, htok_ref[:, deep * part : deep * part + deep])
    x0 = own.astype(BF).astype(F32)
    h = rim.astype(BF).astype(F32)
    lane = lax.broadcasted_iota(jnp.int32, x0.shape, 1)
    last, before = (jnp.broadcast_to(h[:, k : k + 1], x0.shape) for k in (7, 6))
    x1 = jnp.where(lane == 0, last, pltpu.roll(x0, 1, 1))
    x2 = jnp.where(lane == 0, before, jnp.where(lane == 1, last, pltpu.roll(x0, 2, 1)))
    conv = (cqk_ref[0] * x0 + cqk_ref[1] * x1 + cqk_ref[2] * x2).astype(BF)
    for peer in range(out_ref.shape[0]):
        out_ref[peer, :32] = turned_ref[0, 32 * peer : 32 * peer + 32]
        out_ref[peer, 32:64] = turned_ref[1, 32 * peer : 32 * peer + 32]
        out_ref[peer, 64:] = conv


def state_body(in_ref, before_ref, krows_ref, out_ref):
    blocks = in_ref.shape[0]
    total = jnp.zeros((32, ROWS), F32)
    for b in range(blocks):
        k_rows = rows_of(in_ref[b, 80:].astype(F32)).astype(BF)
        krows_ref[b] = k_rows
        before_ref[b] = total
        total = total + nt(in_ref[b, :32], k_rows)
    total = total.astype(BF)
    for peer in range(out_ref.shape[0]):
        out_ref[peer] = total


def local_body(in_ref, mixed_ref, kernel_ref, slope_ref, qrows_ref):
    row = lax.broadcasted_iota(jnp.int32, (POS, POS), 0)
    col = lax.broadcasted_iota(jnp.int32, (POS, POS), 1)
    causal = row <= col
    for b in range(in_ref.shape[0]):
        queries = in_ref[b, 64:80]
        dotted = tn(in_ref[b, 80:], queries) * 0.25
        kernel = jnp.where(causal, 1.0 + dotted + 0.5 * dotted * dotted, 0.0).astype(BF)
        slope_ref[b] = jnp.where(causal, (1.0 + dotted) * 0.25, 0.0)
        kernel_ref[b] = kernel
        mixed_ref[b] = nn(in_ref[b, :32], kernel)
        qrows_ref[b] = rows_of(queries.astype(F32)).astype(BF)


def mix_body(at_ref, sums_ref, before_ref, in_ref, local_ref, qrows_ref, mixed_ref, prior_ref, out_ref):
    at = at_ref[0]
    total = jnp.zeros((32, ROWS), F32)
    for x in range(sums_ref.shape[0]):
        total = total + jnp.where(x < at, sums_ref[x].astype(F32), 0.0)
    gain = gains()
    squares, products = [], []
    for b in range(in_ref.shape[0]):
        prior = before_ref[b] + total
        prior_ref[b] = prior.astype(BF)
        mixed = local_ref[b] + nn((prior * gain).astype(BF), qrows_ref[b])
        mixed_ref[b] = mixed
        squares.append(jnp.sum(mixed * mixed, axis=0, keepdims=True))
        products.append(jnp.sum(in_ref[b, 32:64].astype(F32) * mixed, axis=0, keepdims=True))
    rows = jnp.concatenate(squares + products, axis=0)
    for peer in range(out_ref.shape[0]):
        out_ref[peer] = rows


def norm_body(sums_ref, in_ref, mixed_ref, qrows_ref, att_ref, dmix_ref, after_ref, out_ref):
    rows = sums_ref[0]
    for peer in range(1, sums_ref.shape[0]):
        rows = rows + sums_ref[peer]
    rows = rows * (1.0 / E)
    blocks = in_ref.shape[0]
    total = jnp.zeros((32, ROWS), F32)
    for b in reversed(range(blocks)):
        inv = lax.rsqrt(rows[b : b + 1] + eps_norm)
        normed = mixed_ref[b] * inv
        att_ref[b] = normed.astype(BF)
        grad = in_ref[b, 32:64].astype(F32)
        d_mixed = (inv * (grad - normed * (inv * rows[blocks + b : blocks + b + 1]))).astype(BF)
        dmix_ref[b] = d_mixed
        after_ref[b] = total
        total = total + nt(d_mixed, qrows_ref[b])
    total = total.astype(BF)
    for peer in range(out_ref.shape[0]):
        out_ref[peer] = total


def back_body(in_ref, kernel_ref, slope_ref, dmix_ref, prior_ref, dqk_ref, dval_ref):
    for b in range(in_ref.shape[0]):
        queries, keys = in_ref[b, 64:80], in_ref[b, 80:]
        d_mixed = dmix_ref[b]
        d_score = (tn(in_ref[b, :32], d_mixed) * slope_ref[b]).astype(BF)
        dqk_ref[b, :F] = nn(keys, d_score) + rows_back(queries.astype(F32), tn(prior_ref[b], d_mixed))
        dqk_ref[b, F:] = nt(queries, d_score)
        dval_ref[b] = nt(d_mixed, kernel_ref[b])


def later_body(at_ref, sums_ref, after_ref, in_ref, krows_ref, dqk_ref, dval_ref, att_ref, out_ref):
    at = at_ref[0]
    total = jnp.zeros((32, ROWS), F32)
    for x in range(sums_ref.shape[0]):
        total = total + jnp.where(x > at, sums_ref[x].astype(F32), 0.0)
    gain = gains()
    for b in range(in_ref.shape[0]):
        later = after_ref[b] + total
        out_ref[b, :F] = dqk_ref[b, :F].astype(BF)
        keys = in_ref[b, 80:].astype(F32)
        d_key = dqk_ref[b, F:] + rows_back(keys, tn(later.astype(BF), in_ref[b, :32]))
        out_ref[b, F : 2 * F] = d_key.astype(BF)
        out_ref[b, 32:64] = att_ref[b]
        out_ref[b, 64:] = (dval_ref[b] + nn((later * gain).astype(BF), krows_ref[b])).astype(BF)


def grad_body(sums_ref, tok_ref, htok_ref, cqk_ref, out_ref):
    d = sums_ref[0, : 2 * F].astype(F32)
    for peer in range(1, sums_ref.shape[0]):
        d = d + sums_ref[peer, : 2 * F].astype(F32)
    lane = lax.broadcasted_iota(jnp.int32, d.shape, 1)
    d1, d2 = cqk_ref[1] * d, cqk_ref[2] * d
    own = cqk_ref[0] * d
    own = own + jnp.where(lane < POS - 1, pltpu.roll(d1, POS - 1, 1), 0.0)
    own = own + jnp.where(lane < POS - 2, pltpu.roll(d2, POS - 2, 1), 0.0)
    to_last = pltpu.roll(d2, 6, 1)
    rim = jnp.where(lane == 6, to_last, jnp.where(lane == 7, pltpu.roll(d1, 7, 1) + to_last, 0.0))
    own_b, rim_b = own.astype(BF), rim[:, :8].astype(BF)
    group = lax.broadcasted_iota(jnp.int32, (8, 128), 1) // 32
    chunk = 512
    for start in range(0, tok_ref.shape[1], chunk):
        part = nn(own_b, tok_ref[:, start : start + chunk]) + nn(rim_b, htok_ref[:, start : start + chunk])
        for at_lane in range(0, chunk, 128):
            blocks = [part[8 * i : 8 * i + 8, at_lane : at_lane + 128] for i in range(4)]
            for q in range(4):
                moved = [pltpu.roll(b, 32 * ((i - q) % 4), 1) if i != q else b for i, b in enumerate(blocks)]
                packed = jnp.where(
                    group == 0, moved[0], jnp.where(group == 1, moved[1], jnp.where(group == 2, moved[2], moved[3]))
                )
                out_ref[(start + at_lane) // 32 + q] = packed.astype(out_ref.dtype)


def return_body(in_ref, cv_ref, att_ref, gval_ref, head_ref):
    square = eye(POS)
    peers = range(in_ref.shape[0])
    att = jnp.concatenate([in_ref[j, 32:64] for j in peers], axis=0)
    d_rows = jnp.concatenate([in_ref[j, 64:] for j in peers], axis=0)
    att_ref[...] = nt(square, att).astype(BF)
    dv = nt(square, d_rows)
    head_ref[...] = dv[:8]
    at = lax.broadcasted_iota(jnp.int32, dv.shape, 0)
    gval = cv_ref[0:1] * dv
    gval = gval + cv_ref[1:2] * jnp.where(at < POS - 1, pltpu.roll(dv, POS - 1, 0), 0.0)
    gval = gval + cv_ref[2:3] * jnp.where(at < POS - 2, pltpu.roll(dv, POS - 2, 0), 0.0)
    gval_ref[...] = gval


def rim_body(gval_ref, next_ref, cv_ref, out_ref):
    out_ref[...] = gval_ref[...].astype(BF)
    nxt = next_ref[...]
    at = lax.broadcasted_iota(jnp.int32, nxt.shape, 0)
    c1, c2 = cv_ref[1:2], cv_ref[2:3]
    first, second = (jnp.broadcast_to(nxt[k : k + 1], nxt.shape) for k in (0, 1))
    more = jnp.where(at == 6, c2 * first, jnp.where(at == 7, c1 * first + c2 * second, 0.0))
    out_ref[POS - 8 :] = (gval_ref[POS - 8 :] + more).astype(BF)


def sum_body(parts_ref, out_ref, *, scale):
    totals = [parts_ref[k].astype(F32) for k in range(8)]
    for k in range(8, parts_ref.shape[0]):
        totals[k % 8] = totals[k % 8] + parts_ref[k].astype(F32)
    while len(totals) > 1:
        totals = [a + b for a, b in zip(totals[::2], totals[1::2])]
    total = totals[0] * scale
    stacked = jnp.concatenate([total] + [pltpu.roll(total, 128 - 32 * i, 1) for i in (1, 2, 3)], axis=0)
    square = jnp.concatenate([stacked, jnp.zeros((96, 128), F32)], axis=0).T
    out_ref[...] = square[:32, :32]


def to_next(value, axes, by):
    size = lax.axis_size(axes)
    pairs = [(i, i + by) for i in range(size) if 0 <= i + by < size]
    return lax.ppermute(value, axes, pairs)


def exchange(value, axes):
    return lax.all_to_all(value, axes, split_axis=0, concat_axis=0, tiled=True)


def shards(inputs, values, w_qk, conv_qk, conv_v, d_attn):
    tokens, own_values = inputs[0], values[0]
    depth = tokens.shape[1]
    splits = lax.axis_size("fsdp")
    lines = lax.axis_size("ctx_0")
    blocks = lax.axis_size(SLAB)
    peers = lax.axis_size(CTX_BATCH)
    deep = w_qk.shape[0]
    place = lax.axis_index("ctx_0").astype(jnp.int32).reshape(1)

    (turned,) = call(turn_body, [struct((splits, 2 * F, deep), BF)], w_qk, name="turn")
    weights = exchange(turned, "fsdp")
    rim = to_next(jnp.concatenate([tokens[POS - 8 :], own_values[POS - 8 :]], axis=1), CTX, 1)
    rim_tokens, rim_values = rim[:, :depth], rim[:, depth:]
    taps = jnp.broadcast_to(conv_qk[:, :, None], (CONV, 2 * F, POS))

    (value_rows,) = call(
        values_body, [struct((2, E, POS), BF)], own_values, rim_values, d_attn[0], conv_v, name="values"
    )
    (spread,) = call(
        spread_body, [struct((blocks, 96, POS), BF)], weights, tokens, rim_tokens, value_rows, taps, name="spread"
    )
    slab = exchange(spread, SLAB)
    before, k_rows, state = call(
        state_body,
        [struct((blocks, 32, ROWS), F32), struct((blocks, ROWS, POS), BF), struct((lines, 32, ROWS), BF)],
        slab,
        name="state",
    )
    states = exchange(state, "ctx_0")
    mixed_own, kernel, slope, q_rows = call(
        local_body,
        [
            struct((blocks, 32, POS), F32), struct((blocks, POS, POS), BF),
            struct((blocks, POS, POS), F32), struct((blocks, ROWS, POS), BF),
        ],
        slab,
        flops=2 * blocks * POS * POS * 48, name="local",
    )
    mixed, prior, norm = call(
        mix_body,
        [struct((blocks, 32, POS), F32), struct((blocks, 32, ROWS), BF), struct((blocks, 2 * blocks, POS), F32)],
        place, states, before, slab, mixed_own, q_rows,
        name="mix",
    )
    norms = exchange(norm, SLAB)
    att_rows, d_mixed, after, grad_state = call(
        norm_body,
        [
            struct((blocks, 32, POS), BF), struct((blocks, 32, POS), BF),
            struct((blocks, 32, ROWS), F32), struct((lines, 32, ROWS), BF),
        ],
        norms, slab, mixed, q_rows,
        name="norm",
    )
    grad_states = exchange(grad_state, "ctx_0")
    d_qk, d_val = call(
        back_body,
        [struct((blocks, 32, POS), F32), struct((blocks, 32, POS), F32)],
        slab, kernel, slope, d_mixed, prior,
        flops=2 * blocks * POS * POS * 128, name="back",
    )
    (parts,) = call(
        later_body,
        [struct((blocks, 96, POS), BF)],
        place, grad_states, after, slab, k_rows, d_qk, d_val, att_rows,
        name="later",
    )
    home = exchange(parts, SLAB)
    (grad_parts,) = call(
        grad_body,
        [struct((peers, 8, 128), BF)],
        home, tokens, rim_tokens, taps,
        flops=2 * POS * depth * 2 * F, name="grad",
    )
    arrived = exchange(grad_parts, CTX_BATCH)
    home, _ = lax.optimization_barrier((home, grad_parts))
    attended, g_val, head = call(
        return_body, [struct((POS, E), BF), struct((POS, E), F32), struct((8, E), F32)], home, conv_v, name="return"
    )
    next_rows = to_next(head, CTX, -1)
    (grad_v,) = call(rim_body, [struct((POS, E), BF)], g_val, next_rows, conv_v, name="rim")
    scale = float(POS * peers) ** (-0.5)
    (grad_w,) = call(
        lambda a, b: sum_body(a, b, scale=scale), [struct((2 * F, 2 * F), F32)], arrived, name="sum"
    )
    return (attended[None], grad_v[None], grad_w)


def solution(mesh):
    split = Mesh(
        mesh.devices.reshape(8, 4, 2, mesh.shape["fsdp"], mesh.shape["batch"]),
        ("ctx_0", "ctx_1", "ctx_2", "fsdp", "batch"),
    )
    in_specs = (
        P("batch", CTX, None),
        P("batch", CTX, "fsdp"),
        P("fsdp", None),
        P(None, "fsdp"),
        P(None, "fsdp"),
        P("batch", CTX, "fsdp"),
    )
    out_specs = (P("batch", CTX, "fsdp"), P("batch", CTX, "fsdp"), P(CTX_BATCH, "fsdp"))
    return jax.shard_map(
        shards, mesh=split, in_specs=in_specs, out_specs=out_specs, check_vma=False
    )
```

time: 140 us -> 129 us (0.921)
  waiting for transfers between devices: 42.4 us -> 28.2 us
  starting transfers between devices: 39.9 us -> 42.8 us
  Pallas kernels: 7.57 us -> 9.8 us
    all_to_all x4, waiting for transfers between devices: 37.8 us -> 23.6 us  [exchange(): return lax.all_to_all(value, axes, split_axis=0, concat_axis=0, tiled=True)]
    all_to_all x4, starting transfers between devices: 31.7 us -> 34.5 us  [exchange(): return lax.all_to_all(value, axes, split_axis=0, concat_axis=0, tiled=True)]
    pallas_call x10 -> x13, Pallas kernels: 7.57 us -> 9.8 us  [call(): pl.pallas_call(body, out_shape=outs, in_specs=[pl.BlockSpec(memory_space=...]
    all_to_all x2 -> x3, blocking collectives: 46 us -> 45.1 us  [exchange(): return lax.all_to_all(value, axes, split_axis=0, concat_axis=0, tiled=True)]
  transfers between devices with their start and end apart: 6 -> 6, of which waited for: 6 -> 6; matrix products, arithmetic and copies ran while one was open for 1% -> 1% of each run, Pallas kernels for 1% -> 3%
where the time goes in v2:
time: 129 us; the launch traced here: 128 us
  blocking collectives  45.1 us (35%)
  starting transfers between devices  42.8 us (33%)
  waiting for transfers between devices  28.2 us (22%)
  Pallas kernels  9.8 us (8%)
  local copies, waits for them, and re-layouts  1.83 us (1%)
    all_to_all x3, blocking collectives, exchange(): return lax.all_to_all(value, axes, split_axis=0, concat_axis=0, tiled=True)  45.1 us
    all_to_all x4, starting transfers between devices, exchange(): return lax.all_to_all(value, axes, split_axis=0, concat_axis=0, tiled=True)  34.5 us
    all_to_all x4, waiting for transfers between devices, exchange(): return lax.all_to_all(value, axes, split_axis=0, concat_axis=0, tiled=True)  23.6 us
    pallas_call x13, Pallas kernels, call(): pl.pallas_call(body, out_shape=outs, in_specs=[pl.BlockSpec(memory_space=...  9.8 us
    ppermute x2, starting transfers between devices, to_next(): return lax.ppermute(value, axes, pairs)  8.31 us
    ppermute x2, waiting for transfers between devices, to_next(): return lax.ppermute(value, axes, pairs)  4.6 us
  transfers between devices with their start and end apart: 6, of which 6 were waited for; matrix products, arithmetic and copies ran while one was open for 1% of the time, Pallas kernels for 3%

profile of v2, /device:TPU:1, one launch (start us, length us, event | category | flops | bytes accessed | tf_op | source)
XLA Modules:
  0.0 128.5 jit_solution(14666422445577830097)
XLA Ops:
  0.6 1.0 copy-done.1
  1.7 1.0 turn.1
  2.6 17.2 %all-to-all-start = ((bf16[8,32,512]{2,1,0:T(8,128)(2,1)}), bf16[8,32,512]{2,1,0:T(8,128)(2,1)S(1)}, u32[]{:S(2)}, u32[]{:S(2)}) async-start(bf16[8,32,512]{2,1,0:T(8,128)(2,1)} %turn.1), calls=%async_computation | async-start | bytes 524288 | tf_op jit(solution)/shard_map/all_to_all | solution.py:294
  19.9 0.7 slice_bitcast_fusion.1
  20.6 5.4 %collective-permute-start = (bf16[8,4352]{1,0:T(8,128)(2,1)S(1)}, bf16[8,4352]{1,0:T(8,128)(2,1)S(1)}, u32[]{:S(2)}, u32[]{:S(2)}) collective-permute-start(bf16[8,4352]{1,0:T(8,128)(2,1)S(1)} %pad_maximum_fusion), channel_id=1, source_target_pairs={{0,16},{16,32},{32,48},{48,64},{64,80},{80,96},{96,112},{112,128},... | collective-permute-start | bytes 208904 | tf_op jit(solution)/shard_map/ppermute | solution.py:290
  26.0 1.3 %collective-permute-done = bf16[8,4352]{1,0:T(8,128)(2,1)S(1)} collective-permute-done((bf16[8,4352]{1,0:T(8,128)(2,1)S(1)}, bf16[8,4352]{1,0:T(8,128)(2,1)S(1)}, u32[]{:S(2)}, u32[]{:S(2)}) %collective-permute-start) | collective-permute-done | bytes 69664 | tf_op jit(solution)/shard_map/ppermute | solution.py:290
  27.7 2.7 %all-to-all-done.w_ref = bf16[8,32,512]{2,1,0:T(8,128)(2,1)S(1)} async-done(((bf16[8,32,512]{2,1,0:T(8,128)(2,1)}), bf16[8,32,512]{2,1,0:T(8,128)(2,1)S(1)}, u32[]{:S(2)}, u32[]{:S(2)}) %all-to-all-start) | async-done | bytes 262176 | tf_op jit(solution)/shard_map/all_to_all | solution.py:294
  31.0 18.3 %all_to_all.35.in_ref = bf16[8,96,128]{2,1,0:T(8,128)(2,1)S(1)} all-to-all(bf16[8,96,128]{2,1,0:T(8,128)(2,1)S(1)} %spread.1), channel_id=1, replica_groups=mesh['ctx_0'=8,'ctx_1'=4,'ctx_2'=2,'fsdp'=8,'batch'=2] {'ctx_1','ctx_2'}, dimensions={0} | all-to-all | bytes 393216 | tf_op jit(solution)/shard_map/all_to_all | solution.py:294
  49.3 1.0 state.1
  50.3 6.5 %all-to-all-start.2 = ((bf16[8,32,160]{2,1,0:T(8,128)(2,1)}), bf16[8,32,160]{2,1,0:T(8,128)(2,1)S(1)}, u32[]{:S(2)}, u32[]{:S(2)}) async-start(bf16[8,32,160]{2,1,0:T(8,128)(2,1)} %get-tuple-element.23), calls=%async_computation.2 | async-start | bytes 262144 | tf_op jit(solution)/shard_map/all_to_all | solution.py:294
  57.3 7.6 %all-to-all-done.2.sums_ref = bf16[8,32,160]{2,1,0:T(8,128)(2,1)S(1)} async-done(((bf16[8,32,160]{2,1,0:T(8,128)(2,1)}), bf16[8,32,160]{2,1,0:T(8,128)(2,1)S(1)}, u32[]{:S(2)}, u32[]{:S(2)}) %all-to-all-start.2) | async-done | bytes 81952 | tf_op jit(solution)/shard_map/all_to_all | solution.py:294
  65.1 13.5 %all_to_all.36.sums_ref = f32[8,16,128]{2,1,0:T(8,128)S(1)} all-to-all(f32[8,16,128]{2,1,0:T(8,128)S(1)} %get-tuple-element.27), channel_id=1, replica_groups=mesh['ctx_0'=8,'ctx_1'=4,'ctx_2'=2,'fsdp'=8,'batch'=2] {'ctx_1','ctx_2'}, dimensions={0} | all-to-all | bytes 131072 | tf_op jit(solution)/shard_map/all_to_all | solution.py:294
  78.5 1.0 norm.1
  79.5 3.4 %all-to-all-start.4 = ((bf16[8,32,160]{2,1,0:T(8,128)(2,1)}), bf16[8,32,160]{2,1,0:T(8,128)(2,1)S(1)}, u32[]{:S(2)}, u32[]{:S(2)}) async-start(bf16[8,32,160]{2,1,0:T(8,128)(2,1)} %get-tuple-element.29), calls=%async_computation.4 | async-start | bytes 262144 | tf_op jit(solution)/shard_map/all_to_all | solution.py:294
  82.9 1.4 %back.1 = (f32[8,32,128]{2,1,0:T(8,128)S(1)}, f32[8,32,128]{2,1,0:T(8,128)S(1)}) custom-call(bf16[8,96,128]{2,1,0:T(8,128)(2,1)S(1)} %all_to_all.35.in_ref, bf16[8,128,128]{2,1,0:T(8,128)(2,1)S(1)} %get-tuple-element.32.kernel_ref, f32[8,128,128]{2,1,0:T(8,128)S(1)} %get-tuple-element.33.slope_ref, bf16[8,32,128]{2,1,0:T(8,128)(2,1)S(1)} %get-tuple-element.34.dmix_ref, ...), custom_call_target="tpu_custom_call" | custom-call | flops 33554432 | bytes 1392640 | tf_op jit(solution)/shard_map/back/pallas_call | solution.py:36
  84.3 6.2 %all-to-all-done.4.sums_ref = bf16[8,32,160]{2,1,0:T(8,128)(2,1)S(1)} async-done(((bf16[8,32,160]{2,1,0:T(8,128)(2,1)}), bf16[8,32,160]{2,1,0:T(8,128)(2,1)S(1)}, u32[]{:S(2)}, u32[]{:S(2)}) %all-to-all-start.4) | async-done | bytes 81952 | tf_op jit(solution)/shard_map/all_to_all | solution.py:294
  90.9 13.3 %all_to_all.37.sums_ref.in_ref = bf16[8,96,128]{2,1,0:T(8,128)(2,1)S(1)} all-to-all(bf16[8,96,128]{2,1,0:T(8,128)(2,1)S(1)} %later.1), channel_id=1, replica_groups=mesh['ctx_0'=8,'ctx_1'=4,'ctx_2'=2,'fsdp'=8,'batch'=2] {'ctx_1','ctx_2'}, dimensions={0} | all-to-all | bytes 393216 | tf_op jit(solution)/shard_map/all_to_all | solution.py:294
  104.2 1.3 %grad.1 = bf16[128,8,128]{2,1,0:T(8,128)(2,1)} custom-call(bf16[8,96,128]{2,1,0:T(8,128)(2,1)S(1)} %all_to_all.37.sums_ref.in_ref, bf16[128,4096]{1,0:T(8,128)(2,1)S(1)} %bitcast.11, bf16[8,4096]{1,0:T(8,128)(2,1)S(1)} %slice.24.htok_ref, f32[3,32,128]{2,1,0:T(8,128)S(1)} %broadcast_in_dim.12.cqk_ref), custom_call_target="tpu_custom_call" | custom-call | flops 33554432 | bytes 1622016 | tf_op jit(solution)/shard_map/grad/pallas_call | solution.py:36
  105.5 7.4 %all-to-all-start.6 = ((bf16[128,8,128]{2,1,0:T(8,128)(2,1)}), bf16[128,8,128]{2,1,0:T(8,128)(2,1)S(1)}, u32[]{:S(2)}, u32[]{:S(2)}) async-start(bf16[128,8,128]{2,1,0:T(8,128)(2,1)} %grad.1), calls=%async_computation.6 | async-start | bytes 524288 | tf_op jit(solution)/shard_map/all_to_all | solution.py:294
  112.9 0.8 return.1
  113.8 2.9 %collective-permute-start.1 = (f32[8,256]{1,0:T(8,128)S(1)}, f32[8,256]{1,0:T(8,128)S(1)}, u32[]{:S(2)}, u32[]{:S(2)}) collective-permute-start(f32[8,256]{1,0:T(8,128)S(1)} %get-tuple-element.42), channel_id=1, source_target_pairs={{16,0},{32,16},{48,32},{64,48},{80,64},{96,80},{112,96},{128,112},... | collective-permute-start | bytes 24584 | tf_op jit(solution)/shard_map/ppermute | solution.py:290
  116.7 3.2 %collective-permute-done.1.next_ref = f32[8,256]{1,0:T(8,128)S(1)} collective-permute-done((f32[8,256]{1,0:T(8,128)S(1)}, f32[8,256]{1,0:T(8,128)S(1)}, u32[]{:S(2)}, u32[]{:S(2)}) %collective-permute-start.1) | collective-permute-done | bytes 8224 | tf_op jit(solution)/shard_map/ppermute | solution.py:290
  120.5 7.2 %all-to-all-done.6.a = bf16[128,8,128]{2,1,0:T(8,128)(2,1)S(1)} async-done(((bf16[128,8,128]{2,1,0:T(8,128)(2,1)}), bf16[128,8,128]{2,1,0:T(8,128)(2,1)S(1)}, u32[]{:S(2)}, u32[]{:S(2)}) %all-to-all-start.6) | async-done | bytes 262176 | tf_op jit(solution)/shard_map/all_to_all | solution.py:294
  127.7 0.8 sum.1
  (22 shorter events, 2.7 us)
Async XLA Ops:
  0.6 19.9 %copy-start = (bf16[1,128,4096]{2,1,0:T(8,128)(2,1)S(1)}, bf16[1,128,4096]{2,1,0:T(8,128)(2,1)}, u32[]{:S(2)}) copy-start(bf16[1,128,4096]{2,1,0:T(8,128)(2,1)} %param.6) | copy-start | bytes 3145732
  0.6 1.0 copy-start.1
  2.6 27.7 %all-to-all-start = ((bf16[8,32,512]{2,1,0:T(8,128)(2,1)}), bf16[8,32,512]{2,1,0:T(8,128)(2,1)S(1)}, u32[]{:S(2)}, u32[]{:S(2)}) async-start(bf16[8,32,512]{2,1,0:T(8,128)(2,1)} %turn.1), calls=%async_computation | async-start | bytes 524288 | tf_op jit(solution)/shard_map/all_to_all | solution.py:294
  20.6 6.8 %copy-start.2 = (bf16[1,128,256]{2,1,0:T(8,128)(2,1)S(1)}, bf16[1,128,256]{2,1,0:T(8,128)(2,1)}, u32[]{:S(2)}) copy-start(bf16[1,128,256]{2,1,0:T(8,128)(2,1)} %param.7) | copy-start | bytes 196612
  20.6 6.8 %copy-start.3 = (bf16[1,128,256]{2,1,0:T(8,128)(2,1)S(1)}, bf16[1,128,256]{2,1,0:T(8,128)(2,1)}, u32[]{:S(2)}) copy-start(bf16[1,128,256]{2,1,0:T(8,128)(2,1)} %param.11) | copy-start | bytes 196612
  20.6 6.8 %copy-start.4 = (f32[3,256]{1,0:T(4,128)S(1)}, f32[3,256]{1,0:T(4,128)}, u32[]{:S(2)}) copy-start(f32[3,256]{1,0:T(4,128)} %cv_ref.5) | copy-start | bytes 9220
  20.6 6.8 %collective-permute-start = (bf16[8,4352]{1,0:T(8,128)(2,1)S(1)}, bf16[8,4352]{1,0:T(8,128)(2,1)S(1)}, u32[]{:S(2)}, u32[]{:S(2)}) collective-permute-start(bf16[8,4352]{1,0:T(8,128)(2,1)S(1)} %pad_maximum_fusion), channel_id=1, source_target_pairs={{0,16},{16,32},{32,48},{48,64},{64,80},{80,96},{96,112},{112,128},... | collective-permute-start | bytes 208904 | tf_op jit(solution)/shard_map/ppermute | solution.py:290
  27.7 2.7 %copy-start.5 = (f32[3,32]{1,0:T(4,128)S(1)}, f32[3,32]{1,0:T(4,128)}, u32[]{:S(2)}) copy-start(f32[3,32]{1,0:T(4,128)} %param.9) | copy-start | bytes 1156
  50.3 14.5 %all-to-all-start.2 = ((bf16[8,32,160]{2,1,0:T(8,128)(2,1)}), bf16[8,32,160]{2,1,0:T(8,128)(2,1)S(1)}, u32[]{:S(2)}, u32[]{:S(2)}) async-start(bf16[8,32,160]{2,1,0:T(8,128)(2,1)} %get-tuple-element.23), calls=%async_computation.2 | async-start | bytes 262144 | tf_op jit(solution)/shard_map/all_to_all | solution.py:294
  79.5 11.0 %all-to-all-start.4 = ((bf16[8,32,160]{2,1,0:T(8,128)(2,1)}), bf16[8,32,160]{2,1,0:T(8,128)(2,1)S(1)}, u32[]{:S(2)}, u32[]{:S(2)}) async-start(bf16[8,32,160]{2,1,0:T(8,128)(2,1)} %get-tuple-element.29), calls=%async_computation.4 | async-start | bytes 262144 | tf_op jit(solution)/shard_map/all_to_all | solution.py:294
  105.5 22.2 %all-to-all-start.6 = ((bf16[128,8,128]{2,1,0:T(8,128)(2,1)}), bf16[128,8,128]{2,1,0:T(8,128)(2,1)S(1)}, u32[]{:S(2)}, u32[]{:S(2)}) async-start(bf16[128,8,128]{2,1,0:T(8,128)(2,1)} %grad.1), calls=%async_computation.6 | async-start | bytes 524288 | tf_op jit(solution)/shard_map/all_to_all | solution.py:294
  113.8 6.2 %collective-permute-start.1 = (f32[8,256]{1,0:T(8,128)S(1)}, f32[8,256]{1,0:T(8,128)S(1)}, u32[]{:S(2)}, u32[]{:S(2)}) collective-permute-start(f32[8,256]{1,0:T(8,128)S(1)} %get-tuple-element.42), channel_id=1, source_target_pairs={{16,0},{32,16},{48,32},{64,48},{80,64},{96,80},{112,96},{128,112},... | collective-permute-start | bytes 24584 | tf_op jit(solution)/shard_map/ppermute | solution.py:290

commit v3 on v2

--- a/solution.py
+++ b/solution.py
@@ -94,7 +94,13 @@
         out_ref[part] = turned[32 * part : 32 * part + 32]
 
 
-def values_body(val_ref, hval_ref, grad_ref, cv_ref, out_ref):
+def values_body(val_ref, hval_ref, grad_ref, cv_ref, cqk_ref, out_ref, taps_ref):
+    width = cqk_ref.shape[1]
+    row = lax.broadcasted_iota(jnp.int32, (width, width), 0)
+    col = lax.broadcasted_iota(jnp.int32, (width, width), 1)
+    for tap in range(CONV):
+        spread = jnp.where(row == col, jnp.broadcast_to(cqk_ref[tap : tap + 1], (width, width)), 0.0)
+        taps_ref[tap] = jnp.broadcast_to(jnp.sum(spread, axis=1, keepdims=True), (width, POS))
     v0 = val_ref[...].astype(F32)
     hv = hval_ref[...].astype(F32)
     at = lax.broadcasted_iota(jnp.int32, v0.shape, 0)
@@ -128,6 +134,16 @@
         out_ref[peer, 64:] = conv
 
 
+def pack(total):
+    side = [total[8 * i : 8 * i + 8, POS:] for i in range(4)]
+    return jnp.concatenate([total[:, :POS], jnp.concatenate(side, axis=1)], axis=0)
+
+
+def unpack(packed):
+    side = jnp.concatenate([packed[32:, 32 * i : 32 * i + 32] for i in range(4)], axis=0)
+    return jnp.concatenate([packed[:32], side], axis=1)
+
+
 def state_body(in_ref, before_ref, krows_ref, out_ref):
     blocks = in_ref.shape[0]
     total = jnp.zeros((32, ROWS), F32)
@@ -136,7 +152,7 @@
         krows_ref[b] = k_rows
         before_ref[b] = total
         total = total + nt(in_ref[b, :32], k_rows)
-    total = total.astype(BF)
+    total = pack(total).astype(BF)
     for peer in range(out_ref.shape[0]):
         out_ref[peer] = total
 
@@ -157,9 +173,10 @@
 
 def mix_body(at_ref, sums_ref, before_ref, in_ref, local_ref, qrows_ref, mixed_ref, prior_ref, out_ref):
     at = at_ref[0]
-    total = jnp.zeros((32, ROWS), F32)
+    total = jnp.zeros(sums_ref.shape[1:], F32)
     for x in range(sums_ref.shape[0]):
         total = total + jnp.where(x < at, sums_ref[x].astype(F32), 0.0)
+    total = unpack(total)
     gain = gains()
     squares, products = [], []
     for b in range(in_ref.shape[0]):
@@ -190,7 +207,7 @@
         dmix_ref[b] = d_mixed
         after_ref[b] = total
         total = total + nt(d_mixed, qrows_ref[b])
-    total = total.astype(BF)
+    total = pack(total).astype(BF)
     for peer in range(out_ref.shape[0]):
         out_ref[peer] = total
 
@@ -207,9 +224,10 @@
 
 def later_body(at_ref, sums_ref, after_ref, in_ref, krows_ref, dqk_ref, dval_ref, att_ref, out_ref):
     at = at_ref[0]
-    total = jnp.zeros((32, ROWS), F32)
+    total = jnp.zeros(sums_ref.shape[1:], F32)
     for x in range(sums_ref.shape[0]):
         total = total + jnp.where(x > at, sums_ref[x].astype(F32), 0.0)
+    total = unpack(total)
     gain = gains()
     for b in range(in_ref.shape[0]):
         later = after_ref[b] + total
@@ -308,10 +326,12 @@
     weights = exchange(turned, "fsdp")
     rim = to_next(jnp.concatenate([tokens[POS - 8 :], own_values[POS - 8 :]], axis=1), CTX, 1)
     rim_tokens, rim_values = rim[:, :depth], rim[:, depth:]
-    taps = jnp.broadcast_to(conv_qk[:, :, None], (CONV, 2 * F, POS))
-
-    (value_rows,) = call(
-        values_body, [struct((2, E, POS), BF)], own_values, rim_values, d_attn[0], conv_v, name="values"
+
+    value_rows, taps = call(
+        values_body,
+        [struct((2, E, POS), BF), struct((CONV, 2 * F, POS), F32)],
+        own_values, rim_values, d_attn[0], conv_v, conv_qk,
+        name="values",
     )
     (spread,) = call(
         spread_body, [struct((blocks, 96, POS), BF)], weights, tokens, rim_tokens, value_rows, taps, name="spread"
@@ -319,7 +339,7 @@
     slab = exchange(spread, SLAB)
     before, k_rows, state = call(
         state_body,
-        [struct((blocks, 32, ROWS), F32), struct((blocks, ROWS, POS), BF), struct((lines, 32, ROWS), BF)],
+        [struct((blocks, 32, ROWS), F32), struct((blocks, ROWS, POS), BF), struct((lines, 40, POS), BF)],
         slab,
         name="state",
     )
@@ -344,7 +364,7 @@
         norm_body,
         [
             struct((blocks, 32, POS), BF), struct((blocks, 32, POS), BF),
-            struct((blocks, 32, ROWS), F32), struct((lines, 32, ROWS), BF),
+            struct((blocks, 32, ROWS), F32), struct((lines, 40, POS), BF),
         ],
         norms, slab, mixed, q_rows,
         name="norm",

time: 129 us -> 128 us (level)
  waiting for transfers between devices: 28.2 us -> 26.6 us
    all_to_all x4, waiting for transfers between devices: 23.6 us -> 22 us  [exchange(): return lax.all_to_all(value, axes, split_axis=0, concat_axis=0, tiled=True)]
where the time goes in v3:
time: 128 us
  blocking collectives  44.8 us (35%)
  starting transfers between devices  42.9 us (34%)
  waiting for transfers between devices  26.6 us (21%)
  Pallas kernels  10 us (8%)
  local copies, waits for them, and re-layouts  2.42 us (2%)
    all_to_all x3, blocking collectives, exchange(): return lax.all_to_all(value, axes, split_axis=0, concat_axis=0, tiled=True)  44.8 us
    all_to_all x4, starting transfers between devices, exchange(): return lax.all_to_all(value, axes, split_axis=0, concat_axis=0, tiled=True)  34.6 us
    all_to_all x4, waiting for transfers between devices, exchange(): return lax.all_to_all(value, axes, split_axis=0, concat_axis=0, tiled=True)  22 us
    pallas_call x13, Pallas kernels, call(): pl.pallas_call(body, out_shape=outs, in_specs=[pl.BlockSpec(memory_space=...  10 us
    ppermute x2, starting transfers between devices, to_next(): return lax.ppermute(value, axes, pairs)  8.31 us
    ppermute x2, waiting for transfers between devices, to_next(): return lax.ppermute(value, axes, pairs)  4.6 us
  transfers between devices with their start and end apart: 6, of which 6 were waited for; matrix products, arithmetic and copies ran while one was open for 1% of the time, Pallas kernels for 3%

profile of v3, /device:TPU:1, one launch (start us, length us, event | category | flops | bytes accessed | tf_op | source)
XLA Modules:
  0.0 127.6 jit_solution(15795749476433637522)
XLA Ops:
  0.6 1.0 copy-done.1
  1.7 1.0 turn.1
  2.6 17.2 %all-to-all-start = ((bf16[8,32,512]{2,1,0:T(8,128)(2,1)}), bf16[8,32,512]{2,1,0:T(8,128)(2,1)S(1)}, u32[]{:S(2)}, u32[]{:S(2)}) async-start(bf16[8,32,512]{2,1,0:T(8,128)(2,1)} %turn.1), calls=%async_computation | async-start | bytes 524288 | tf_op jit(solution)/shard_map/all_to_all | solution.py:312
  19.9 0.7 slice_bitcast_fusion.1
  20.6 5.4 %collective-permute-start = (bf16[8,4352]{1,0:T(8,128)(2,1)S(1)}, bf16[8,4352]{1,0:T(8,128)(2,1)S(1)}, u32[]{:S(2)}, u32[]{:S(2)}) collective-permute-start(bf16[8,4352]{1,0:T(8,128)(2,1)S(1)} %pad_maximum_fusion), channel_id=1, source_target_pairs={{0,16},{16,32},{32,48},{48,64},{64,80},{80,96},{96,112},{112,128},... | collective-permute-start | bytes 208904 | tf_op jit(solution)/shard_map/ppermute | solution.py:308
  26.0 1.3 %collective-permute-done = bf16[8,4352]{1,0:T(8,128)(2,1)S(1)} collective-permute-done((bf16[8,4352]{1,0:T(8,128)(2,1)S(1)}, bf16[8,4352]{1,0:T(8,128)(2,1)S(1)}, u32[]{:S(2)}, u32[]{:S(2)}) %collective-permute-start) | collective-permute-done | bytes 69664 | tf_op jit(solution)/shard_map/ppermute | solution.py:308
  28.3 2.0 %all-to-all-done.w_ref = bf16[8,32,512]{2,1,0:T(8,128)(2,1)S(1)} async-done(((bf16[8,32,512]{2,1,0:T(8,128)(2,1)}), bf16[8,32,512]{2,1,0:T(8,128)(2,1)S(1)}, u32[]{:S(2)}, u32[]{:S(2)}) %all-to-all-start) | async-done | bytes 262176 | tf_op jit(solution)/shard_map/all_to_all | solution.py:312
  31.0 18.3 %all_to_all.35.in_ref = bf16[8,96,128]{2,1,0:T(8,128)(2,1)S(1)} all-to-all(bf16[8,96,128]{2,1,0:T(8,128)(2,1)S(1)} %spread.1), channel_id=1, replica_groups=mesh['ctx_0'=8,'ctx_1'=4,'ctx_2'=2,'fsdp'=8,'batch'=2] {'ctx_1','ctx_2'}, dimensions={0} | all-to-all | bytes 393216 | tf_op jit(solution)/shard_map/all_to_all | solution.py:312
  49.3 1.0 state.1
  50.3 6.5 %all-to-all-start.2 = ((bf16[8,40,128]{2,1,0:T(8,128)(2,1)}), bf16[8,40,128]{2,1,0:T(8,128)(2,1)S(1)}, u32[]{:S(2)}, u32[]{:S(2)}) async-start(bf16[8,40,128]{2,1,0:T(8,128)(2,1)} %get-tuple-element.27), calls=%async_computation.2 | async-start | bytes 163840 | tf_op jit(solution)/shard_map/all_to_all | solution.py:312
  57.2 6.9 %all-to-all-done.2.sums_ref = bf16[8,40,128]{2,1,0:T(8,128)(2,1)S(1)} async-done(((bf16[8,40,128]{2,1,0:T(8,128)(2,1)}), bf16[8,40,128]{2,1,0:T(8,128)(2,1)S(1)}, u32[]{:S(2)}, u32[]{:S(2)}) %all-to-all-start.2) | async-done | bytes 81952 | tf_op jit(solution)/shard_map/all_to_all | solution.py:312
  64.5 13.6 %all_to_all.36.sums_ref = f32[8,16,128]{2,1,0:T(8,128)S(1)} all-to-all(f32[8,16,128]{2,1,0:T(8,128)S(1)} %get-tuple-element.31), channel_id=1, replica_groups=mesh['ctx_0'=8,'ctx_1'=4,'ctx_2'=2,'fsdp'=8,'batch'=2] {'ctx_1','ctx_2'}, dimensions={0} | all-to-all | bytes 131072 | tf_op jit(solution)/shard_map/all_to_all | solution.py:312
  78.1 1.0 norm.1
  79.1 3.4 %all-to-all-start.4 = ((bf16[8,40,128]{2,1,0:T(8,128)(2,1)}), bf16[8,40,128]{2,1,0:T(8,128)(2,1)S(1)}, u32[]{:S(2)}, u32[]{:S(2)}) async-start(bf16[8,40,128]{2,1,0:T(8,128)(2,1)} %get-tuple-element.33), calls=%async_computation.4 | async-start | bytes 163840 | tf_op jit(solution)/shard_map/all_to_all | solution.py:312
  82.5 1.4 %back.1 = (f32[8,32,128]{2,1,0:T(8,128)S(1)}, f32[8,32,128]{2,1,0:T(8,128)S(1)}) custom-call(bf16[8,96,128]{2,1,0:T(8,128)(2,1)S(1)} %all_to_all.35.in_ref, bf16[8,128,128]{2,1,0:T(8,128)(2,1)S(1)} %get-tuple-element.36.kernel_ref, f32[8,128,128]{2,1,0:T(8,128)S(1)} %get-tuple-element.37.slope_ref, bf16[8,32,128]{2,1,0:T(8,128)(2,1)S(1)} %get-tuple-element.38.dmix_ref, ...), custom_call_target="tpu_custom_call" | custom-call | flops 33554432 | bytes 1392640 | tf_op jit(solution)/shard_map/back/pallas_call | solution.py:36
  83.9 5.9 %all-to-all-done.4.sums_ref = bf16[8,40,128]{2,1,0:T(8,128)(2,1)S(1)} async-done(((bf16[8,40,128]{2,1,0:T(8,128)(2,1)}), bf16[8,40,128]{2,1,0:T(8,128)(2,1)S(1)}, u32[]{:S(2)}, u32[]{:S(2)}) %all-to-all-start.4) | async-done | bytes 81952 | tf_op jit(solution)/shard_map/all_to_all | solution.py:312
  90.2 12.9 %all_to_all.37.sums_ref.in_ref = bf16[8,96,128]{2,1,0:T(8,128)(2,1)S(1)} all-to-all(bf16[8,96,128]{2,1,0:T(8,128)(2,1)S(1)} %later.1), channel_id=1, replica_groups=mesh['ctx_0'=8,'ctx_1'=4,'ctx_2'=2,'fsdp'=8,'batch'=2] {'ctx_1','ctx_2'}, dimensions={0} | all-to-all | bytes 393216 | tf_op jit(solution)/shard_map/all_to_all | solution.py:312
  103.2 1.3 %grad.1 = bf16[128,8,128]{2,1,0:T(8,128)(2,1)} custom-call(bf16[8,96,128]{2,1,0:T(8,128)(2,1)S(1)} %all_to_all.37.sums_ref.in_ref, bf16[128,4096]{1,0:T(8,128)(2,1)S(1)} %bitcast.11, bf16[8,4096]{1,0:T(8,128)(2,1)S(1)} %slice.24.htok_ref, f32[3,32,128]{2,1,0:T(8,128)S(1)} %get-tuple-element.26.cqk_ref), custom_call_target="tpu_custom_call" | custom-call | flops 33554432 | bytes 1622016 | tf_op jit(solution)/shard_map/grad/pallas_call | solution.py:36
  104.5 7.6 %all-to-all-start.6 = ((bf16[128,8,128]{2,1,0:T(8,128)(2,1)}), bf16[128,8,128]{2,1,0:T(8,128)(2,1)S(1)}, u32[]{:S(2)}, u32[]{:S(2)}) async-start(bf16[128,8,128]{2,1,0:T(8,128)(2,1)} %grad.1), calls=%async_computation.6 | async-start | bytes 524288 | tf_op jit(solution)/shard_map/all_to_all | solution.py:312
  112.0 0.8 return.1
  112.8 2.9 %collective-permute-start.1 = (f32[8,256]{1,0:T(8,128)S(1)}, f32[8,256]{1,0:T(8,128)S(1)}, u32[]{:S(2)}, u32[]{:S(2)}) collective-permute-start(f32[8,256]{1,0:T(8,128)S(1)} %get-tuple-element.46), channel_id=1, source_target_pairs={{16,0},{32,16},{48,32},{64,48},{80,64},{96,80},{112,96},{128,112},... | collective-permute-start | bytes 24584 | tf_op jit(solution)/shard_map/ppermute | solution.py:308
  115.7 3.3 %collective-permute-done.1.next_ref = f32[8,256]{1,0:T(8,128)S(1)} collective-permute-done((f32[8,256]{1,0:T(8,128)S(1)}, f32[8,256]{1,0:T(8,128)S(1)}, u32[]{:S(2)}, u32[]{:S(2)}) %collective-permute-start.1) | collective-permute-done | bytes 8224 | tf_op jit(solution)/shard_map/ppermute | solution.py:308
  119.6 7.1 %all-to-all-done.6.a = bf16[128,8,128]{2,1,0:T(8,128)(2,1)S(1)} async-done(((bf16[128,8,128]{2,1,0:T(8,128)(2,1)}), bf16[128,8,128]{2,1,0:T(8,128)(2,1)S(1)}, u32[]{:S(2)}, u32[]{:S(2)}) %all-to-all-start.6) | async-done | bytes 262176 | tf_op jit(solution)/shard_map/all_to_all | solution.py:312
  126.8 0.8 sum.1
  (21 shorter events, 3.4 us)
Async XLA Ops:
  0.6 19.9 %copy-start = (bf16[1,128,4096]{2,1,0:T(8,128)(2,1)S(1)}, bf16[1,128,4096]{2,1,0:T(8,128)(2,1)}, u32[]{:S(2)}) copy-start(bf16[1,128,4096]{2,1,0:T(8,128)(2,1)} %param.6) | copy-start | bytes 3145732
  0.6 1.0 copy-start.1
  2.6 27.7 %all-to-all-start = ((bf16[8,32,512]{2,1,0:T(8,128)(2,1)}), bf16[8,32,512]{2,1,0:T(8,128)(2,1)S(1)}, u32[]{:S(2)}, u32[]{:S(2)}) async-start(bf16[8,32,512]{2,1,0:T(8,128)(2,1)} %turn.1), calls=%async_computation | async-start | bytes 524288 | tf_op jit(solution)/shard_map/all_to_all | solution.py:312
  20.6 6.8 %copy-start.2 = (bf16[1,128,256]{2,1,0:T(8,128)(2,1)S(1)}, bf16[1,128,256]{2,1,0:T(8,128)(2,1)}, u32[]{:S(2)}) copy-start(bf16[1,128,256]{2,1,0:T(8,128)(2,1)} %param.7) | copy-start | bytes 196612
  20.6 6.8 %copy-start.3 = (bf16[1,128,256]{2,1,0:T(8,128)(2,1)S(1)}, bf16[1,128,256]{2,1,0:T(8,128)(2,1)}, u32[]{:S(2)}) copy-start(bf16[1,128,256]{2,1,0:T(8,128)(2,1)} %param.11) | copy-start | bytes 196612
  20.6 6.8 %copy-start.4 = (f32[3,256]{1,0:T(4,128)S(1)}, f32[3,256]{1,0:T(4,128)}, u32[]{:S(2)}) copy-start(f32[3,256]{1,0:T(4,128)} %cv_ref.5) | copy-start | bytes 9220
  20.6 6.8 %collective-permute-start = (bf16[8,4352]{1,0:T(8,128)(2,1)S(1)}, bf16[8,4352]{1,0:T(8,128)(2,1)S(1)}, u32[]{:S(2)}, u32[]{:S(2)}) collective-permute-start(bf16[8,4352]{1,0:T(8,128)(2,1)S(1)} %pad_maximum_fusion), channel_id=1, source_target_pairs={{0,16},{16,32},{32,48},{48,64},{64,80},{80,96},{96,112},{112,128},... | collective-permute-start | bytes 208904 | tf_op jit(solution)/shard_map/ppermute | solution.py:308
  27.4 0.7 copy-start.5
  50.3 13.9 %all-to-all-start.2 = ((bf16[8,40,128]{2,1,0:T(8,128)(2,1)}), bf16[8,40,128]{2,1,0:T(8,128)(2,1)S(1)}, u32[]{:S(2)}, u32[]{:S(2)}) async-start(bf16[8,40,128]{2,1,0:T(8,128)(2,1)} %get-tuple-element.27), calls=%async_computation.2 | async-start | bytes 163840 | tf_op jit(solution)/shard_map/all_to_all | solution.py:312
  79.1 10.7 %all-to-all-start.4 = ((bf16[8,40,128]{2,1,0:T(8,128)(2,1)}), bf16[8,40,128]{2,1,0:T(8,128)(2,1)S(1)}, u32[]{:S(2)}, u32[]{:S(2)}) async-start(bf16[8,40,128]{2,1,0:T(8,128)(2,1)} %get-tuple-element.33), calls=%async_computation.4 | async-start | bytes 163840 | tf_op jit(solution)/shard_map/all_to_all | solution.py:312
  104.5 22.3 %all-to-all-start.6 = ((bf16[128,8,128]{2,1,0:T(8,128)(2,1)}), bf16[128,8,128]{2,1,0:T(8,128)(2,1)S(1)}, u32[]{:S(2)}, u32[]{:S(2)}) async-start(bf16[128,8,128]{2,1,0:T(8,128)(2,1)} %grad.1), calls=%async_computation.6 | async-start | bytes 524288 | tf_op jit(solution)/shard_map/all_to_all | solution.py:312
  112.8 6.2 %collective-permute-start.1 = (f32[8,256]{1,0:T(8,128)S(1)}, f32[8,256]{1,0:T(8,128)S(1)}, u32[]{:S(2)}, u32[]{:S(2)}) collective-permute-start(f32[8,256]{1,0:T(8,128)S(1)} %get-tuple-element.46), channel_id=1, source_target_pairs={{16,0},{32,16},{48,32},{64,48},{80,64},{96,80},{112,96},{128,112},... | collective-permute-start | bytes 24584 | tf_op jit(solution)/shard_map/ppermute | solution.py:308

commit v4 on v3

--- a/solution.py
+++ b/solution.py
@@ -13,6 +13,7 @@
 ROWS = 160
 SLAB = ("ctx_1", "ctx_2")
 CTX = ("ctx_0", "ctx_1", "ctx_2")
+CHIPS = ("ctx_0", "ctx_1", "batch")
 CTX_BATCH = ("ctx_0", "ctx_1", "ctx_2", "batch")
 BF = jnp.bfloat16
 F32 = jnp.float32
@@ -31,7 +32,7 @@
     return lax.dot_general(a, b, (((0,), (0,)), ((), ())), preferred_element_type=F32)
 
 
-def call(body, outs, *args, flops=0, name=None):
+def call(body, outs, *args, flops=0):
     moved = sum(a.size * a.dtype.itemsize for a in (*args, *outs))
     return pl.pallas_call(
         body,
@@ -41,8 +42,7 @@
         ],
         out_specs=[pl.BlockSpec(memory_space=pltpu.VMEM)] * len(outs),
         cost_estimate=pl.CostEstimate(flops=flops, bytes_accessed=moved, transcendentals=0),
-        compiler_params=pltpu.CompilerParams(vmem_limit_bytes=16 << 20),
-        name=name,
+        compiler_params=pltpu.CompilerParams(vmem_limit_bytes=8 << 20),
     )(*args)
 
 
@@ -144,31 +144,31 @@
     return jnp.concatenate([packed[:32], side], axis=1)
 
 
-def state_body(in_ref, before_ref, krows_ref, out_ref):
-    blocks = in_ref.shape[0]
-    total = jnp.zeros((32, ROWS), F32)
-    for b in range(blocks):
-        k_rows = rows_of(in_ref[b, 80:].astype(F32)).astype(BF)
-        krows_ref[b] = k_rows
-        before_ref[b] = total
-        total = total + nt(in_ref[b, :32], k_rows)
-    total = pack(total).astype(BF)
+def state_body(in_ref, krows_ref, out_ref):
+    blocks = range(in_ref.shape[0])
+    for b in blocks:
+        krows_ref[b] = rows_of(in_ref[b, 80:].astype(F32)).astype(BF)
+    values = jnp.concatenate([in_ref[b, :32] for b in blocks], axis=1)
+    total = pack(nt(values, jnp.concatenate([krows_ref[b] for b in blocks], axis=1))).astype(BF)
     for peer in range(out_ref.shape[0]):
         out_ref[peer] = total
 
 
-def local_body(in_ref, mixed_ref, kernel_ref, slope_ref, qrows_ref):
+def scores(in_ref, b):
     row = lax.broadcasted_iota(jnp.int32, (POS, POS), 0)
     col = lax.broadcasted_iota(jnp.int32, (POS, POS), 1)
+    dotted = tn(in_ref[b, 80:], in_ref[b, 64:80]) * 0.25
     causal = row <= col
+    return dotted, causal, jnp.where(causal, 1.0 + dotted + 0.5 * dotted * dotted, 0.0).astype(BF)
+
+
+def local_body(in_ref, krows_ref, before_ref, mixed_ref, qrows_ref):
+    total = jnp.zeros((32, ROWS), F32)
     for b in range(in_ref.shape[0]):
-        queries = in_ref[b, 64:80]
-        dotted = tn(in_ref[b, 80:], queries) * 0.25
-        kernel = jnp.where(causal, 1.0 + dotted + 0.5 * dotted * dotted, 0.0).astype(BF)
-        slope_ref[b] = jnp.where(causal, (1.0 + dotted) * 0.25, 0.0)
-        kernel_ref[b] = kernel
-        mixed_ref[b] = nn(in_ref[b, :32], kernel)
-        qrows_ref[b] = rows_of(queries.astype(F32)).astype(BF)
+        before_ref[b] = total
+        total = total + nt(in_ref[b, :32], krows_ref[b])
+        mixed_ref[b] = nn(in_ref[b, :32], scores(in_ref, b)[2])
+        qrows_ref[b] = rows_of(in_ref[b, 64:80].astype(F32)).astype(BF)
 
 
 def mix_body(at_ref, sums_ref, before_ref, in_ref, local_ref, qrows_ref, mixed_ref, prior_ref, out_ref):
@@ -186,40 +186,43 @@
         mixed_ref[b] = mixed
         squares.append(jnp.sum(mixed * mixed, axis=0, keepdims=True))
         products.append(jnp.sum(in_ref[b, 32:64].astype(F32) * mixed, axis=0, keepdims=True))
-    rows = jnp.concatenate(squares + products, axis=0)
+    rows = jnp.concatenate(squares + products, axis=0).astype(BF)
     for peer in range(out_ref.shape[0]):
         out_ref[peer] = rows
 
 
-def norm_body(sums_ref, in_ref, mixed_ref, qrows_ref, att_ref, dmix_ref, after_ref, out_ref):
-    rows = sums_ref[0]
+def norm_body(sums_ref, in_ref, mixed_ref, qrows_ref, att_ref, dmix_ref, out_ref):
+    rows = sums_ref[0].astype(F32)
     for peer in range(1, sums_ref.shape[0]):
-        rows = rows + sums_ref[peer]
+        rows = rows + sums_ref[peer].astype(F32)
     rows = rows * (1.0 / E)
     blocks = in_ref.shape[0]
-    total = jnp.zeros((32, ROWS), F32)
-    for b in reversed(range(blocks)):
+    for b in range(blocks):
         inv = lax.rsqrt(rows[b : b + 1] + eps_norm)
         normed = mixed_ref[b] * inv
         att_ref[b] = normed.astype(BF)
         grad = in_ref[b, 32:64].astype(F32)
-        d_mixed = (inv * (grad - normed * (inv * rows[blocks + b : blocks + b + 1]))).astype(BF)
-        dmix_ref[b] = d_mixed
-        after_ref[b] = total
-        total = total + nt(d_mixed, qrows_ref[b])
-    total = pack(total).astype(BF)
+        d_mixed = inv * (grad - normed * (inv * rows[blocks + b : blocks + b + 1]))
+        dmix_ref[b] = d_mixed.astype(BF)
+    d_all = jnp.concatenate([dmix_ref[b] for b in range(blocks)], axis=1)
+    total = pack(nt(d_all, jnp.concatenate([qrows_ref[b] for b in range(blocks)], axis=1))).astype(BF)
     for peer in range(out_ref.shape[0]):
         out_ref[peer] = total
 
 
-def back_body(in_ref, kernel_ref, slope_ref, dmix_ref, prior_ref, dqk_ref, dval_ref):
-    for b in range(in_ref.shape[0]):
+def back_body(in_ref, dmix_ref, prior_ref, qrows_ref, after_ref, dqk_ref, dval_ref):
+    total = jnp.zeros((32, ROWS), F32)
+    for b in reversed(range(in_ref.shape[0])):
+        after_ref[b] = total
+        total = total + nt(dmix_ref[b], qrows_ref[b])
         queries, keys = in_ref[b, 64:80], in_ref[b, 80:]
         d_mixed = dmix_ref[b]
-        d_score = (tn(in_ref[b, :32], d_mixed) * slope_ref[b]).astype(BF)
+        dotted, causal, kernel = scores(in_ref, b)
+        slope = jnp.where(causal, (1.0 + dotted) * 0.25, 0.0)
+        d_score = (tn(in_ref[b, :32], d_mixed) * slope).astype(BF)
         dqk_ref[b, :F] = nn(keys, d_score) + rows_back(queries.astype(F32), tn(prior_ref[b], d_mixed))
         dqk_ref[b, F:] = nt(queries, d_score)
-        dval_ref[b] = nt(d_mixed, kernel_ref[b])
+        dval_ref[b] = nt(d_mixed, kernel)
 
 
 def later_body(at_ref, sums_ref, after_ref, in_ref, krows_ref, dqk_ref, dval_ref, att_ref, out_ref):
@@ -231,45 +234,61 @@
     gain = gains()
     for b in range(in_ref.shape[0]):
         later = after_ref[b] + total
-        out_ref[b, :F] = dqk_ref[b, :F].astype(BF)
         keys = in_ref[b, 80:].astype(F32)
         d_key = dqk_ref[b, F:] + rows_back(keys, tn(later.astype(BF), in_ref[b, :32]))
-        out_ref[b, F : 2 * F] = d_key.astype(BF)
-        out_ref[b, 32:64] = att_ref[b]
-        out_ref[b, 64:] = (dval_ref[b] + nn((later * gain).astype(BF), krows_ref[b])).astype(BF)
-
-
-def grad_body(sums_ref, tok_ref, htok_ref, cqk_ref, out_ref):
-    d = sums_ref[0, : 2 * F].astype(F32)
+        part = jnp.concatenate([dqk_ref[b, :F], d_key], axis=0).astype(BF)
+        first, at_row = b - b % 2, 32 * (b % 2)
+        out_ref[first, at_row : at_row + 32] = part
+        out_ref[first + 1, at_row : at_row + 32] = part
+        out_ref[b, 64:96] = att_ref[b]
+        out_ref[b, 96:] = (dval_ref[b] + nn((later * gain).astype(BF), krows_ref[b])).astype(BF)
+
+
+def grad_body(core_ref, sums_ref, tok_ref, other_ref, htok_ref, hother_ref, cqk_ref, out_ref):
+    pair = sums_ref[0, : 4 * F].astype(F32)
     for peer in range(1, sums_ref.shape[0]):
-        d = d + sums_ref[peer, : 2 * F].astype(F32)
-    lane = lax.broadcasted_iota(jnp.int32, d.shape, 1)
-    d1, d2 = cqk_ref[1] * d, cqk_ref[2] * d
-    own = cqk_ref[0] * d
-    own = own + jnp.where(lane < POS - 1, pltpu.roll(d1, POS - 1, 1), 0.0)
-    own = own + jnp.where(lane < POS - 2, pltpu.roll(d2, POS - 2, 1), 0.0)
-    to_last = pltpu.roll(d2, 6, 1)
-    rim = jnp.where(lane == 6, to_last, jnp.where(lane == 7, pltpu.roll(d1, 7, 1) + to_last, 0.0))
-    own_b, rim_b = own.astype(BF), rim[:, :8].astype(BF)
+        pair = pair + sums_ref[peer, : 4 * F].astype(F32)
+    first, second = pair[: 2 * F], pair[2 * F :]
+    core = core_ref[0]
+    lane = lax.broadcasted_iota(jnp.int32, first.shape, 1)
+
+    def ahead(d, nxt, by):
+        return jnp.where(lane < POS - by, pltpu.roll(d, POS - by, 1), pltpu.roll(nxt, POS - by, 1))
+
+    zero = jnp.zeros_like(first)
+    of_first = cqk_ref[0] * first + cqk_ref[1] * ahead(first, second, 1) + cqk_ref[2] * ahead(first, second, 2)
+    of_second = cqk_ref[0] * second + cqk_ref[1] * ahead(second, zero, 1) + cqk_ref[2] * ahead(second, zero, 2)
+    to_last = pltpu.roll(cqk_ref[2] * first, 6, 1)
+    near = pltpu.roll(cqk_ref[1] * first, 7, 1) + to_last
+    rim = jnp.where(lane == 6, to_last, jnp.where(lane == 7, near, 0.0))[:, :8]
+    own_b = jnp.where(core == 0, of_first, of_second).astype(BF)
+    other_b = jnp.where(core == 0, of_second, of_first).astype(BF)
+    rim_own = jnp.where(core == 0, rim, 0.0).astype(BF)
+    rim_other = jnp.where(core == 0, 0.0, rim).astype(BF)
+
     group = lax.broadcasted_iota(jnp.int32, (8, 128), 1) // 32
     chunk = 512
     for start in range(0, tok_ref.shape[1], chunk):
-        part = nn(own_b, tok_ref[:, start : start + chunk]) + nn(rim_b, htok_ref[:, start : start + chunk])
+        at = slice(start, start + chunk)
+        part = nn(own_b, tok_ref[:, at]) + nn(other_b, other_ref[:, at])
+        part = part + nn(rim_own, htok_ref[:, at]) + nn(rim_other, hother_ref[:, at])
         for at_lane in range(0, chunk, 128):
-            blocks = [part[8 * i : 8 * i + 8, at_lane : at_lane + 128] for i in range(4)]
-            for q in range(4):
+            cols = part[:, at_lane : at_lane + 128]
+            cols = jnp.where(core == 0, cols, pltpu.roll(cols, 64, 1))
+            blocks = [cols[8 * i : 8 * i + 8] for i in range(4)]
+            for q in range(2):
                 moved = [pltpu.roll(b, 32 * ((i - q) % 4), 1) if i != q else b for i, b in enumerate(blocks)]
                 packed = jnp.where(
                     group == 0, moved[0], jnp.where(group == 1, moved[1], jnp.where(group == 2, moved[2], moved[3]))
                 )
-                out_ref[(start + at_lane) // 32 + q] = packed.astype(out_ref.dtype)
+                out_ref[(start + at_lane) // 64 + q] = packed.astype(out_ref.dtype)
 
 
 def return_body(in_ref, cv_ref, att_ref, gval_ref, head_ref):
     square = eye(POS)
     peers = range(in_ref.shape[0])
-    att = jnp.concatenate([in_ref[j, 32:64] for j in peers], axis=0)
-    d_rows = jnp.concatenate([in_ref[j, 64:] for j in peers], axis=0)
+    att = jnp.concatenate([in_ref[j, 64:96] for j in peers], axis=0)
+    d_rows = jnp.concatenate([in_ref[j, 96:] for j in peers], axis=0)
     att_ref[...] = nt(square, att).astype(BF)
     dv = nt(square, d_rows)
     head_ref[...] = dv[:8]
@@ -308,6 +327,10 @@
     return lax.ppermute(value, axes, pairs)
 
 
+def swapped(value):
+    return lax.ppermute(value, "ctx_2", [(0, 1), (1, 0)])
+
+
 def exchange(value, axes):
     return lax.all_to_all(value, axes, split_axis=0, concat_axis=0, tiled=True)
 
@@ -320,9 +343,11 @@
     blocks = lax.axis_size(SLAB)
     peers = lax.axis_size(CTX_BATCH)
     deep = w_qk.shape[0]
+    chips = lax.axis_size(CHIPS)
     place = lax.axis_index("ctx_0").astype(jnp.int32).reshape(1)
-
-    (turned,) = call(turn_body, [struct((splits, 2 * F, deep), BF)], w_qk, name="turn")
+    core = lax.axis_index("ctx_2").astype(jnp.int32).reshape(1)
+
+    (turned,) = call(turn_body, [struct((splits, 2 * F, deep), BF)], w_qk)
     weights = exchange(turned, "fsdp")
     rim = to_next(jnp.concatenate([tokens[POS - 8 :], own_values[POS - 8 :]], axis=1), CTX, 1)
     rim_tokens, rim_values = rim[:, :depth], rim[:, depth:]
@@ -331,75 +356,61 @@
         values_body,
         [struct((2, E, POS), BF), struct((CONV, 2 * F, POS), F32)],
         own_values, rim_values, d_attn[0], conv_v, conv_qk,
-        name="values",
-    )
-    (spread,) = call(
-        spread_body, [struct((blocks, 96, POS), BF)], weights, tokens, rim_tokens, value_rows, taps, name="spread"
-    )
+    )
+    (spread,) = call(spread_body, [struct((blocks, 96, POS), BF)], weights, tokens, rim_tokens, value_rows, taps)
     slab = exchange(spread, SLAB)
-    before, k_rows, state = call(
-        state_body,
-        [struct((blocks, 32, ROWS), F32), struct((blocks, ROWS, POS), BF), struct((lines, 40, POS), BF)],
-        slab,
-        name="state",
-    )
+    k_rows, state = call(state_body, [struct((blocks, ROWS, POS), BF), struct((lines, 40, POS), BF)], slab)
     states = exchange(state, "ctx_0")
-    mixed_own, kernel, slope, q_rows = call(
+    before, mixed_own, q_rows = call(
         local_body,
         [
-            struct((blocks, 32, POS), F32), struct((blocks, POS, POS), BF),
-            struct((blocks, POS, POS), F32), struct((blocks, ROWS, POS), BF),
+            struct((blocks, 32, ROWS), F32), struct((blocks, 32, POS), F32), struct((blocks, ROWS, POS), BF),
         ],
-        slab,
-        flops=2 * blocks * POS * POS * 48, name="local",
+        slab, k_rows,
+        flops=2 * blocks * POS * POS * 48,
     )
     mixed, prior, norm = call(
         mix_body,
-        [struct((blocks, 32, POS), F32), struct((blocks, 32, ROWS), BF), struct((blocks, 2 * blocks, POS), F32)],
+        [struct((blocks, 32, POS), F32), struct((blocks, 32, ROWS), BF), struct((blocks, 2 * blocks, POS), BF)],
         place, states, before, slab, mixed_own, q_rows,
-        name="mix",
     )
     norms = exchange(norm, SLAB)
-    att_rows, d_mixed, after, grad_state = call(
+    att_rows, d_mixed, grad_state = call(
         norm_body,
-        [
-            struct((blocks, 32, POS), BF), struct((blocks, 32, POS), BF),
-            struct((blocks, 32, ROWS), F32), struct((lines, 40, POS), BF),
-        ],
+        [struct((blocks, 32, POS), BF), struct((blocks, 32, POS), BF), struct((lines, 40, POS), BF)],
         norms, slab, mixed, q_rows,
-        name="norm",
     )
     grad_states = exchange(grad_state, "ctx_0")
-    d_qk, d_val = call(
+    after, d_qk, d_val = call(
         back_body,
-        [struct((blocks, 32, POS), F32), struct((blocks, 32, POS), F32)],
-        slab, kernel, slope, d_mixed, prior,
-        flops=2 * blocks * POS * POS * 128, name="back",
+        [struct((blocks, 32, ROWS), F32), struct((blocks, 32, POS), F32), struct((blocks, 32, POS), F32)],
+        slab, d_mixed, prior, q_rows,
+        flops=2 * blocks * POS * POS * 144,
     )
     (parts,) = call(
         later_body,
-        [struct((blocks, 96, POS), BF)],
+        [struct((blocks, 128, POS), BF)],
         place, grad_states, after, slab, k_rows, d_qk, d_val, att_rows,
-        name="later",
-    )
+    )
+    sent, sent_rim, parts = lax.optimization_barrier((tokens, rim_tokens, parts))
     home = exchange(parts, SLAB)
+    other_tokens = swapped(sent)
+    other_rim = swapped(sent_rim)
     (grad_parts,) = call(
         grad_body,
-        [struct((peers, 8, 128), BF)],
-        home, tokens, rim_tokens, taps,
-        flops=2 * POS * depth * 2 * F, name="grad",
-    )
-    arrived = exchange(grad_parts, CTX_BATCH)
+        [struct((chips, 8, 128), BF)],
+        core, home, tokens, other_tokens, rim_tokens, other_rim, taps,
+        flops=4 * POS * depth * 2 * F,
+    )
+    arrived = exchange(grad_parts, CHIPS)
     home, _ = lax.optimization_barrier((home, grad_parts))
     attended, g_val, head = call(
-        return_body, [struct((POS, E), BF), struct((POS, E), F32), struct((8, E), F32)], home, conv_v, name="return"
+        return_body, [struct((POS, E), BF), struct((POS, E), F32), struct((8, E), F32)], home, conv_v
     )
     next_rows = to_next(head, CTX, -1)
-    (grad_v,) = call(rim_body, [struct((POS, E), BF)], g_val, next_rows, conv_v, name="rim")
+    (grad_v,) = call(rim_body, [struct((POS, E), BF)], g_val, next_rows, conv_v)
     scale = float(POS * peers) ** (-0.5)
-    (grad_w,) = call(
-        lambda a, b: sum_body(a, b, scale=scale), [struct((2 * F, 2 * F), F32)], arrived, name="sum"
-    )
+    (grad_w,) = call(lambda a, b: sum_body(a, b, scale=scale), [struct((2 * F, 2 * F), F32)], arrived)
     return (attended[None], grad_v[None], grad_w)
 
 

time: 128 us -> 128 us (level); the launches traced: 128 us -> 126 us
  blocking collectives: 44.8 us -> 31.4 us
  starting transfers between devices: 42.9 us -> 51.4 us
  waiting for transfers between devices: 26.6 us -> 28.2 us
  Pallas kernels: 10 us -> 11.5 us
    all_to_all x3 -> x2, blocking collectives: 44.8 us -> 31.4 us  [exchange(): return lax.all_to_all(value, axes, split_axis=0, concat_axis=0, tiled=True)]
    ppermute x0 -> x2, starting transfers between devices: none -> 5.75 us  [swapped(): return lax.ppermute(value, 'ctx_2', [(0, 1), (1, 0)])]
    ppermute x2, starting transfers between devices: 8.31 us -> 10.1 us  [to_next(): return lax.ppermute(value, axes, pairs)]
    pallas_call x13, Pallas kernels: 10 us -> 11.5 us  [call(): pl.pallas_call(body, out_shape=outs, in_specs=[pl.BlockSpec(memory_space=...]
    all_to_all x4 -> x5, starting transfers between devices: 34.6 us -> 35.5 us  [exchange(): return lax.all_to_all(value, axes, split_axis=0, concat_axis=0, tiled=True)]
    all_to_all x4 -> x5, waiting for transfers between devices: 22 us -> 21.9 us  [exchange(): return lax.all_to_all(value, axes, split_axis=0, concat_axis=0, tiled=True)]
  transfers between devices with their start and end apart: 6 -> 9, of which waited for: 6 -> 8; matrix products, arithmetic and copies ran while one was open for 1% -> 1% of each run, Pallas kernels for 3% -> 4%
where the time goes in v4:
time: 128 us; the launch traced here: 126 us
  starting transfers between devices  51.4 us (40%)
  blocking collectives  31.4 us (25%)
  waiting for transfers between devices  28.2 us (22%)
  Pallas kernels  11.5 us (9%)
  local copies, waits for them, and re-layouts  2.42 us (2%)
    all_to_all x5, starting transfers between devices, exchange(): return lax.all_to_all(value, axes, split_axis=0, concat_axis=0, tiled=True)  35.5 us
    all_to_all x2, blocking collectives, exchange(): return lax.all_to_all(value, axes, split_axis=0, concat_axis=0, tiled=True)  31.4 us
    all_to_all x5, waiting for transfers between devices, exchange(): return lax.all_to_all(value, axes, split_axis=0, concat_axis=0, tiled=True)  21.9 us
    pallas_call x13, Pallas kernels, call(): pl.pallas_call(body, out_shape=outs, in_specs=[pl.BlockSpec(memory_space=...  11.5 us
    ppermute x2, starting transfers between devices, to_next(): return lax.ppermute(value, axes, pairs)  10.1 us
    ppermute x2, starting transfers between devices, swapped(): return lax.ppermute(value, 'ctx_2', [(0, 1), (1, 0)])  5.75 us
    ppermute x2, waiting for transfers between devices, to_next(): return lax.ppermute(value, axes, pairs)  5.12 us
  transfers between devices with their start and end apart: 9, of which 8 were waited for; matrix products, arithmetic and copies ran while one was open for 1% of the time, Pallas kernels for 4%

profile of v4, /device:TPU:1, one launch (start us, length us, event | category | flops | bytes accessed | tf_op | source)
XLA Modules:
  0.0 125.8 jit_solution(13020565651815458894)
XLA Ops:
  0.6 1.0 copy-done.1
  2.6 17.2 %all-to-all-start = ((bf16[8,32,512]{2,1,0:T(8,128)(2,1)}), bf16[8,32,512]{2,1,0:T(8,128)(2,1)S(1)}, u32[]{:S(2)}, u32[]{:S(2)}) async-start(bf16[8,32,512]{2,1,0:T(8,128)(2,1)} %shard_map.85), calls=%async_computation | async-start | bytes 524288 | tf_op jit(solution)/shard_map/all_to_all | solution.py:335
  20.6 5.4 %collective-permute-start = (bf16[8,4352]{1,0:T(8,128)(2,1)S(1)}, bf16[8,4352]{1,0:T(8,128)(2,1)S(1)}, u32[]{:S(2)}, u32[]{:S(2)}) collective-permute-start(bf16[8,4352]{1,0:T(8,128)(2,1)S(1)} %pad_maximum_fusion), channel_id=1, source_target_pairs={{0,16},{16,32},{32,48},{48,64},{64,80},{80,96},{96,112},{112,128},... | collective-permute-start | bytes 208904 | tf_op jit(solution)/shard_map/ppermute | solution.py:327
  26.0 1.3 %collective-permute-done = bf16[8,4352]{1,0:T(8,128)(2,1)S(1)} collective-permute-done((bf16[8,4352]{1,0:T(8,128)(2,1)S(1)}, bf16[8,4352]{1,0:T(8,128)(2,1)S(1)}, u32[]{:S(2)}, u32[]{:S(2)}) %collective-permute-start) | collective-permute-done | bytes 69664 | tf_op jit(solution)/shard_map/ppermute | solution.py:327
  28.3 2.0 %all-to-all-done.w_ref = bf16[8,32,512]{2,1,0:T(8,128)(2,1)S(1)} async-done(((bf16[8,32,512]{2,1,0:T(8,128)(2,1)}), bf16[8,32,512]{2,1,0:T(8,128)(2,1)S(1)}, u32[]{:S(2)}, u32[]{:S(2)}) %all-to-all-start) | async-done | bytes 262176 | tf_op jit(solution)/shard_map/all_to_all | solution.py:335
  31.0 18.3 %all_to_all.35.in_ref = bf16[8,96,128]{2,1,0:T(8,128)(2,1)S(1)} all-to-all(bf16[8,96,128]{2,1,0:T(8,128)(2,1)S(1)} %shard_map.87), channel_id=1, replica_groups=mesh['ctx_0'=8,'ctx_1'=4,'ctx_2'=2,'fsdp'=8,'batch'=2] {'ctx_1','ctx_2'}, dimensions={0} | all-to-all | bytes 393216 | tf_op jit(solution)/shard_map/all_to_all | solution.py:335
  50.2 6.5 %all-to-all-start.2 = ((bf16[8,40,128]{2,1,0:T(8,128)(2,1)}), bf16[8,40,128]{2,1,0:T(8,128)(2,1)S(1)}, u32[]{:S(2)}, u32[]{:S(2)}) async-start(bf16[8,40,128]{2,1,0:T(8,128)(2,1)} %get-tuple-element.28), calls=%async_computation.2 | async-start | bytes 163840 | tf_op jit(solution)/shard_map/all_to_all | solution.py:335
  56.7 1.0 shard_map.89
  57.7 6.4 %all-to-all-done.2.sums_ref = bf16[8,40,128]{2,1,0:T(8,128)(2,1)S(1)} async-done(((bf16[8,40,128]{2,1,0:T(8,128)(2,1)}), bf16[8,40,128]{2,1,0:T(8,128)(2,1)S(1)}, u32[]{:S(2)}, u32[]{:S(2)}) %all-to-all-start.2) | async-done | bytes 81952 | tf_op jit(solution)/shard_map/all_to_all | solution.py:335
  64.4 13.1 %all_to_all.36.sums_ref = bf16[8,16,128]{2,1,0:T(8,128)(2,1)S(1)} all-to-all(bf16[8,16,128]{2,1,0:T(8,128)(2,1)S(1)} %get-tuple-element.33), channel_id=1, replica_groups=mesh['ctx_0'=8,'ctx_1'=4,'ctx_2'=2,'fsdp'=8,'batch'=2] {'ctx_1','ctx_2'}, dimensions={0} | all-to-all | bytes 65536 | tf_op jit(solution)/shard_map/all_to_all | solution.py:335
  78.5 3.4 %all-to-all-start.4 = ((bf16[8,40,128]{2,1,0:T(8,128)(2,1)}), bf16[8,40,128]{2,1,0:T(8,128)(2,1)S(1)}, u32[]{:S(2)}, u32[]{:S(2)}) async-start(bf16[8,40,128]{2,1,0:T(8,128)(2,1)} %get-tuple-element.35), calls=%async_computation.4 | async-start | bytes 163840 | tf_op jit(solution)/shard_map/all_to_all | solution.py:335
  81.8 1.7 %shard_map.92 = (f32[8,32,160]{2,1,0:T(8,128)S(1)}, f32[8,32,128]{2,1,0:T(8,128)S(1)}, f32[8,32,128]{2,1,0:T(8,128)S(1)}) custom-call(bf16[8,96,128]{2,1,0:T(8,128)(2,1)S(1)} %all_to_all.35.in_ref, bf16[8,32,128]{2,1,0:T(8,128)(2,1)S(1)} %get-tuple-element.36.dmix_ref, bf16[8,32,160]{2,1,0:T(8,128)(2,1)S(1)} %get-tuple-element.37.prior_ref, ...), custom_call_target="tpu_custom_call" | custom-call | flops 37748736 | bytes 1097728 | tf_op jit(solution)/shard_map/pallas_call | solution.py:37
  83.5 5.6 %all-to-all-done.4.sums_ref = bf16[8,40,128]{2,1,0:T(8,128)(2,1)S(1)} async-done(((bf16[8,40,128]{2,1,0:T(8,128)(2,1)}), bf16[8,40,128]{2,1,0:T(8,128)(2,1)S(1)}, u32[]{:S(2)}, u32[]{:S(2)}) %all-to-all-start.4) | async-done | bytes 81952 | tf_op jit(solution)/shard_map/all_to_all | solution.py:335
  89.2 1.1 shard_map.93
  90.3 3.8 %collective-permute-start.1 = (bf16[128,4096]{1,0:T(8,128)(2,1)S(1)}, bf16[128,4096]{1,0:T(8,128)(2,1)S(1)}, u32[]{:S(2)}, u32[]{:S(2)}) collective-permute-start(bf16[128,4096]{1,0:T(8,128)(2,1)S(1)} %bitcast.12), channel_id=1, source_target_pairs={{0,16},{16,0},{1,17},{17,1},{2,18},{18,2},{3,19},{19,3},{4,20},{20... | collective-permute-start | bytes 3145736 | tf_op jit(solution)/shard_map/ppermute | solution.py:331
  94.1 3.4 %all-to-all-start.5 = ((bf16[8,128,128]{2,1,0:T(8,128)(2,1)}), bf16[8,128,128]{2,1,0:T(8,128)(2,1)S(1)}, u32[]{:S(2)}, u32[]{:S(2)}) async-start(bf16[8,128,128]{2,1,0:T(8,128)(2,1)} %shard_map.93), calls=%async_computation.5 | async-start | bytes 524288 | tf_op jit(solution)/shard_map/all_to_all | solution.py:335
  97.5 2.0 %collective-permute-start.2 = (bf16[8,4096]{1,0:T(8,128)(2,1)S(1)}, bf16[8,4096]{1,0:T(8,128)(2,1)S(1)}, u32[]{:S(2)}, u32[]{:S(2)}) collective-permute-start(bf16[8,4096]{1,0:T(8,128)(2,1)S(1)} %slice.24.htok_ref), channel_id=1, source_target_pairs={{0,16},{16,0},{1,17},{17,1},{2,18},{18,2},{3,19},{19,3},{4,20},{20... | collective-permute-start | bytes 196616 | tf_op jit(solution)/shard_map/ppermute | solution.py:331
  99.4 1.2 collective-permute-done.2.hother_ref
  100.6 6.2 %all-to-all-done.5.sums_ref.in_ref = bf16[8,128,128]{2,1,0:T(8,128)(2,1)S(1)} async-done(((bf16[8,128,128]{2,1,0:T(8,128)(2,1)}), bf16[8,128,128]{2,1,0:T(8,128)(2,1)S(1)}, u32[]{:S(2)}, u32[]{:S(2)}) %all-to-all-start.5) | async-done | bytes 262176 | tf_op jit(solution)/shard_map/all_to_all | solution.py:335
  106.8 1.5 %shard_map.94 = bf16[64,8,128]{2,1,0:T(8,128)(2,1)} custom-call(s32[1]{0:T(128)} %bitcast.6.core_ref, bf16[8,128,128]{2,1,0:T(8,128)(2,1)S(1)} %all-to-all-done.5.sums_ref.in_ref, bf16[128,4096]{1,0:T(8,128)(2,1)S(1)} %bitcast.13, bf16[128,4096]{1,0:T(8,128)(2,1)S(1)} %collective-permute-done.1.other_ref, bf16[8,4096]{1,0:T(8,128)(2,1)S(1)} %slice.24.htok_ref, ...), custom_call_target="tpu_custom_call" | custom-call | flops 67108864 | bytes 2670596 | tf_op jit(solution)/shard_map/pallas_call | solution.py:37
  108.3 5.1 %all-to-all-start.6 = ((bf16[64,8,128]{2,1,0:T(8,128)(2,1)}), bf16[64,8,128]{2,1,0:T(8,128)(2,1)S(1)}, u32[]{:S(2)}, u32[]{:S(2)}) async-start(bf16[64,8,128]{2,1,0:T(8,128)(2,1)} %shard_map.94), calls=%async_computation.6 | async-start | bytes 262144 | tf_op jit(solution)/shard_map/all_to_all | solution.py:335
  114.2 4.7 %collective-permute-start.3 = (f32[8,256]{1,0:T(8,128)S(1)}, f32[8,256]{1,0:T(8,128)S(1)}, u32[]{:S(2)}, u32[]{:S(2)}) collective-permute-start(f32[8,256]{1,0:T(8,128)S(1)} %get-tuple-element.48), channel_id=1, source_target_pairs={{16,0},{32,16},{48,32},{64,48},{80,64},{96,80},{112,96},{128,112},... | collective-permute-start | bytes 24584 | tf_op jit(solution)/shard_map/ppermute | solution.py:327
  118.9 3.8 %collective-permute-done.3.next_ref = f32[8,256]{1,0:T(8,128)S(1)} collective-permute-done((f32[8,256]{1,0:T(8,128)S(1)}, f32[8,256]{1,0:T(8,128)S(1)}, u32[]{:S(2)}, u32[]{:S(2)}) %collective-permute-start.3) | collective-permute-done | bytes 8224 | tf_op jit(solution)/shard_map/ppermute | solution.py:327
  123.3 1.7 %all-to-all-done.6.a = bf16[64,8,128]{2,1,0:T(8,128)(2,1)S(1)} async-done(((bf16[64,8,128]{2,1,0:T(8,128)(2,1)}), bf16[64,8,128]{2,1,0:T(8,128)(2,1)S(1)}, u32[]{:S(2)}, u32[]{:S(2)}) %all-to-all-start.6) | async-done | bytes 131104 | tf_op jit(solution)/shard_map/all_to_all | solution.py:335
  (26 shorter events, 7.6 us)
Async XLA Ops:
  0.6 19.9 %copy-start = (bf16[1,128,4096]{2,1,0:T(8,128)(2,1)S(1)}, bf16[1,128,4096]{2,1,0:T(8,128)(2,1)}, u32[]{:S(2)}) copy-start(bf16[1,128,4096]{2,1,0:T(8,128)(2,1)} %param.6) | copy-start | bytes 3145732
  0.6 1.0 copy-start.1
  2.6 27.7 %all-to-all-start = ((bf16[8,32,512]{2,1,0:T(8,128)(2,1)}), bf16[8,32,512]{2,1,0:T(8,128)(2,1)S(1)}, u32[]{:S(2)}, u32[]{:S(2)}) async-start(bf16[8,32,512]{2,1,0:T(8,128)(2,1)} %shard_map.85), calls=%async_computation | async-start | bytes 524288 | tf_op jit(solution)/shard_map/all_to_all | solution.py:335
  20.6 6.8 %copy-start.2 = (bf16[1,128,256]{2,1,0:T(8,128)(2,1)S(1)}, bf16[1,128,256]{2,1,0:T(8,128)(2,1)}, u32[]{:S(2)}) copy-start(bf16[1,128,256]{2,1,0:T(8,128)(2,1)} %param.7) | copy-start | bytes 196612
  20.6 6.8 %copy-start.3 = (bf16[1,128,256]{2,1,0:T(8,128)(2,1)S(1)}, bf16[1,128,256]{2,1,0:T(8,128)(2,1)}, u32[]{:S(2)}) copy-start(bf16[1,128,256]{2,1,0:T(8,128)(2,1)} %param.11) | copy-start | bytes 196612
  20.6 6.8 %copy-start.4 = (f32[3,256]{1,0:T(4,128)S(1)}, f32[3,256]{1,0:T(4,128)}, u32[]{:S(2)}) copy-start(f32[3,256]{1,0:T(4,128)} %cv_ref.5) | copy-start | bytes 9220
  20.6 6.8 %collective-permute-start = (bf16[8,4352]{1,0:T(8,128)(2,1)S(1)}, bf16[8,4352]{1,0:T(8,128)(2,1)S(1)}, u32[]{:S(2)}, u32[]{:S(2)}) collective-permute-start(bf16[8,4352]{1,0:T(8,128)(2,1)S(1)} %pad_maximum_fusion), channel_id=1, source_target_pairs={{0,16},{16,32},{32,48},{48,64},{64,80},{80,96},{96,112},{112,128},... | collective-permute-start | bytes 208904 | tf_op jit(solution)/shard_map/ppermute | solution.py:327
  27.4 0.7 copy-start.5
  50.2 13.9 %all-to-all-start.2 = ((bf16[8,40,128]{2,1,0:T(8,128)(2,1)}), bf16[8,40,128]{2,1,0:T(8,128)(2,1)S(1)}, u32[]{:S(2)}, u32[]{:S(2)}) async-start(bf16[8,40,128]{2,1,0:T(8,128)(2,1)} %get-tuple-element.28), calls=%async_computation.2 | async-start | bytes 163840 | tf_op jit(solution)/shard_map/all_to_all | solution.py:335
  78.5 10.7 %all-to-all-start.4 = ((bf16[8,40,128]{2,1,0:T(8,128)(2,1)}), bf16[8,40,128]{2,1,0:T(8,128)(2,1)S(1)}, u32[]{:S(2)}, u32[]{:S(2)}) async-start(bf16[8,40,128]{2,1,0:T(8,128)(2,1)} %get-tuple-element.35), calls=%async_computation.4 | async-start | bytes 163840 | tf_op jit(solution)/shard_map/all_to_all | solution.py:335
  90.3 16.5 %collective-permute-start.1 = (bf16[128,4096]{1,0:T(8,128)(2,1)S(1)}, bf16[128,4096]{1,0:T(8,128)(2,1)S(1)}, u32[]{:S(2)}, u32[]{:S(2)}) collective-permute-start(bf16[128,4096]{1,0:T(8,128)(2,1)S(1)} %bitcast.12), channel_id=1, source_target_pairs={{0,16},{16,0},{1,17},{17,1},{2,18},{18,2},{3,19},{19,3},{4,20},{20... | collective-permute-start | bytes 3145736 | tf_op jit(solution)/shard_map/ppermute | solution.py:331
  94.1 12.7 %all-to-all-start.5 = ((bf16[8,128,128]{2,1,0:T(8,128)(2,1)}), bf16[8,128,128]{2,1,0:T(8,128)(2,1)S(1)}, u32[]{:S(2)}, u32[]{:S(2)}) async-start(bf16[8,128,128]{2,1,0:T(8,128)(2,1)} %shard_map.93), calls=%async_computation.5 | async-start | bytes 524288 | tf_op jit(solution)/shard_map/all_to_all | solution.py:335
  97.5 3.1 %collective-permute-start.2 = (bf16[8,4096]{1,0:T(8,128)(2,1)S(1)}, bf16[8,4096]{1,0:T(8,128)(2,1)S(1)}, u32[]{:S(2)}, u32[]{:S(2)}) collective-permute-start(bf16[8,4096]{1,0:T(8,128)(2,1)S(1)} %slice.24.htok_ref), channel_id=1, source_target_pairs={{0,16},{16,0},{1,17},{17,1},{2,18},{18,2},{3,19},{19,3},{4,20},{20... | collective-permute-start | bytes 196616 | tf_op jit(solution)/shard_map/ppermute | solution.py:331
  108.3 16.7 %all-to-all-start.6 = ((bf16[64,8,128]{2,1,0:T(8,128)(2,1)}), bf16[64,8,128]{2,1,0:T(8,128)(2,1)S(1)}, u32[]{:S(2)}, u32[]{:S(2)}) async-start(bf16[64,8,128]{2,1,0:T(8,128)(2,1)} %shard_map.94), calls=%async_computation.6 | async-start | bytes 262144 | tf_op jit(solution)/shard_map/all_to_all | solution.py:335
  114.2 8.5 %collective-permute-start.3 = (f32[8,256]{1,0:T(8,128)S(1)}, f32[8,256]{1,0:T(8,128)S(1)}, u32[]{:S(2)}, u32[]{:S(2)}) collective-permute-start(f32[8,256]{1,0:T(8,128)S(1)} %get-tuple-element.48), channel_id=1, source_target_pairs={{16,0},{32,16},{48,32},{64,48},{80,64},{96,80},{112,96},{128,112},... | collective-permute-start | bytes 24584 | tf_op jit(solution)/shard_map/ppermute | solution.py:327

commit v5 on v4

--- a/solution.py
+++ b/solution.py
@@ -88,19 +88,19 @@
     return total + (1.0 / 16.0) * half
 
 
-def turn_body(w_ref, out_ref):
+def turn_body(w_ref, cqk_ref, out_ref, taps_ref):
     turned = nt(eye(w_ref.shape[1]), w_ref[...]).astype(BF)
     for part in range(out_ref.shape[0]):
         out_ref[part] = turned[32 * part : 32 * part + 32]
-
-
-def values_body(val_ref, hval_ref, grad_ref, cv_ref, cqk_ref, out_ref, taps_ref):
     width = cqk_ref.shape[1]
     row = lax.broadcasted_iota(jnp.int32, (width, width), 0)
     col = lax.broadcasted_iota(jnp.int32, (width, width), 1)
     for tap in range(CONV):
         spread = jnp.where(row == col, jnp.broadcast_to(cqk_ref[tap : tap + 1], (width, width)), 0.0)
         taps_ref[tap] = jnp.broadcast_to(jnp.sum(spread, axis=1, keepdims=True), (width, POS))
+
+
+def values_body(val_ref, hval_ref, grad_ref, cv_ref, out_ref):
     v0 = val_ref[...].astype(F32)
     hv = hval_ref[...].astype(F32)
     at = lax.broadcasted_iota(jnp.int32, v0.shape, 0)
@@ -244,7 +244,21 @@
         out_ref[b, 96:] = (dval_ref[b] + nn((later * gain).astype(BF), krows_ref[b])).astype(BF)
 
 
-def grad_body(core_ref, sums_ref, tok_ref, other_ref, htok_ref, hother_ref, cqk_ref, out_ref):
+def halves_body(core_ref, tok_ref, htok_ref, mine_ref, theirs_ref):
+    for refs, wanted in (((mine_ref, theirs_ref), 0), ((theirs_ref, mine_ref), 1)):
+
+        @pl.when(core_ref[0] == wanted)
+        def _(refs=refs):
+            for in_ref, at in ((tok_ref, slice(0, POS)), (htok_ref, slice(POS, POS + 8))):
+                for m in range(in_ref.shape[1] // 256):
+                    left = in_ref[:, 256 * m : 256 * m + 128]
+                    right = in_ref[:, 256 * m + 128 : 256 * m + 256]
+                    cols = slice(128 * m, 128 * m + 128)
+                    refs[0][at, cols] = jnp.concatenate([left[:, :64], right[:, :64]], axis=1)
+                    refs[1][at, cols] = jnp.concatenate([left[:, 64:], right[:, 64:]], axis=1)
+
+
+def grad_body(core_ref, sums_ref, tok_ref, other_ref, cqk_ref, out_ref):
     pair = sums_ref[0, : 4 * F].astype(F32)
     for peer in range(1, sums_ref.shape[0]):
         pair = pair + sums_ref[peer, : 4 * F].astype(F32)
@@ -270,18 +284,16 @@
     chunk = 512
     for start in range(0, tok_ref.shape[1], chunk):
         at = slice(start, start + chunk)
-        part = nn(own_b, tok_ref[:, at]) + nn(other_b, other_ref[:, at])
-        part = part + nn(rim_own, htok_ref[:, at]) + nn(rim_other, hother_ref[:, at])
+        part = nn(own_b, tok_ref[:POS, at]) + nn(other_b, other_ref[:POS, at])
+        part = part + nn(rim_own, tok_ref[POS:, at]) + nn(rim_other, other_ref[POS:, at])
         for at_lane in range(0, chunk, 128):
-            cols = part[:, at_lane : at_lane + 128]
-            cols = jnp.where(core == 0, cols, pltpu.roll(cols, 64, 1))
-            blocks = [cols[8 * i : 8 * i + 8] for i in range(4)]
-            for q in range(2):
+            blocks = [part[8 * i : 8 * i + 8, at_lane : at_lane + 128] for i in range(4)]
+            for q in range(4):
                 moved = [pltpu.roll(b, 32 * ((i - q) % 4), 1) if i != q else b for i, b in enumerate(blocks)]
                 packed = jnp.where(
                     group == 0, moved[0], jnp.where(group == 1, moved[1], jnp.where(group == 2, moved[2], moved[3]))
                 )
-                out_ref[(start + at_lane) // 64 + q] = packed.astype(out_ref.dtype)
+                out_ref[(start + at_lane) // 32 + q] = packed.astype(out_ref.dtype)
 
 
 def return_body(in_ref, cv_ref, att_ref, gval_ref, head_ref):
@@ -347,18 +359,23 @@
     place = lax.axis_index("ctx_0").astype(jnp.int32).reshape(1)
     core = lax.axis_index("ctx_2").astype(jnp.int32).reshape(1)
 
-    (turned,) = call(turn_body, [struct((splits, 2 * F, deep), BF)], w_qk)
+    turned, taps = call(
+        turn_body,
+        [struct((splits, 2 * F, deep), BF), struct((CONV, 2 * F, POS), F32)],
+        w_qk, conv_qk,
+    )
     weights = exchange(turned, "fsdp")
     rim = to_next(jnp.concatenate([tokens[POS - 8 :], own_values[POS - 8 :]], axis=1), CTX, 1)
     rim_tokens, rim_values = rim[:, :depth], rim[:, depth:]
 
-    value_rows, taps = call(
-        values_body,
-        [struct((2, E, POS), BF), struct((CONV, 2 * F, POS), F32)],
-        own_values, rim_values, d_attn[0], conv_v, conv_qk,
-    )
+    (value_rows,) = call(values_body, [struct((2, E, POS), BF)], own_values, rim_values, d_attn[0], conv_v)
     (spread,) = call(spread_body, [struct((blocks, 96, POS), BF)], weights, tokens, rim_tokens, value_rows, taps)
+    whole, rim_tokens, spread = lax.optimization_barrier((tokens, rim_tokens, spread))
     slab = exchange(spread, SLAB)
+    half = struct((POS + 8, depth // 2), BF)
+    own_half, sent = call(halves_body, [half, half], core, whole, rim_tokens)
+    other_half = swapped(sent)
+    slab, other_half = lax.optimization_barrier((slab, other_half))
     k_rows, state = call(state_body, [struct((blocks, ROWS, POS), BF), struct((lines, 40, POS), BF)], slab)
     states = exchange(state, "ctx_0")
     before, mixed_own, q_rows = call(
@@ -392,15 +409,12 @@
         [struct((blocks, 128, POS), BF)],
         place, grad_states, after, slab, k_rows, d_qk, d_val, att_rows,
     )
-    sent, sent_rim, parts = lax.optimization_barrier((tokens, rim_tokens, parts))
     home = exchange(parts, SLAB)
-    other_tokens = swapped(sent)
-    other_rim = swapped(sent_rim)
     (grad_parts,) = call(
         grad_body,
         [struct((chips, 8, 128), BF)],
-        core, home, tokens, other_tokens, rim_tokens, other_rim, taps,
-        flops=4 * POS * depth * 2 * F,
+        core, home, own_half, other_half, taps,
+        flops=2 * POS * depth * 2 * F,
     )
     arrived = exchange(grad_parts, CHIPS)
     home, _ = lax.optimization_barrier((home, grad_parts))

time: 128 us -> 127 us (level)
  blocking collectives: 31.4 us -> 42.8 us
  waiting for transfers between devices: 28.2 us -> 19.2 us
  starting transfers between devices: 51.4 us -> 46.3 us
  local copies, waits for them, and re-layouts: 2.42 us -> 4.94 us
    all_to_all x2 -> x3, blocking collectives: 31.4 us -> 42.8 us  [exchange(): return lax.all_to_all(value, axes, split_axis=0, concat_axis=0, tiled=True)]
    all_to_all x5 -> x4, waiting for transfers between devices: 21.9 us -> 14.1 us  [exchange(): return lax.all_to_all(value, axes, split_axis=0, concat_axis=0, tiled=True)]
    all_to_all x5 -> x4, starting transfers between devices: 35.5 us -> 32.2 us  [exchange(): return lax.all_to_all(value, axes, split_axis=0, concat_axis=0, tiled=True)]
    unnamed x12, local copies, waits for them, and re-layouts: 1.72 us -> 3.4 us
    ppermute x2 -> x1, starting transfers between devices: 5.75 us -> 4.23 us  [swapped(): return lax.ppermute(value, 'ctx_2', [(0, 1), (1, 0)])]
    pallas_call x13 -> x14, Pallas kernels: 11.5 us -> 10.9 us  [call(): pl.pallas_call(body, out_shape=outs, in_specs=[pl.BlockSpec(memory_space=...]
  transfers between devices with their start and end apart: 9 -> 7, of which waited for: 8 -> 6; matrix products, arithmetic and copies ran while one was open for 1% -> 1% of each run, Pallas kernels for 4% -> 4%
where the time goes in v5:
time: 127 us; the launch traced here: 125 us
  starting transfers between devices  46.3 us (36%)
  blocking collectives  42.8 us (34%)
  waiting for transfers between devices  19.2 us (15%)
  Pallas kernels  10.9 us (9%)
  local copies, waits for them, and re-layouts  4.94 us (4%)
    all_to_all x3, blocking collectives, exchange(): return lax.all_to_all(value, axes, split_axis=0, concat_axis=0, tiled=True)  42.8 us
    all_to_all x4, starting transfers between devices, exchange(): return lax.all_to_all(value, axes, split_axis=0, concat_axis=0, tiled=True)  32.2 us
    all_to_all x4, waiting for transfers between devices, exchange(): return lax.all_to_all(value, axes, split_axis=0, concat_axis=0, tiled=True)  14.1 us
    pallas_call x14, Pallas kernels, call(): pl.pallas_call(body, out_shape=outs, in_specs=[pl.BlockSpec(memory_space=...  10.9 us
    ppermute x2, starting transfers between devices, to_next(): return lax.ppermute(value, axes, pairs)  9.92 us
    ppermute x2, waiting for transfers between devices, to_next(): return lax.ppermute(value, axes, pairs)  5.08 us
    ppermute x1, starting transfers between devices, swapped(): return lax.ppermute(value, 'ctx_2', [(0, 1), (1, 0)])  4.23 us
    unnamed x12, local copies, waits for them, and re-layouts  3.4 us
  transfers between devices with their start and end apart: 7, of which 6 were waited for; matrix products, arithmetic and copies ran while one was open for 1% of the time, Pallas kernels for 4%

profile of v5, /device:TPU:1, one launch (start us, length us, event | category | flops | bytes accessed | tf_op | source)
XLA Modules:
  0.0 125.0 jit_solution(7788287622467396114)
XLA Ops:
  0.7 1.0 copy-done.1
  2.4 1.0 shard_map.85
  3.3 17.2 %all-to-all-start = ((bf16[8,32,512]{2,1,0:T(8,128)(2,1)}), bf16[8,32,512]{2,1,0:T(8,128)(2,1)S(1)}, u32[]{:S(2)}, u32[]{:S(2)}) async-start(bf16[8,32,512]{2,1,0:T(8,128)(2,1)} %get-tuple-element.30), calls=%async_computation | async-start | bytes 524288 | tf_op jit(solution)/shard_map/all_to_all | solution.py:347
  21.2 0.8 slice_bitcast_fusion
  22.1 5.3 %collective-permute-start = (bf16[8,4352]{1,0:T(8,128)(2,1)S(1)}, bf16[8,4352]{1,0:T(8,128)(2,1)S(1)}, u32[]{:S(2)}, u32[]{:S(2)}) collective-permute-start(bf16[8,4352]{1,0:T(8,128)(2,1)S(1)} %pad_maximum_fusion), channel_id=1, source_target_pairs={{0,16},{16,32},{32,48},{48,64},{64,80},{80,96},{96,112},{112,128},... | collective-permute-start | bytes 208904 | tf_op jit(solution)/shard_map/ppermute | solution.py:339
  27.4 1.3 %collective-permute-done = bf16[8,4352]{1,0:T(8,128)(2,1)S(1)} collective-permute-done((bf16[8,4352]{1,0:T(8,128)(2,1)S(1)}, bf16[8,4352]{1,0:T(8,128)(2,1)S(1)}, u32[]{:S(2)}, u32[]{:S(2)}) %collective-permute-start) | collective-permute-done | bytes 69664 | tf_op jit(solution)/shard_map/ppermute | solution.py:339
  28.8 0.8 copy-done.2
  32.1 4.2 %collective-permute-start.1 = (bf16[136,2048]{1,0:T(8,128)(2,1)S(1)}, bf16[136,2048]{1,0:T(8,128)(2,1)S(1)}, u32[]{:S(2)}, u32[]{:S(2)}) collective-permute-start(bf16[136,2048]{1,0:T(8,128)(2,1)S(1)} %get-tuple-element.35), channel_id=1, source_target_pairs={{0,16},{16,0},{1,17},{17,1},{2,18},{18,2},{3,19},{19,3},{4,20},{20... | collective-permute-start | bytes 1671176 | tf_op jit(solution)/shard_map/ppermute | solution.py:343
  36.3 16.1 %all_to_all.35.in_ref = bf16[8,96,128]{2,1,0:T(8,128)(2,1)S(1)} all-to-all(bf16[8,96,128]{2,1,0:T(8,128)(2,1)S(1)} %shard_map.87), channel_id=1, replica_groups=mesh['ctx_0'=8,'ctx_1'=4,'ctx_2'=2,'fsdp'=8,'batch'=2] {'ctx_1','ctx_2'}, dimensions={0} | all-to-all | bytes 393216 | tf_op jit(solution)/shard_map/all_to_all | solution.py:347
  52.4 0.9 shard_map.89
  53.4 6.5 %all-to-all-start.2 = ((bf16[8,40,128]{2,1,0:T(8,128)(2,1)}), bf16[8,40,128]{2,1,0:T(8,128)(2,1)S(1)}, u32[]{:S(2)}, u32[]{:S(2)}) async-start(bf16[8,40,128]{2,1,0:T(8,128)(2,1)} %get-tuple-element.37), calls=%async_computation.2 | async-start | bytes 163840 | tf_op jit(solution)/shard_map/all_to_all | solution.py:347
  59.8 1.0 shard_map.90
  60.8 6.4 %all-to-all-done.2.sums_ref = bf16[8,40,128]{2,1,0:T(8,128)(2,1)S(1)} async-done(((bf16[8,40,128]{2,1,0:T(8,128)(2,1)}), bf16[8,40,128]{2,1,0:T(8,128)(2,1)S(1)}, u32[]{:S(2)}, u32[]{:S(2)}) %all-to-all-start.2) | async-done | bytes 81952 | tf_op jit(solution)/shard_map/all_to_all | solution.py:347
  67.6 13.1 %all_to_all.36.sums_ref = bf16[8,16,128]{2,1,0:T(8,128)(2,1)S(1)} all-to-all(bf16[8,16,128]{2,1,0:T(8,128)(2,1)S(1)} %get-tuple-element.42), channel_id=1, replica_groups=mesh['ctx_0'=8,'ctx_1'=4,'ctx_2'=2,'fsdp'=8,'batch'=2] {'ctx_1','ctx_2'}, dimensions={0} | all-to-all | bytes 65536 | tf_op jit(solution)/shard_map/all_to_all | solution.py:347
  80.7 0.9 shard_map.92
  81.6 3.4 %all-to-all-start.4 = ((bf16[8,40,128]{2,1,0:T(8,128)(2,1)}), bf16[8,40,128]{2,1,0:T(8,128)(2,1)S(1)}, u32[]{:S(2)}, u32[]{:S(2)}) async-start(bf16[8,40,128]{2,1,0:T(8,128)(2,1)} %get-tuple-element.44), calls=%async_computation.4 | async-start | bytes 163840 | tf_op jit(solution)/shard_map/all_to_all | solution.py:347
  85.0 1.7 %shard_map.93 = (f32[8,32,160]{2,1,0:T(8,128)S(1)}, f32[8,32,128]{2,1,0:T(8,128)S(1)}, f32[8,32,128]{2,1,0:T(8,128)S(1)}) custom-call(bf16[8,96,128]{2,1,0:T(8,128)(2,1)S(1)} %all_to_all.35.in_ref, bf16[8,32,128]{2,1,0:T(8,128)(2,1)S(1)} %get-tuple-element.45.dmix_ref, bf16[8,32,160]{2,1,0:T(8,128)(2,1)S(1)} %get-tuple-element.46.prior_ref, ...), custom_call_target="tpu_custom_call" | custom-call | flops 37748736 | bytes 1097728 | tf_op jit(solution)/shard_map/pallas_call | solution.py:37
  86.7 5.6 %all-to-all-done.4.sums_ref = bf16[8,40,128]{2,1,0:T(8,128)(2,1)S(1)} async-done(((bf16[8,40,128]{2,1,0:T(8,128)(2,1)}), bf16[8,40,128]{2,1,0:T(8,128)(2,1)S(1)}, u32[]{:S(2)}, u32[]{:S(2)}) %all-to-all-start.4) | async-done | bytes 81952 | tf_op jit(solution)/shard_map/all_to_all | solution.py:347
  92.7 13.6 %all_to_all.37.sums_ref.in_ref = bf16[8,128,128]{2,1,0:T(8,128)(2,1)S(1)} all-to-all(bf16[8,128,128]{2,1,0:T(8,128)(2,1)S(1)} %shard_map.94), channel_id=1, replica_groups=mesh['ctx_0'=8,'ctx_1'=4,'ctx_2'=2,'fsdp'=8,'batch'=2] {'ctx_1','ctx_2'}, dimensions={0} | all-to-all | bytes 524288 | tf_op jit(solution)/shard_map/all_to_all | solution.py:347
  106.3 1.2 shard_map.95
  107.5 5.1 %all-to-all-start.6 = ((bf16[64,8,128]{2,1,0:T(8,128)(2,1)}), bf16[64,8,128]{2,1,0:T(8,128)(2,1)S(1)}, u32[]{:S(2)}, u32[]{:S(2)}) async-start(bf16[64,8,128]{2,1,0:T(8,128)(2,1)} %shard_map.95), calls=%async_computation.6 | async-start | bytes 262144 | tf_op jit(solution)/shard_map/all_to_all | solution.py:347
  113.5 4.6 %collective-permute-start.2 = (f32[8,256]{1,0:T(8,128)S(1)}, f32[8,256]{1,0:T(8,128)S(1)}, u32[]{:S(2)}, u32[]{:S(2)}) collective-permute-start(f32[8,256]{1,0:T(8,128)S(1)} %get-tuple-element.56), channel_id=1, source_target_pairs={{16,0},{32,16},{48,32},{64,48},{80,64},{96,80},{112,96},{128,112},... | collective-permute-start | bytes 24584 | tf_op jit(solution)/shard_map/ppermute | solution.py:339
  118.1 3.7 %collective-permute-done.2.next_ref = f32[8,256]{1,0:T(8,128)S(1)} collective-permute-done((f32[8,256]{1,0:T(8,128)S(1)}, f32[8,256]{1,0:T(8,128)S(1)}, u32[]{:S(2)}, u32[]{:S(2)}) %collective-permute-start.2) | collective-permute-done | bytes 8224 | tf_op jit(solution)/shard_map/ppermute | solution.py:339
  122.5 1.7 %all-to-all-done.6.a = bf16[64,8,128]{2,1,0:T(8,128)(2,1)S(1)} async-done(((bf16[64,8,128]{2,1,0:T(8,128)(2,1)}), bf16[64,8,128]{2,1,0:T(8,128)(2,1)S(1)}, u32[]{:S(2)}, u32[]{:S(2)}) %all-to-all-start.6) | async-done | bytes 131104 | tf_op jit(solution)/shard_map/all_to_all | solution.py:347
  (24 shorter events, 6.8 us)
Async XLA Ops:
  0.6 30.4 %copy-start = (bf16[1,128,4096]{2,1,0:T(8,128)(2,1)S(1)}, bf16[1,128,4096]{2,1,0:T(8,128)(2,1)}, u32[]{:S(2)}) copy-start(bf16[1,128,4096]{2,1,0:T(8,128)(2,1)} %param.6) | copy-start | bytes 3145732
  0.6 1.0 copy-start.1
  1.7 0.7 copy-start.5
  3.3 27.7 %all-to-all-start = ((bf16[8,32,512]{2,1,0:T(8,128)(2,1)}), bf16[8,32,512]{2,1,0:T(8,128)(2,1)S(1)}, u32[]{:S(2)}, u32[]{:S(2)}) async-start(bf16[8,32,512]{2,1,0:T(8,128)(2,1)} %get-tuple-element.30), calls=%async_computation | async-start | bytes 524288 | tf_op jit(solution)/shard_map/all_to_all | solution.py:347
  22.1 6.6 %collective-permute-start = (bf16[8,4352]{1,0:T(8,128)(2,1)S(1)}, bf16[8,4352]{1,0:T(8,128)(2,1)S(1)}, u32[]{:S(2)}, u32[]{:S(2)}) collective-permute-start(bf16[8,4352]{1,0:T(8,128)(2,1)S(1)} %pad_maximum_fusion), channel_id=1, source_target_pairs={{0,16},{16,32},{32,48},{48,64},{64,80},{80,96},{96,112},{112,128},... | collective-permute-start | bytes 208904 | tf_op jit(solution)/shard_map/ppermute | solution.py:339
  27.4 1.3 %copy-start.4 = (f32[3,256]{1,0:T(4,128)S(1)}, f32[3,256]{1,0:T(4,128)}, u32[]{:S(2)}) copy-start(f32[3,256]{1,0:T(4,128)} %cv_ref.5) | copy-start | bytes 9220
  28.7 0.8 copy-start.2
  29.6 0.8 copy-start.3
  32.1 20.3 %collective-permute-start.1 = (bf16[136,2048]{1,0:T(8,128)(2,1)S(1)}, bf16[136,2048]{1,0:T(8,128)(2,1)S(1)}, u32[]{:S(2)}, u32[]{:S(2)}) collective-permute-start(bf16[136,2048]{1,0:T(8,128)(2,1)S(1)} %get-tuple-element.35), channel_id=1, source_target_pairs={{0,16},{16,0},{1,17},{17,1},{2,18},{18,2},{3,19},{19,3},{4,20},{20... | collective-permute-start | bytes 1671176 | tf_op jit(solution)/shard_map/ppermute | solution.py:343
  53.4 13.9 %all-to-all-start.2 = ((bf16[8,40,128]{2,1,0:T(8,128)(2,1)}), bf16[8,40,128]{2,1,0:T(8,128)(2,1)S(1)}, u32[]{:S(2)}, u32[]{:S(2)}) async-start(bf16[8,40,128]{2,1,0:T(8,128)(2,1)} %get-tuple-element.37), calls=%async_computation.2 | async-start | bytes 163840 | tf_op jit(solution)/shard_map/all_to_all | solution.py:347
  81.6 10.7 %all-to-all-start.4 = ((bf16[8,40,128]{2,1,0:T(8,128)(2,1)}), bf16[8,40,128]{2,1,0:T(8,128)(2,1)S(1)}, u32[]{:S(2)}, u32[]{:S(2)}) async-start(bf16[8,40,128]{2,1,0:T(8,128)(2,1)} %get-tuple-element.44), calls=%async_computation.4 | async-start | bytes 163840 | tf_op jit(solution)/shard_map/all_to_all | solution.py:347
  107.5 16.7 %all-to-all-start.6 = ((bf16[64,8,128]{2,1,0:T(8,128)(2,1)}), bf16[64,8,128]{2,1,0:T(8,128)(2,1)S(1)}, u32[]{:S(2)}, u32[]{:S(2)}) async-start(bf16[64,8,128]{2,1,0:T(8,128)(2,1)} %shard_map.95), calls=%async_computation.6 | async-start | bytes 262144 | tf_op jit(solution)/shard_map/all_to_all | solution.py:347
  113.5 8.4 %collective-permute-start.2 = (f32[8,256]{1,0:T(8,128)S(1)}, f32[8,256]{1,0:T(8,128)S(1)}, u32[]{:S(2)}, u32[]{:S(2)}) collective-permute-start(f32[8,256]{1,0:T(8,128)S(1)} %get-tuple-element.56), channel_id=1, source_target_pairs={{16,0},{32,16},{48,32},{64,48},{80,64},{96,80},{112,96},{128,112},... | collective-permute-start | bytes 24584 | tf_op jit(solution)/shard_map/ppermute | solution.py:339

commit v6 on v5

--- a/solution.py
+++ b/solution.py
@@ -88,26 +88,49 @@
     return total + (1.0 / 16.0) * half
 
 
-def turn_body(w_ref, cqk_ref, out_ref, taps_ref):
-    turned = nt(eye(w_ref.shape[1]), w_ref[...]).astype(BF)
+def turn_body(w_hbm, cqk_hbm, tok_hbm, val_hbm, grad_hbm, cv_hbm, out_ref, rim_ref, val_ref, grad_ref, w_buf, cqk_buf, val_buf, sems):
+    depth = tok_hbm.shape[1]
+    pairs = (
+        (w_hbm, w_buf),
+        (cqk_hbm, cqk_buf),
+        (tok_hbm.at[POS - 8 :], rim_ref.at[:, :depth]),
+        (val_hbm.at[POS - 8 :], rim_ref.at[:, depth:]),
+        (val_hbm, val_buf),
+        (grad_hbm, grad_ref),
+        (cv_hbm, val_ref.at[POS : POS + CONV]),
+    )
+    copies = [pltpu.make_async_copy(source, target, sems.at[k]) for k, (source, target) in enumerate(pairs)]
+    for copy in copies:
+        copy.start()
+    copies[0].wait()
+    turned = nt(eye(w_buf.shape[1]), w_buf[...]).astype(BF)
     for part in range(out_ref.shape[0]):
         out_ref[part] = turned[32 * part : 32 * part + 32]
-    width = cqk_ref.shape[1]
+    copies[1].wait()
+    width = cqk_buf.shape[1]
     row = lax.broadcasted_iota(jnp.int32, (width, width), 0)
     col = lax.broadcasted_iota(jnp.int32, (width, width), 1)
     for tap in range(CONV):
-        spread = jnp.where(row == col, jnp.broadcast_to(cqk_ref[tap : tap + 1], (width, width)), 0.0)
-        taps_ref[tap] = jnp.broadcast_to(jnp.sum(spread, axis=1, keepdims=True), (width, POS))
-
-
-def values_body(val_ref, hval_ref, grad_ref, cv_ref, out_ref):
-    v0 = val_ref[...].astype(F32)
+        spread = jnp.where(row == col, jnp.broadcast_to(cqk_buf[tap : tap + 1], (width, width)), 0.0)
+        at = POS + 8 + width * tap
+        val_ref[at : at + width, :POS] = jnp.broadcast_to(jnp.sum(spread, axis=1, keepdims=True), (width, POS))
+    for copy in copies[2:]:
+        copy.wait()
+    val_ref[:POS] = val_buf[...].astype(F32)
+
+
+def values_body(val_ref, hval_ref, grad_ref, out_ref, taps_ref):
+    for tap in range(CONV):
+        at = POS + 8 + 2 * F * tap
+        taps_ref[tap] = val_ref[at : at + 2 * F, :POS]
+    v0 = val_ref[:POS]
+    first, second, third = (val_ref[POS + k : POS + k + 1] for k in range(CONV))
     hv = hval_ref[...].astype(F32)
     at = lax.broadcasted_iota(jnp.int32, v0.shape, 0)
     last, before = (jnp.broadcast_to(hv[k : k + 1], v0.shape) for k in (7, 6))
     v1 = jnp.where(at == 0, last, pltpu.roll(v0, 1, 0))
     v2 = jnp.where(at == 0, before, jnp.where(at == 1, last, pltpu.roll(v0, 2, 0)))
-    valued = (cv_ref[0:1] * v0 + cv_ref[1:2] * v1 + cv_ref[2:3] * v2).astype(BF)
+    valued = (first * v0 + second * v1 + third * v2).astype(BF)
     square = eye(E)
     out_ref[0] = nt(square, valued).astype(BF)
     out_ref[1] = nt(square, grad_ref[...]).astype(BF)
@@ -359,16 +382,31 @@
     place = lax.axis_index("ctx_0").astype(jnp.int32).reshape(1)
     core = lax.axis_index("ctx_2").astype(jnp.int32).reshape(1)
 
-    turned, taps = call(
+    sources = (w_qk, conv_qk, tokens, own_values, d_attn[0], conv_v)
+    fetched = [
+        struct((splits, 2 * F, deep), BF), struct((8, depth + E), BF),
+        struct((POS + 8 + CONV * 2 * F, E), F32), struct((POS, E), BF),
+    ]
+    turned, rim, own_values, own_grad = pl.pallas_call(
         turn_body,
-        [struct((splits, 2 * F, deep), BF), struct((CONV, 2 * F, POS), F32)],
-        w_qk, conv_qk,
-    )
+        out_shape=fetched,
+        in_specs=[pl.BlockSpec(memory_space=pltpu.HBM)] * len(sources),
+        out_specs=[pl.BlockSpec(memory_space=pltpu.VMEM)] * len(fetched),
+        scratch_shapes=[
+            pltpu.VMEM(w_qk.shape, BF), pltpu.VMEM(conv_qk.shape, F32), pltpu.VMEM((POS, E), BF), pltpu.SemaphoreType.DMA((7,))
+        ],
+        compiler_params=pltpu.CompilerParams(vmem_limit_bytes=60 * 1024 * 1024),
+        name="turn",
+    )(*sources)
     weights = exchange(turned, "fsdp")
-    rim = to_next(jnp.concatenate([tokens[POS - 8 :], own_values[POS - 8 :]], axis=1), CTX, 1)
+    rim = to_next(rim, CTX, 1)
     rim_tokens, rim_values = rim[:, :depth], rim[:, depth:]
 
-    (value_rows,) = call(values_body, [struct((2, E, POS), BF)], own_values, rim_values, d_attn[0], conv_v)
+    value_rows, taps = call(
+        values_body,
+        [struct((2, E, POS), BF), struct((CONV, 2 * F, POS), F32)],
+        own_values, rim_values, own_grad,
+    )
     (spread,) = call(spread_body, [struct((blocks, 96, POS), BF)], weights, tokens, rim_tokens, value_rows, taps)
     whole, rim_tokens, spread = lax.optimization_barrier((tokens, rim_tokens, spread))
     slab = exchange(spread, SLAB)

time: 127 us -> 127 us (level)
  local copies, waits for them, and re-layouts: 4.94 us -> 0.03 us
  waiting for transfers between devices: 19.2 us -> 22.5 us
  Pallas kernels: 10.9 us -> 12.2 us
    unnamed x12 -> x10, local copies, waits for them, and re-layouts: 3.4 us -> 0.02 us
    all_to_all x4, waiting for transfers between devices: 14.1 us -> 17.4 us  [exchange(): return lax.all_to_all(value, axes, split_axis=0, concat_axis=0, tiled=True)]
    pallas_call x0 -> x1, Pallas kernels: none -> 2.28 us  [shards(): pl.pallas_call(turn_body, out_shape=fetched, in_specs=[pl.BlockSpec(memor...]
    slice x2 -> x0, local copies, waits for them, and re-layouts: 1.53 us -> none  [the longest x1 0.84 us: shards(): tokens[POS - 8:]]
    pallas_call x14 -> x13, Pallas kernels: 10.9 us -> 9.92 us  [call(): pl.pallas_call(body, out_shape=outs, in_specs=[pl.BlockSpec(memory_space=...]
  transfers between devices with their start and end apart: 7 -> 7, of which waited for: 6 -> 6; matrix products, arithmetic and copies ran while one was open for 1% -> 0% of each run, Pallas kernels for 4% -> 4%
where the time goes in v6:
time: 127 us; the launch traced here: 125 us
  starting transfers between devices  46.6 us (37%)
  blocking collectives  42.8 us (34%)
  waiting for transfers between devices  22.5 us (18%)
  Pallas kernels  12.2 us (10%)
    all_to_all x3, blocking collectives, exchange(): return lax.all_to_all(value, axes, split_axis=0, concat_axis=0, tiled=True)  42.8 us
    all_to_all x4, starting transfers between devices, exchange(): return lax.all_to_all(value, axes, split_axis=0, concat_axis=0, tiled=True)  32.5 us
    all_to_all x4, waiting for transfers between devices, exchange(): return lax.all_to_all(value, axes, split_axis=0, concat_axis=0, tiled=True)  17.4 us
    pallas_call x13, Pallas kernels, call(): pl.pallas_call(body, out_shape=outs, in_specs=[pl.BlockSpec(memory_space=...  9.92 us
    ppermute x2, starting transfers between devices, to_next(): return lax.ppermute(value, axes, pairs)  9.85 us
    ppermute x2, waiting for transfers between devices, to_next(): return lax.ppermute(value, axes, pairs)  5.03 us
    ppermute x1, starting transfers between devices, swapped(): return lax.ppermute(value, 'ctx_2', [(0, 1), (1, 0)])  4.27 us
  transfers between devices with their start and end apart: 7, of which 6 were waited for; matrix products, arithmetic and copies ran while one was open for 0% of the time, Pallas kernels for 4%

profile of v6, /device:TPU:1, one launch (start us, length us, event | category | flops | bytes accessed | tf_op | source)
XLA Modules:
  0.0 124.9 jit_solution(14352139471498731033)
XLA Ops:
  0.6 2.3 %turn.1 = (bf16[8,32,512]{2,1,0:T(8,128)(2,1)}, bf16[8,4352]{1,0:T(8,128)(2,1)}, f32[232,256]{1,0:T(8,128)}, bf16[128,256]{1,0:T(8,128)(2,1)}) custom-call(bf16[512,256]{1,0:T(8,128)(2,1)} %w_hbm.1, f32[3,32]{1,0:T(4,128)} %cqk_hbm.1, bf16[128,4096]{1,0:T(8,128)(2,1)} %bitcast.7, bf16[128,256]{1,0:T(8,128)(2,1)} %bitcast.10, bf16[128,256]{1,0:T(8,128)(2,1)} %bitcast.11, ...), custom_call_target="tpu_custom_call" | custom-call | tf_op jit(solution)/shard_map/turn/pallas_call | solution.py:390
  3.0 17.4 %all-to-all-start = ((bf16[8,32,512]{2,1,0:T(8,128)(2,1)}), bf16[8,32,512]{2,1,0:T(8,128)(2,1)S(1)}, u32[]{:S(2)}, u32[]{:S(2)}) async-start(bf16[8,32,512]{2,1,0:T(8,128)(2,1)} %get-tuple-element.35), calls=%async_computation | async-start | bytes 524288 | tf_op jit(solution)/shard_map/all_to_all | solution.py:370
  20.3 5.3 %collective-permute-start = (bf16[8,4352]{1,0:T(8,128)(2,1)S(1)}, bf16[8,4352]{1,0:T(8,128)(2,1)S(1)}, u32[]{:S(2)}, u32[]{:S(2)}) collective-permute-start(bf16[8,4352]{1,0:T(8,128)(2,1)S(1)} %copy-done.4), channel_id=1, source_target_pairs={{0,16},{16,32},{32,48},{48,64},{64,80},{80,96},{96,112},{112,128},... | collective-permute-start | bytes 208904 | tf_op jit(solution)/shard_map/ppermute | solution.py:362
  25.6 1.3 %collective-permute-done = bf16[8,4352]{1,0:T(8,128)(2,1)S(1)} collective-permute-done((bf16[8,4352]{1,0:T(8,128)(2,1)S(1)}, bf16[8,4352]{1,0:T(8,128)(2,1)S(1)}, u32[]{:S(2)}, u32[]{:S(2)}) %collective-permute-start) | collective-permute-done | bytes 69664 | tf_op jit(solution)/shard_map/ppermute | solution.py:362
  27.2 3.6 %all-to-all-done.w_ref = bf16[8,32,512]{2,1,0:T(8,128)(2,1)S(1)} async-done(((bf16[8,32,512]{2,1,0:T(8,128)(2,1)}), bf16[8,32,512]{2,1,0:T(8,128)(2,1)S(1)}, u32[]{:S(2)}, u32[]{:S(2)}) %all-to-all-start) | async-done | bytes 262176 | tf_op jit(solution)/shard_map/all_to_all | solution.py:370
  31.8 4.3 %collective-permute-start.1 = (bf16[136,2048]{1,0:T(8,128)(2,1)S(1)}, bf16[136,2048]{1,0:T(8,128)(2,1)S(1)}, u32[]{:S(2)}, u32[]{:S(2)}) collective-permute-start(bf16[136,2048]{1,0:T(8,128)(2,1)S(1)} %get-tuple-element.43), channel_id=1, source_target_pairs={{0,16},{16,0},{1,17},{17,1},{2,18},{18,2},{3,19},{19,3},{4,20},{20... | collective-permute-start | bytes 1671176 | tf_op jit(solution)/shard_map/ppermute | solution.py:366
  36.1 16.1 %all_to_all.35.in_ref = bf16[8,96,128]{2,1,0:T(8,128)(2,1)S(1)} all-to-all(bf16[8,96,128]{2,1,0:T(8,128)(2,1)S(1)} %shard_map.86), channel_id=1, replica_groups=mesh['ctx_0'=8,'ctx_1'=4,'ctx_2'=2,'fsdp'=8,'batch'=2] {'ctx_1','ctx_2'}, dimensions={0} | all-to-all | bytes 393216 | tf_op jit(solution)/shard_map/all_to_all | solution.py:370
  52.2 0.9 shard_map.88
  53.1 6.5 %all-to-all-start.2 = ((bf16[8,40,128]{2,1,0:T(8,128)(2,1)}), bf16[8,40,128]{2,1,0:T(8,128)(2,1)S(1)}, u32[]{:S(2)}, u32[]{:S(2)}) async-start(bf16[8,40,128]{2,1,0:T(8,128)(2,1)} %get-tuple-element.45), calls=%async_computation.2 | async-start | bytes 163840 | tf_op jit(solution)/shard_map/all_to_all | solution.py:370
  59.6 1.0 shard_map.89
  60.6 6.4 %all-to-all-done.2.sums_ref = bf16[8,40,128]{2,1,0:T(8,128)(2,1)S(1)} async-done(((bf16[8,40,128]{2,1,0:T(8,128)(2,1)}), bf16[8,40,128]{2,1,0:T(8,128)(2,1)S(1)}, u32[]{:S(2)}, u32[]{:S(2)}) %all-to-all-start.2) | async-done | bytes 81952 | tf_op jit(solution)/shard_map/all_to_all | solution.py:370
  67.3 13.1 %all_to_all.36.sums_ref = bf16[8,16,128]{2,1,0:T(8,128)(2,1)S(1)} all-to-all(bf16[8,16,128]{2,1,0:T(8,128)(2,1)S(1)} %get-tuple-element.50), channel_id=1, replica_groups=mesh['ctx_0'=8,'ctx_1'=4,'ctx_2'=2,'fsdp'=8,'batch'=2] {'ctx_1','ctx_2'}, dimensions={0} | all-to-all | bytes 65536 | tf_op jit(solution)/shard_map/all_to_all | solution.py:370
  80.5 0.9 shard_map.91
  81.4 3.4 %all-to-all-start.4 = ((bf16[8,40,128]{2,1,0:T(8,128)(2,1)}), bf16[8,40,128]{2,1,0:T(8,128)(2,1)S(1)}, u32[]{:S(2)}, u32[]{:S(2)}) async-start(bf16[8,40,128]{2,1,0:T(8,128)(2,1)} %get-tuple-element.52), calls=%async_computation.4 | async-start | bytes 163840 | tf_op jit(solution)/shard_map/all_to_all | solution.py:370
  84.7 1.7 %shard_map.92 = (f32[8,32,160]{2,1,0:T(8,128)S(1)}, f32[8,32,128]{2,1,0:T(8,128)S(1)}, f32[8,32,128]{2,1,0:T(8,128)S(1)}) custom-call(bf16[8,96,128]{2,1,0:T(8,128)(2,1)S(1)} %all_to_all.35.in_ref, bf16[8,32,128]{2,1,0:T(8,128)(2,1)S(1)} %get-tuple-element.53.dmix_ref, bf16[8,32,160]{2,1,0:T(8,128)(2,1)S(1)} %get-tuple-element.54.prior_ref, ...), custom_call_target="tpu_custom_call" | custom-call | flops 37748736 | bytes 1097728 | tf_op jit(solution)/shard_map/pallas_call | solution.py:37
  86.4 5.6 %all-to-all-done.4.sums_ref = bf16[8,40,128]{2,1,0:T(8,128)(2,1)S(1)} async-done(((bf16[8,40,128]{2,1,0:T(8,128)(2,1)}), bf16[8,40,128]{2,1,0:T(8,128)(2,1)S(1)}, u32[]{:S(2)}, u32[]{:S(2)}) %all-to-all-start.4) | async-done | bytes 81952 | tf_op jit(solution)/shard_map/all_to_all | solution.py:370
  92.5 13.6 %all_to_all.37.sums_ref.in_ref = bf16[8,128,128]{2,1,0:T(8,128)(2,1)S(1)} all-to-all(bf16[8,128,128]{2,1,0:T(8,128)(2,1)S(1)} %shard_map.93), channel_id=1, replica_groups=mesh['ctx_0'=8,'ctx_1'=4,'ctx_2'=2,'fsdp'=8,'batch'=2] {'ctx_1','ctx_2'}, dimensions={0} | all-to-all | bytes 524288 | tf_op jit(solution)/shard_map/all_to_all | solution.py:370
  106.1 1.2 shard_map.94
  107.3 5.3 %all-to-all-start.6 = ((bf16[64,8,128]{2,1,0:T(8,128)(2,1)}), bf16[64,8,128]{2,1,0:T(8,128)(2,1)S(1)}, u32[]{:S(2)}, u32[]{:S(2)}) async-start(bf16[64,8,128]{2,1,0:T(8,128)(2,1)} %shard_map.94), calls=%async_computation.6 | async-start | bytes 262144 | tf_op jit(solution)/shard_map/all_to_all | solution.py:370
  112.6 0.8 shard_map.95
  113.4 4.6 %collective-permute-start.2 = (f32[8,256]{1,0:T(8,128)S(1)}, f32[8,256]{1,0:T(8,128)S(1)}, u32[]{:S(2)}, u32[]{:S(2)}) collective-permute-start(f32[8,256]{1,0:T(8,128)S(1)} %get-tuple-element.64), channel_id=1, source_target_pairs={{16,0},{32,16},{48,32},{64,48},{80,64},{96,80},{112,96},{128,112},... | collective-permute-start | bytes 24584 | tf_op jit(solution)/shard_map/ppermute | solution.py:362
  118.0 3.7 %collective-permute-done.2.next_ref = f32[8,256]{1,0:T(8,128)S(1)} collective-permute-done((f32[8,256]{1,0:T(8,128)S(1)}, f32[8,256]{1,0:T(8,128)S(1)}, u32[]{:S(2)}, u32[]{:S(2)}) %collective-permute-start.2) | collective-permute-done | bytes 8224 | tf_op jit(solution)/shard_map/ppermute | solution.py:362
  122.3 1.8 %all-to-all-done.6.a = bf16[64,8,128]{2,1,0:T(8,128)(2,1)S(1)} async-done(((bf16[64,8,128]{2,1,0:T(8,128)(2,1)}), bf16[64,8,128]{2,1,0:T(8,128)(2,1)S(1)}, u32[]{:S(2)}, u32[]{:S(2)}) %all-to-all-start.6) | async-done | bytes 131104 | tf_op jit(solution)/shard_map/all_to_all | solution.py:370
  124.1 0.8 shard_map.97
  (19 shorter events, 2.6 us)
Async XLA Ops:
  0.6 30.2 %copy-start = (bf16[1,128,4096]{2,1,0:T(8,128)(2,1)S(1)}, bf16[1,128,4096]{2,1,0:T(8,128)(2,1)}, u32[]{:S(2)}) copy-start(bf16[1,128,4096]{2,1,0:T(8,128)(2,1)} %param.6) | copy-start | bytes 3145732
  2.9 17.4 %copy-start.4 = (bf16[8,4352]{1,0:T(8,128)(2,1)S(1)}, bf16[8,4352]{1,0:T(8,128)(2,1)}, u32[]{:S(2)}) copy-start(bf16[8,4352]{1,0:T(8,128)(2,1)} %get-tuple-element.34) | copy-start | bytes 208900
  2.9 24.0 %copy-start.1 = (f32[232,256]{1,0:T(8,128)S(1)}, f32[232,256]{1,0:T(8,128)}, u32[]{:S(2)}) copy-start(f32[232,256]{1,0:T(8,128)} %get-tuple-element.36.val_ref) | copy-start | bytes 712708
  2.9 24.0 %copy-start.2 = (bf16[128,256]{1,0:T(8,128)(2,1)S(1)}, bf16[128,256]{1,0:T(8,128)(2,1)}, u32[]{:S(2)}) copy-start(bf16[128,256]{1,0:T(8,128)(2,1)} %get-tuple-element.37.grad_ref) | copy-start | bytes 196612
  3.0 27.8 %all-to-all-start = ((bf16[8,32,512]{2,1,0:T(8,128)(2,1)}), bf16[8,32,512]{2,1,0:T(8,128)(2,1)S(1)}, u32[]{:S(2)}, u32[]{:S(2)}) async-start(bf16[8,32,512]{2,1,0:T(8,128)(2,1)} %get-tuple-element.35), calls=%async_computation | async-start | bytes 524288 | tf_op jit(solution)/shard_map/all_to_all | solution.py:370
  20.3 6.6 %collective-permute-start = (bf16[8,4352]{1,0:T(8,128)(2,1)S(1)}, bf16[8,4352]{1,0:T(8,128)(2,1)S(1)}, u32[]{:S(2)}, u32[]{:S(2)}) collective-permute-start(bf16[8,4352]{1,0:T(8,128)(2,1)S(1)} %copy-done.4), channel_id=1, source_target_pairs={{0,16},{16,32},{32,48},{48,64},{64,80},{80,96},{96,112},{112,128},... | collective-permute-start | bytes 208904 | tf_op jit(solution)/shard_map/ppermute | solution.py:362
  31.8 20.4 %collective-permute-start.1 = (bf16[136,2048]{1,0:T(8,128)(2,1)S(1)}, bf16[136,2048]{1,0:T(8,128)(2,1)S(1)}, u32[]{:S(2)}, u32[]{:S(2)}) collective-permute-start(bf16[136,2048]{1,0:T(8,128)(2,1)S(1)} %get-tuple-element.43), channel_id=1, source_target_pairs={{0,16},{16,0},{1,17},{17,1},{2,18},{18,2},{3,19},{19,3},{4,20},{20... | collective-permute-start | bytes 1671176 | tf_op jit(solution)/shard_map/ppermute | solution.py:366
  53.1 13.9 %all-to-all-start.2 = ((bf16[8,40,128]{2,1,0:T(8,128)(2,1)}), bf16[8,40,128]{2,1,0:T(8,128)(2,1)S(1)}, u32[]{:S(2)}, u32[]{:S(2)}) async-start(bf16[8,40,128]{2,1,0:T(8,128)(2,1)} %get-tuple-element.45), calls=%async_computation.2 | async-start | bytes 163840 | tf_op jit(solution)/shard_map/all_to_all | solution.py:370
  81.4 10.7 %all-to-all-start.4 = ((bf16[8,40,128]{2,1,0:T(8,128)(2,1)}), bf16[8,40,128]{2,1,0:T(8,128)(2,1)S(1)}, u32[]{:S(2)}, u32[]{:S(2)}) async-start(bf16[8,40,128]{2,1,0:T(8,128)(2,1)} %get-tuple-element.52), calls=%async_computation.4 | async-start | bytes 163840 | tf_op jit(solution)/shard_map/all_to_all | solution.py:370
  107.3 5.3 %copy-start.3 = (f32[3,256]{1,0:T(4,128)S(1)}, f32[3,256]{1,0:T(4,128)}, u32[]{:S(2)}) copy-start(f32[3,256]{1,0:T(4,128)} %cv_ref.3) | copy-start | bytes 9220
  107.3 16.9 %all-to-all-start.6 = ((bf16[64,8,128]{2,1,0:T(8,128)(2,1)}), bf16[64,8,128]{2,1,0:T(8,128)(2,1)S(1)}, u32[]{:S(2)}, u32[]{:S(2)}) async-start(bf16[64,8,128]{2,1,0:T(8,128)(2,1)} %shard_map.94), calls=%async_computation.6 | async-start | bytes 262144 | tf_op jit(solution)/shard_map/all_to_all | solution.py:370
  113.4 8.3 %collective-permute-start.2 = (f32[8,256]{1,0:T(8,128)S(1)}, f32[8,256]{1,0:T(8,128)S(1)}, u32[]{:S(2)}, u32[]{:S(2)}) collective-permute-start(f32[8,256]{1,0:T(8,128)S(1)} %get-tuple-element.64), channel_id=1, source_target_pairs={{16,0},{32,16},{48,32},{64,48},{80,64},{96,80},{112,96},{128,112},... | collective-permute-start | bytes 24584 | tf_op jit(solution)/shard_map/ppermute | solution.py:362

commit v7 on v6

--- a/solution.py
+++ b/solution.py
@@ -32,7 +32,7 @@
     return lax.dot_general(a, b, (((0,), (0,)), ((), ())), preferred_element_type=F32)
 
 
-def call(body, outs, *args, flops=0):
+def call(body, outs, *args, flops=0, sent=False, scratch=()):
     moved = sum(a.size * a.dtype.itemsize for a in (*args, *outs))
     return pl.pallas_call(
         body,
@@ -40,7 +40,8 @@
         in_specs=[
             pl.BlockSpec(memory_space=pltpu.SMEM if a.dtype == jnp.int32 else pltpu.VMEM) for a in args
         ],
-        out_specs=[pl.BlockSpec(memory_space=pltpu.VMEM)] * len(outs),
+        out_specs=[pl.BlockSpec(memory_space=pl.ANY if sent else pltpu.VMEM)] * len(outs),
+        scratch_shapes=scratch,
         cost_estimate=pl.CostEstimate(flops=flops, bytes_accessed=moved, transcendentals=0),
         compiler_params=pltpu.CompilerParams(vmem_limit_bytes=8 << 20),
     )(*args)
@@ -88,10 +89,12 @@
     return total + (1.0 / 16.0) * half
 
 
-def turn_body(w_hbm, cqk_hbm, tok_hbm, val_hbm, grad_hbm, cv_hbm, out_ref, rim_ref, val_ref, grad_ref, w_buf, cqk_buf, val_buf, sems):
+def turn_body(w_hbm, cqk_hbm, tok_hbm, val_hbm, grad_hbm, cv_hbm, out_hbm, rim_ref, val_ref, grad_ref, w_buf, cqk_buf, val_buf, out_buf, sems):
     depth = tok_hbm.shape[1]
+    half = w_hbm.shape[0] // 2
     pairs = (
-        (w_hbm, w_buf),
+        (w_hbm.at[:half], w_buf.at[:half]),
+        (w_hbm.at[half:], w_buf.at[half:]),
         (cqk_hbm, cqk_buf),
         (tok_hbm.at[POS - 8 :], rim_ref.at[:, :depth]),
         (val_hbm.at[POS - 8 :], rim_ref.at[:, depth:]),
@@ -102,11 +105,17 @@
     copies = [pltpu.make_async_copy(source, target, sems.at[k]) for k, (source, target) in enumerate(pairs)]
     for copy in copies:
         copy.start()
-    copies[0].wait()
-    turned = nt(eye(w_buf.shape[1]), w_buf[...]).astype(BF)
-    for part in range(out_ref.shape[0]):
-        out_ref[part] = turned[32 * part : 32 * part + 32]
-    copies[1].wait()
+    square = eye(w_buf.shape[1])
+    sent = []
+    for k in range(2):
+        at = slice(half * k, half * k + half)
+        copies[k].wait()
+        turned = nt(square, w_buf[at]).astype(BF)
+        for part in range(out_buf.shape[0]):
+            out_buf[part, :, at] = turned[32 * part : 32 * part + 32]
+        sent.append(pltpu.make_async_copy(out_buf.at[:, :, at], out_hbm.at[:, :, at], sems.at[8 + k]))
+        sent[-1].start()
+    copies[2].wait()
     width = cqk_buf.shape[1]
     row = lax.broadcasted_iota(jnp.int32, (width, width), 0)
     col = lax.broadcasted_iota(jnp.int32, (width, width), 1)
@@ -114,7 +123,7 @@
         spread = jnp.where(row == col, jnp.broadcast_to(cqk_buf[tap : tap + 1], (width, width)), 0.0)
         at = POS + 8 + width * tap
         val_ref[at : at + width, :POS] = jnp.broadcast_to(jnp.sum(spread, axis=1, keepdims=True), (width, POS))
-    for copy in copies[2:]:
+    for copy in copies[3:] + sent:
         copy.wait()
     val_ref[:POS] = val_buf[...].astype(F32)
 
@@ -136,7 +145,17 @@
     out_ref[1] = nt(square, grad_ref[...]).astype(BF)
 
 
-def spread_body(w_ref, tok_ref, htok_ref, turned_ref, cqk_ref, out_ref):
+def spread_body(w_ref, tok_ref, htok_ref, turned_ref, cqk_ref, out_hbm, conv_buf, sems):
+    peers = range(out_hbm.shape[0])
+    copies = [
+        pltpu.make_async_copy(
+            turned_ref.at[k, 32 * peer : 32 * peer + 32], out_hbm.at[peer, 32 * k : 32 * k + 32], sems.at[k, peer]
+        )
+        for k in range(2)
+        for peer in peers
+    ]
+    for copy in copies:
+        copy.start()
     parts, _, deep = w_ref.shape
     own = jnp.zeros((2 * F, POS), F32)
     rim = jnp.zeros((2 * F, htok_ref.shape[0]), F32)
@@ -150,11 +169,12 @@
     last, before = (jnp.broadcast_to(h[:, k : k + 1], x0.shape) for k in (7, 6))
     x1 = jnp.where(lane == 0, last, pltpu.roll(x0, 1, 1))
     x2 = jnp.where(lane == 0, before, jnp.where(lane == 1, last, pltpu.roll(x0, 2, 1)))
-    conv = (cqk_ref[0] * x0 + cqk_ref[1] * x1 + cqk_ref[2] * x2).astype(BF)
-    for peer in range(out_ref.shape[0]):
-        out_ref[peer, :32] = turned_ref[0, 32 * peer : 32 * peer + 32]
-        out_ref[peer, 32:64] = turned_ref[1, 32 * peer : 32 * peer + 32]
-        out_ref[peer, 64:] = conv
+    conv_buf[...] = (cqk_ref[0] * x0 + cqk_ref[1] * x1 + cqk_ref[2] * x2).astype(BF)
+    last = [pltpu.make_async_copy(conv_buf, out_hbm.at[peer, 64:], sems.at[2, peer]) for peer in peers]
+    for copy in last:
+        copy.start()
+    for copy in copies + last:
+        copy.wait()
 
 
 def pack(total):
@@ -281,7 +301,7 @@
                     refs[1][at, cols] = jnp.concatenate([left[:, 64:], right[:, 64:]], axis=1)
 
 
-def grad_body(core_ref, sums_ref, tok_ref, other_ref, cqk_ref, out_ref):
+def grad_body(core_ref, sums_ref, tok_ref, other_ref, cqk_ref, out_hbm, out_ref, sems):
     pair = sums_ref[0, : 4 * F].astype(F32)
     for peer in range(1, sums_ref.shape[0]):
         pair = pair + sums_ref[peer, : 4 * F].astype(F32)
@@ -305,6 +325,7 @@
 
     group = lax.broadcasted_iota(jnp.int32, (8, 128), 1) // 32
     chunk = 512
+    copies = []
     for start in range(0, tok_ref.shape[1], chunk):
         at = slice(start, start + chunk)
         part = nn(own_b, tok_ref[:POS, at]) + nn(other_b, other_ref[:POS, at])
@@ -317,6 +338,11 @@
                     group == 0, moved[0], jnp.where(group == 1, moved[1], jnp.where(group == 2, moved[2], moved[3]))
                 )
                 out_ref[(start + at_lane) // 32 + q] = packed.astype(out_ref.dtype)
+        tiles = slice(start // 32, (start + chunk) // 32)
+        copies.append(pltpu.make_async_copy(out_ref.at[tiles], out_hbm.at[tiles], sems.at[start // chunk]))
+        copies[-1].start()
+    for copy in copies:
+        copy.wait()
 
 
 def return_body(in_ref, cv_ref, att_ref, gval_ref, head_ref):
@@ -391,9 +417,10 @@
         turn_body,
         out_shape=fetched,
         in_specs=[pl.BlockSpec(memory_space=pltpu.HBM)] * len(sources),
-        out_specs=[pl.BlockSpec(memory_space=pltpu.VMEM)] * len(fetched),
+        out_specs=[pl.BlockSpec(memory_space=pl.ANY)] + [pl.BlockSpec(memory_space=pltpu.VMEM)] * (len(fetched) - 1),
         scratch_shapes=[
-            pltpu.VMEM(w_qk.shape, BF), pltpu.VMEM(conv_qk.shape, F32), pltpu.VMEM((POS, E), BF), pltpu.SemaphoreType.DMA((7,))
+            pltpu.VMEM(w_qk.shape, BF), pltpu.VMEM(conv_qk.shape, F32), pltpu.VMEM((POS, E), BF),
+            pltpu.VMEM((splits, 2 * F, deep), BF), pltpu.SemaphoreType.DMA((10,)),
         ],
         compiler_params=pltpu.CompilerParams(vmem_limit_bytes=60 * 1024 * 1024),
         name="turn",
@@ -407,7 +434,11 @@
         [struct((2, E, POS), BF), struct((CONV, 2 * F, POS), F32)],
         own_values, rim_values, own_grad,
     )
-    (spread,) = call(spread_body, [struct((blocks, 96, POS), BF)], weights, tokens, rim_tokens, value_rows, taps)
+    (spread,) = call(
+        spread_body, [struct((blocks, 96, POS), BF)], weights, tokens, rim_tokens, value_rows, taps,
+        sent=True,
+        scratch=[pltpu.VMEM((2 * F, POS), BF), pltpu.SemaphoreType.DMA((3, blocks))],
+    )
     whole, rim_tokens, spread = lax.optimization_barrier((tokens, rim_tokens, spread))
     slab = exchange(spread, SLAB)
     half = struct((POS + 8, depth // 2), BF)
@@ -452,7 +483,8 @@
         grad_body,
         [struct((chips, 8, 128), BF)],
         core, home, own_half, other_half, taps,
-        flops=2 * POS * depth * 2 * F,
+        flops=2 * POS * depth * 2 * F, sent=True,
+        scratch=[pltpu.VMEM((chips, 8, 128), BF), pltpu.SemaphoreType.DMA((depth // 1024,))],
     )
     arrived = exchange(grad_parts, CHIPS)
     home, _ = lax.optimization_barrier((home, grad_parts))

time: 127 us -> 128 us (level)
  no operation moved by 1% of the time
where the time goes in v7:
time: 128 us; the launch traced here: 126 us
  starting transfers between devices  46.4 us (36%)
  blocking collectives  42.8 us (33%)
  waiting for transfers between devices  22.5 us (18%)
  Pallas kernels  13.4 us (10%)
    all_to_all x3, blocking collectives, exchange(): return lax.all_to_all(value, axes, split_axis=0, concat_axis=0, tiled=True)  42.8 us
    all_to_all x4, starting transfers between devices, exchange(): return lax.all_to_all(value, axes, split_axis=0, concat_axis=0, tiled=True)  32.3 us
    all_to_all x4, waiting for transfers between devices, exchange(): return lax.all_to_all(value, axes, split_axis=0, concat_axis=0, tiled=True)  17.4 us
    pallas_call x13, Pallas kernels, call(): pl.pallas_call(body, out_shape=outs, in_specs=[pl.BlockSpec(memory_space=...  10.4 us
    ppermute x2, starting transfers between devices, to_next(): return lax.ppermute(value, axes, pairs)  9.85 us
    ppermute x2, waiting for transfers between devices, to_next(): return lax.ppermute(value, axes, pairs)  5.03 us
    ppermute x1, starting transfers between devices, swapped(): return lax.ppermute(value, 'ctx_2', [(0, 1), (1, 0)])  4.25 us
    pallas_call x1, Pallas kernels, shards(): pl.pallas_call(turn_body, out_shape=fetched, in_specs=[pl.BlockSpec(memor...  2.97 us
  transfers between devices with their start and end apart: 7, of which 6 were waited for; matrix products, arithmetic and copies ran while one was open for 0% of the time, Pallas kernels for 4%

profile of v7, /device:TPU:1, one launch (start us, length us, event | category | flops | bytes accessed | tf_op | source)
XLA Modules:
  0.0 126.0 jit_solution(2444637786734774857)
XLA Ops:
  0.6 3.0 %turn.1 = (bf16[8,32,512]{2,1,0:T(8,128)(2,1)}, bf16[8,4352]{1,0:T(8,128)(2,1)}, f32[232,256]{1,0:T(8,128)}, bf16[128,256]{1,0:T(8,128)(2,1)}) custom-call(bf16[512,256]{1,0:T(8,128)(2,1)} %w_hbm.1, f32[3,32]{1,0:T(4,128)} %cqk_hbm.1, bf16[128,4096]{1,0:T(8,128)(2,1)} %bitcast.7, bf16[128,256]{1,0:T(8,128)(2,1)} %bitcast.10, bf16[128,256]{1,0:T(8,128)(2,1)} %bitcast.11, ...), custom_call_target="tpu_custom_call" | custom-call | tf_op jit(solution)/shard_map/turn/pallas_call | solution.py:416
  3.7 17.4 %all-to-all-start = ((bf16[8,32,512]{2,1,0:T(8,128)(2,1)}), bf16[8,32,512]{2,1,0:T(8,128)(2,1)S(1)}, u32[]{:S(2)}, u32[]{:S(2)}) async-start(bf16[8,32,512]{2,1,0:T(8,128)(2,1)} %get-tuple-element.35), calls=%async_computation | async-start | bytes 524288 | tf_op jit(solution)/shard_map/all_to_all | solution.py:396
  21.0 5.3 %collective-permute-start = (bf16[8,4352]{1,0:T(8,128)(2,1)S(1)}, bf16[8,4352]{1,0:T(8,128)(2,1)S(1)}, u32[]{:S(2)}, u32[]{:S(2)}) collective-permute-start(bf16[8,4352]{1,0:T(8,128)(2,1)S(1)} %copy-done.4), channel_id=1, source_target_pairs={{0,16},{16,32},{32,48},{48,64},{64,80},{80,96},{96,112},{112,128},... | collective-permute-start | bytes 208904 | tf_op jit(solution)/shard_map/ppermute | solution.py:388
  26.3 1.3 %collective-permute-done = bf16[8,4352]{1,0:T(8,128)(2,1)S(1)} collective-permute-done((bf16[8,4352]{1,0:T(8,128)(2,1)S(1)}, bf16[8,4352]{1,0:T(8,128)(2,1)S(1)}, u32[]{:S(2)}, u32[]{:S(2)}) %collective-permute-start) | collective-permute-done | bytes 69664 | tf_op jit(solution)/shard_map/ppermute | solution.py:388
  27.9 3.6 %all-to-all-done.w_ref = bf16[8,32,512]{2,1,0:T(8,128)(2,1)S(1)} async-done(((bf16[8,32,512]{2,1,0:T(8,128)(2,1)}), bf16[8,32,512]{2,1,0:T(8,128)(2,1)S(1)}, u32[]{:S(2)}, u32[]{:S(2)}) %all-to-all-start) | async-done | bytes 262176 | tf_op jit(solution)/shard_map/all_to_all | solution.py:396
  31.5 1.1 shard_map.86
  33.0 4.3 %collective-permute-start.1 = (bf16[136,2048]{1,0:T(8,128)(2,1)S(1)}, bf16[136,2048]{1,0:T(8,128)(2,1)S(1)}, u32[]{:S(2)}, u32[]{:S(2)}) collective-permute-start(bf16[136,2048]{1,0:T(8,128)(2,1)S(1)} %get-tuple-element.43), channel_id=1, source_target_pairs={{0,16},{16,0},{1,17},{17,1},{2,18},{18,2},{3,19},{19,3},{4,20},{20... | collective-permute-start | bytes 1671176 | tf_op jit(solution)/shard_map/ppermute | solution.py:392
  37.3 16.1 %all_to_all.35.in_ref = bf16[8,96,128]{2,1,0:T(8,128)(2,1)S(1)} all-to-all(bf16[8,96,128]{2,1,0:T(8,128)(2,1)S(1)} %shard_map.86), channel_id=1, replica_groups=mesh['ctx_0'=8,'ctx_1'=4,'ctx_2'=2,'fsdp'=8,'batch'=2] {'ctx_1','ctx_2'}, dimensions={0} | all-to-all | bytes 393216 | tf_op jit(solution)/shard_map/all_to_all | solution.py:396
  53.4 0.9 shard_map.88
  54.3 6.5 %all-to-all-start.2 = ((bf16[8,40,128]{2,1,0:T(8,128)(2,1)}), bf16[8,40,128]{2,1,0:T(8,128)(2,1)S(1)}, u32[]{:S(2)}, u32[]{:S(2)}) async-start(bf16[8,40,128]{2,1,0:T(8,128)(2,1)} %get-tuple-element.45), calls=%async_computation.2 | async-start | bytes 163840 | tf_op jit(solution)/shard_map/all_to_all | solution.py:396
  60.8 1.0 shard_map.89
  61.8 6.4 %all-to-all-done.2.sums_ref = bf16[8,40,128]{2,1,0:T(8,128)(2,1)S(1)} async-done(((bf16[8,40,128]{2,1,0:T(8,128)(2,1)}), bf16[8,40,128]{2,1,0:T(8,128)(2,1)S(1)}, u32[]{:S(2)}, u32[]{:S(2)}) %all-to-all-start.2) | async-done | bytes 81952 | tf_op jit(solution)/shard_map/all_to_all | solution.py:396
  68.5 13.1 %all_to_all.36.sums_ref = bf16[8,16,128]{2,1,0:T(8,128)(2,1)S(1)} all-to-all(bf16[8,16,128]{2,1,0:T(8,128)(2,1)S(1)} %get-tuple-element.50), channel_id=1, replica_groups=mesh['ctx_0'=8,'ctx_1'=4,'ctx_2'=2,'fsdp'=8,'batch'=2] {'ctx_1','ctx_2'}, dimensions={0} | all-to-all | bytes 65536 | tf_op jit(solution)/shard_map/all_to_all | solution.py:396
  81.6 0.9 shard_map.91
  82.6 3.4 %all-to-all-start.4 = ((bf16[8,40,128]{2,1,0:T(8,128)(2,1)}), bf16[8,40,128]{2,1,0:T(8,128)(2,1)S(1)}, u32[]{:S(2)}, u32[]{:S(2)}) async-start(bf16[8,40,128]{2,1,0:T(8,128)(2,1)} %get-tuple-element.52), calls=%async_computation.4 | async-start | bytes 163840 | tf_op jit(solution)/shard_map/all_to_all | solution.py:396
  85.9 1.7 %shard_map.92 = (f32[8,32,160]{2,1,0:T(8,128)S(1)}, f32[8,32,128]{2,1,0:T(8,128)S(1)}, f32[8,32,128]{2,1,0:T(8,128)S(1)}) custom-call(bf16[8,96,128]{2,1,0:T(8,128)(2,1)S(1)} %all_to_all.35.in_ref, bf16[8,32,128]{2,1,0:T(8,128)(2,1)S(1)} %get-tuple-element.53.dmix_ref, bf16[8,32,160]{2,1,0:T(8,128)(2,1)S(1)} %get-tuple-element.54.prior_ref, ...), custom_call_target="tpu_custom_call" | custom-call | flops 37748736 | bytes 1097728 | tf_op jit(solution)/shard_map/pallas_call | solution.py:37
  87.6 5.6 %all-to-all-done.4.sums_ref = bf16[8,40,128]{2,1,0:T(8,128)(2,1)S(1)} async-done(((bf16[8,40,128]{2,1,0:T(8,128)(2,1)}), bf16[8,40,128]{2,1,0:T(8,128)(2,1)S(1)}, u32[]{:S(2)}, u32[]{:S(2)}) %all-to-all-start.4) | async-done | bytes 81952 | tf_op jit(solution)/shard_map/all_to_all | solution.py:396
  93.7 13.6 %all_to_all.37.sums_ref.in_ref = bf16[8,128,128]{2,1,0:T(8,128)(2,1)S(1)} all-to-all(bf16[8,128,128]{2,1,0:T(8,128)(2,1)S(1)} %shard_map.93), channel_id=1, replica_groups=mesh['ctx_0'=8,'ctx_1'=4,'ctx_2'=2,'fsdp'=8,'batch'=2] {'ctx_1','ctx_2'}, dimensions={0} | all-to-all | bytes 524288 | tf_op jit(solution)/shard_map/all_to_all | solution.py:396
  107.3 1.2 shard_map.94
  108.5 5.1 %all-to-all-start.6 = ((bf16[64,8,128]{2,1,0:T(8,128)(2,1)}), bf16[64,8,128]{2,1,0:T(8,128)(2,1)S(1)}, u32[]{:S(2)}, u32[]{:S(2)}) async-start(bf16[64,8,128]{2,1,0:T(8,128)(2,1)} %shard_map.94), calls=%async_computation.6 | async-start | bytes 262144 | tf_op jit(solution)/shard_map/all_to_all | solution.py:396
  113.6 0.8 shard_map.95
  114.5 4.6 %collective-permute-start.2 = (f32[8,256]{1,0:T(8,128)S(1)}, f32[8,256]{1,0:T(8,128)S(1)}, u32[]{:S(2)}, u32[]{:S(2)}) collective-permute-start(f32[8,256]{1,0:T(8,128)S(1)} %get-tuple-element.64), channel_id=1, source_target_pairs={{16,0},{32,16},{48,32},{64,48},{80,64},{96,80},{112,96},{128,112},... | collective-permute-start | bytes 24584 | tf_op jit(solution)/shard_map/ppermute | solution.py:388
  119.0 3.7 %collective-permute-done.2.next_ref = f32[8,256]{1,0:T(8,128)S(1)} collective-permute-done((f32[8,256]{1,0:T(8,128)S(1)}, f32[8,256]{1,0:T(8,128)S(1)}, u32[]{:S(2)}, u32[]{:S(2)}) %collective-permute-start.2) | collective-permute-done | bytes 8224 | tf_op jit(solution)/shard_map/ppermute | solution.py:388
  123.4 1.8 %all-to-all-done.6.a = bf16[64,8,128]{2,1,0:T(8,128)(2,1)S(1)} async-done(((bf16[64,8,128]{2,1,0:T(8,128)(2,1)}), bf16[64,8,128]{2,1,0:T(8,128)(2,1)S(1)}, u32[]{:S(2)}, u32[]{:S(2)}) %all-to-all-start.6) | async-done | bytes 131104 | tf_op jit(solution)/shard_map/all_to_all | solution.py:396
  (19 shorter events, 2.8 us)
Async XLA Ops:
  0.6 30.9 %copy-start = (bf16[1,128,4096]{2,1,0:T(8,128)(2,1)S(1)}, bf16[1,128,4096]{2,1,0:T(8,128)(2,1)}, u32[]{:S(2)}) copy-start(bf16[1,128,4096]{2,1,0:T(8,128)(2,1)} %param.6) | copy-start | bytes 3145732
  3.6 17.4 %copy-start.4 = (bf16[8,4352]{1,0:T(8,128)(2,1)S(1)}, bf16[8,4352]{1,0:T(8,128)(2,1)}, u32[]{:S(2)}) copy-start(bf16[8,4352]{1,0:T(8,128)(2,1)} %get-tuple-element.34) | copy-start | bytes 208900
  3.6 24.0 %copy-start.1 = (f32[232,256]{1,0:T(8,128)S(1)}, f32[232,256]{1,0:T(8,128)}, u32[]{:S(2)}) copy-start(f32[232,256]{1,0:T(8,128)} %get-tuple-element.36.val_ref) | copy-start | bytes 712708
  3.6 24.0 %copy-start.2 = (bf16[128,256]{1,0:T(8,128)(2,1)S(1)}, bf16[128,256]{1,0:T(8,128)(2,1)}, u32[]{:S(2)}) copy-start(bf16[128,256]{1,0:T(8,128)(2,1)} %get-tuple-element.37.grad_ref) | copy-start | bytes 196612
  3.7 27.8 %all-to-all-start = ((bf16[8,32,512]{2,1,0:T(8,128)(2,1)}), bf16[8,32,512]{2,1,0:T(8,128)(2,1)S(1)}, u32[]{:S(2)}, u32[]{:S(2)}) async-start(bf16[8,32,512]{2,1,0:T(8,128)(2,1)} %get-tuple-element.35), calls=%async_computation | async-start | bytes 524288 | tf_op jit(solution)/shard_map/all_to_all | solution.py:396
  21.0 6.6 %collective-permute-start = (bf16[8,4352]{1,0:T(8,128)(2,1)S(1)}, bf16[8,4352]{1,0:T(8,128)(2,1)S(1)}, u32[]{:S(2)}, u32[]{:S(2)}) collective-permute-start(bf16[8,4352]{1,0:T(8,128)(2,1)S(1)} %copy-done.4), channel_id=1, source_target_pairs={{0,16},{16,32},{32,48},{48,64},{64,80},{80,96},{96,112},{112,128},... | collective-permute-start | bytes 208904 | tf_op jit(solution)/shard_map/ppermute | solution.py:388
  33.0 20.3 %collective-permute-start.1 = (bf16[136,2048]{1,0:T(8,128)(2,1)S(1)}, bf16[136,2048]{1,0:T(8,128)(2,1)S(1)}, u32[]{:S(2)}, u32[]{:S(2)}) collective-permute-start(bf16[136,2048]{1,0:T(8,128)(2,1)S(1)} %get-tuple-element.43), channel_id=1, source_target_pairs={{0,16},{16,0},{1,17},{17,1},{2,18},{18,2},{3,19},{19,3},{4,20},{20... | collective-permute-start | bytes 1671176 | tf_op jit(solution)/shard_map/ppermute | solution.py:392
  54.3 13.9 %all-to-all-start.2 = ((bf16[8,40,128]{2,1,0:T(8,128)(2,1)}), bf16[8,40,128]{2,1,0:T(8,128)(2,1)S(1)}, u32[]{:S(2)}, u32[]{:S(2)}) async-start(bf16[8,40,128]{2,1,0:T(8,128)(2,1)} %get-tuple-element.45), calls=%async_computation.2 | async-start | bytes 163840 | tf_op jit(solution)/shard_map/all_to_all | solution.py:396
  82.6 10.7 %all-to-all-start.4 = ((bf16[8,40,128]{2,1,0:T(8,128)(2,1)}), bf16[8,40,128]{2,1,0:T(8,128)(2,1)S(1)}, u32[]{:S(2)}, u32[]{:S(2)}) async-start(bf16[8,40,128]{2,1,0:T(8,128)(2,1)} %get-tuple-element.52), calls=%async_computation.4 | async-start | bytes 163840 | tf_op jit(solution)/shard_map/all_to_all | solution.py:396
  108.5 5.2 %copy-start.3 = (f32[3,256]{1,0:T(4,128)S(1)}, f32[3,256]{1,0:T(4,128)}, u32[]{:S(2)}) copy-start(f32[3,256]{1,0:T(4,128)} %cv_ref.3) | copy-start | bytes 9220
  108.5 16.7 %all-to-all-start.6 = ((bf16[64,8,128]{2,1,0:T(8,128)(2,1)}), bf16[64,8,128]{2,1,0:T(8,128)(2,1)S(1)}, u32[]{:S(2)}, u32[]{:S(2)}) async-start(bf16[64,8,128]{2,1,0:T(8,128)(2,1)} %shard_map.94), calls=%async_computation.6 | async-start | bytes 262144 | tf_op jit(solution)/shard_map/all_to_all | solution.py:396
  114.5 8.3 %collective-permute-start.2 = (f32[8,256]{1,0:T(8,128)S(1)}, f32[8,256]{1,0:T(8,128)S(1)}, u32[]{:S(2)}, u32[]{:S(2)}) collective-permute-start(f32[8,256]{1,0:T(8,128)S(1)} %get-tuple-element.64), channel_id=1, source_target_pairs={{16,0},{32,16},{48,32},{64,48},{80,64},{96,80},{112,96},{128,112},... | collective-permute-start | bytes 24584 | tf_op jit(solution)/shard_map/ppermute | solution.py:388

commit v8 on v6

--- a/solution.py
+++ b/solution.py
@@ -267,7 +267,7 @@
         out_ref[b, 96:] = (dval_ref[b] + nn((later * gain).astype(BF), krows_ref[b])).astype(BF)
 
 
-def halves_body(core_ref, tok_ref, htok_ref, mine_ref, theirs_ref):
+def halves_body(core_ref, after_ref, tok_ref, htok_ref, mine_ref, theirs_ref):
     for refs, wanted in (((mine_ref, theirs_ref), 0), ((theirs_ref, mine_ref), 1)):
 
         @pl.when(core_ref[0] == wanted)
@@ -381,6 +381,7 @@
     chips = lax.axis_size(CHIPS)
     place = lax.axis_index("ctx_0").astype(jnp.int32).reshape(1)
     core = lax.axis_index("ctx_2").astype(jnp.int32).reshape(1)
+    place, core, w_qk = lax.optimization_barrier((place, core, w_qk))
 
     sources = (w_qk, conv_qk, tokens, own_values, d_attn[0], conv_v)
     fetched = [
@@ -408,14 +409,12 @@
         own_values, rim_values, own_grad,
     )
     (spread,) = call(spread_body, [struct((blocks, 96, POS), BF)], weights, tokens, rim_tokens, value_rows, taps)
-    whole, rim_tokens, spread = lax.optimization_barrier((tokens, rim_tokens, spread))
     slab = exchange(spread, SLAB)
-    half = struct((POS + 8, depth // 2), BF)
-    own_half, sent = call(halves_body, [half, half], core, whole, rim_tokens)
-    other_half = swapped(sent)
-    slab, other_half = lax.optimization_barrier((slab, other_half))
     k_rows, state = call(state_body, [struct((blocks, ROWS, POS), BF), struct((lines, 40, POS), BF)], slab)
     states = exchange(state, "ctx_0")
+    half = struct((POS + 8, depth // 2), BF)
+    own_half, sent = call(halves_body, [half, half], core, k_rows, tokens, rim_tokens)
+    other_half = swapped(sent)
     before, mixed_own, q_rows = call(
         local_body,
         [
@@ -424,6 +423,7 @@
         slab, k_rows,
         flops=2 * blocks * POS * POS * 48,
     )
+    other_half, mixed_own = lax.optimization_barrier((other_half, mixed_own))
     mixed, prior, norm = call(
         mix_body,
         [struct((blocks, 32, POS), F32), struct((blocks, 32, ROWS), BF), struct((blocks, 2 * blocks, POS), BF)],

time: 127 us -> 127 us (level)
  no operation moved by 1% of the time
where the time goes in v8:
time: 127 us; the launch traced here: 125 us
  starting transfers between devices  46.4 us (37%)
  blocking collectives  43.2 us (34%)
  waiting for transfers between devices  22.4 us (18%)
  Pallas kernels  12.2 us (10%)
    all_to_all x3, blocking collectives, exchange(): return lax.all_to_all(value, axes, split_axis=0, concat_axis=0, tiled=True)  43.2 us
    all_to_all x4, starting transfers between devices, exchange(): return lax.all_to_all(value, axes, split_axis=0, concat_axis=0, tiled=True)  32.5 us
    all_to_all x4, waiting for transfers between devices, exchange(): return lax.all_to_all(value, axes, split_axis=0, concat_axis=0, tiled=True)  17.3 us
    pallas_call x13, Pallas kernels, call(): pl.pallas_call(body, out_shape=outs, in_specs=[pl.BlockSpec(memory_space=...  9.91 us
    ppermute x2, starting transfers between devices, to_next(): return lax.ppermute(value, axes, pairs)  9.84 us
    ppermute x2, waiting for transfers between devices, to_next(): return lax.ppermute(value, axes, pairs)  5.04 us
    ppermute x1, starting transfers between devices, swapped(): return lax.ppermute(value, 'ctx_2', [(0, 1), (1, 0)])  4.04 us
  transfers between devices with their start and end apart: 7, of which 6 were waited for; matrix products, arithmetic and copies ran while one was open for 0% of the time, Pallas kernels for 4%

profile of v8, /device:TPU:1, one launch (start us, length us, event | category | flops | bytes accessed | tf_op | source)
XLA Modules:
  0.0 124.9 jit_solution(14930060491088064977)
XLA Ops:
  0.6 2.3 %turn.1 = (bf16[8,32,512]{2,1,0:T(8,128)(2,1)}, bf16[8,4352]{1,0:T(8,128)(2,1)}, f32[232,256]{1,0:T(8,128)}, bf16[128,256]{1,0:T(8,128)(2,1)}) custom-call(bf16[512,256]{1,0:T(8,128)(2,1)} %w_hbm, f32[3,32]{1,0:T(4,128)} %cqk_hbm.1, bf16[128,4096]{1,0:T(8,128)(2,1)} %bitcast.7, bf16[128,256]{1,0:T(8,128)(2,1)} %bitcast.10, bf16[128,256]{1,0:T(8,128)(2,1)} %bitcast.11, ...), custom_call_target="tpu_custom_call" | custom-call | tf_op jit(solution)/shard_map/turn/pallas_call | solution.py:391
  3.0 17.4 %all-to-all-start = ((bf16[8,32,512]{2,1,0:T(8,128)(2,1)}), bf16[8,32,512]{2,1,0:T(8,128)(2,1)S(1)}, u32[]{:S(2)}, u32[]{:S(2)}) async-start(bf16[8,32,512]{2,1,0:T(8,128)(2,1)} %get-tuple-element.36), calls=%async_computation | async-start | bytes 524288 | tf_op jit(solution)/shard_map/all_to_all | solution.py:370
  20.3 5.3 %collective-permute-start = (bf16[8,4352]{1,0:T(8,128)(2,1)S(1)}, bf16[8,4352]{1,0:T(8,128)(2,1)S(1)}, u32[]{:S(2)}, u32[]{:S(2)}) collective-permute-start(bf16[8,4352]{1,0:T(8,128)(2,1)S(1)} %copy-done.4), channel_id=1, source_target_pairs={{0,16},{16,32},{32,48},{48,64},{64,80},{80,96},{96,112},{112,128},... | collective-permute-start | bytes 208904 | tf_op jit(solution)/shard_map/ppermute | solution.py:362
  25.6 1.3 %collective-permute-done = bf16[8,4352]{1,0:T(8,128)(2,1)S(1)} collective-permute-done((bf16[8,4352]{1,0:T(8,128)(2,1)S(1)}, bf16[8,4352]{1,0:T(8,128)(2,1)S(1)}, u32[]{:S(2)}, u32[]{:S(2)}) %collective-permute-start) | collective-permute-done | bytes 69664 | tf_op jit(solution)/shard_map/ppermute | solution.py:362
  27.2 3.6 %all-to-all-done.w_ref = bf16[8,32,512]{2,1,0:T(8,128)(2,1)S(1)} async-done(((bf16[8,32,512]{2,1,0:T(8,128)(2,1)}), bf16[8,32,512]{2,1,0:T(8,128)(2,1)S(1)}, u32[]{:S(2)}, u32[]{:S(2)}) %all-to-all-start) | async-done | bytes 262176 | tf_op jit(solution)/shard_map/all_to_all | solution.py:370
  31.4 18.3 %all_to_all.35.in_ref = bf16[8,96,128]{2,1,0:T(8,128)(2,1)S(1)} all-to-all(bf16[8,96,128]{2,1,0:T(8,128)(2,1)S(1)} %shard_map.86), channel_id=1, replica_groups=mesh['ctx_0'=8,'ctx_1'=4,'ctx_2'=2,'fsdp'=8,'batch'=2] {'ctx_1','ctx_2'}, dimensions={0} | all-to-all | bytes 393216 | tf_op jit(solution)/shard_map/all_to_all | solution.py:370
  49.7 0.9 shard_map.87
  51.1 4.0 %collective-permute-start.1 = (bf16[136,2048]{1,0:T(8,128)(2,1)S(1)}, bf16[136,2048]{1,0:T(8,128)(2,1)S(1)}, u32[]{:S(2)}, u32[]{:S(2)}) collective-permute-start(bf16[136,2048]{1,0:T(8,128)(2,1)S(1)} %get-tuple-element.46), channel_id=1, source_target_pairs={{0,16},{16,0},{1,17},{17,1},{2,18},{18,2},{3,19},{19,3},{4,20},{20... | collective-permute-start | bytes 1671176 | tf_op jit(solution)/shard_map/ppermute | solution.py:366
  55.1 6.5 %all-to-all-start.2 = ((bf16[8,40,128]{2,1,0:T(8,128)(2,1)}), bf16[8,40,128]{2,1,0:T(8,128)(2,1)S(1)}, u32[]{:S(2)}, u32[]{:S(2)}) async-start(bf16[8,40,128]{2,1,0:T(8,128)(2,1)} %get-tuple-element.42), calls=%async_computation.2 | async-start | bytes 163840 | tf_op jit(solution)/shard_map/all_to_all | solution.py:370
  61.6 1.0 shard_map.88
  62.6 6.3 %all-to-all-done.2.sums_ref = bf16[8,40,128]{2,1,0:T(8,128)(2,1)S(1)} async-done(((bf16[8,40,128]{2,1,0:T(8,128)(2,1)}), bf16[8,40,128]{2,1,0:T(8,128)(2,1)S(1)}, u32[]{:S(2)}, u32[]{:S(2)}) %all-to-all-start.2) | async-done | bytes 81952 | tf_op jit(solution)/shard_map/all_to_all | solution.py:370
  69.3 11.2 %all_to_all.36.sums_ref = bf16[8,16,128]{2,1,0:T(8,128)(2,1)S(1)} all-to-all(bf16[8,16,128]{2,1,0:T(8,128)(2,1)S(1)} %get-tuple-element.50), channel_id=1, replica_groups=mesh['ctx_0'=8,'ctx_1'=4,'ctx_2'=2,'fsdp'=8,'batch'=2] {'ctx_1','ctx_2'}, dimensions={0} | all-to-all | bytes 65536 | tf_op jit(solution)/shard_map/all_to_all | solution.py:370
  80.5 0.9 shard_map.91
  81.4 3.4 %all-to-all-start.4 = ((bf16[8,40,128]{2,1,0:T(8,128)(2,1)}), bf16[8,40,128]{2,1,0:T(8,128)(2,1)S(1)}, u32[]{:S(2)}, u32[]{:S(2)}) async-start(bf16[8,40,128]{2,1,0:T(8,128)(2,1)} %get-tuple-element.52), calls=%async_computation.4 | async-start | bytes 163840 | tf_op jit(solution)/shard_map/all_to_all | solution.py:370
  84.8 1.7 %shard_map.92 = (f32[8,32,160]{2,1,0:T(8,128)S(1)}, f32[8,32,128]{2,1,0:T(8,128)S(1)}, f32[8,32,128]{2,1,0:T(8,128)S(1)}) custom-call(bf16[8,96,128]{2,1,0:T(8,128)(2,1)S(1)} %all_to_all.35.in_ref, bf16[8,32,128]{2,1,0:T(8,128)(2,1)S(1)} %get-tuple-element.53.dmix_ref, bf16[8,32,160]{2,1,0:T(8,128)(2,1)S(1)} %get-tuple-element.54.prior_ref, ...), custom_call_target="tpu_custom_call" | custom-call | flops 37748736 | bytes 1097728 | tf_op jit(solution)/shard_map/pallas_call | solution.py:37
  86.5 5.6 %all-to-all-done.4.sums_ref = bf16[8,40,128]{2,1,0:T(8,128)(2,1)S(1)} async-done(((bf16[8,40,128]{2,1,0:T(8,128)(2,1)}), bf16[8,40,128]{2,1,0:T(8,128)(2,1)S(1)}, u32[]{:S(2)}, u32[]{:S(2)}) %all-to-all-start.4) | async-done | bytes 81952 | tf_op jit(solution)/shard_map/all_to_all | solution.py:370
  92.5 13.6 %all_to_all.37.sums_ref.in_ref = bf16[8,128,128]{2,1,0:T(8,128)(2,1)S(1)} all-to-all(bf16[8,128,128]{2,1,0:T(8,128)(2,1)S(1)} %shard_map.93), channel_id=1, replica_groups=mesh['ctx_0'=8,'ctx_1'=4,'ctx_2'=2,'fsdp'=8,'batch'=2] {'ctx_1','ctx_2'}, dimensions={0} | all-to-all | bytes 524288 | tf_op jit(solution)/shard_map/all_to_all | solution.py:370
  106.1 1.2 shard_map.94
  107.3 5.3 %all-to-all-start.6 = ((bf16[64,8,128]{2,1,0:T(8,128)(2,1)}), bf16[64,8,128]{2,1,0:T(8,128)(2,1)S(1)}, u32[]{:S(2)}, u32[]{:S(2)}) async-start(bf16[64,8,128]{2,1,0:T(8,128)(2,1)} %shard_map.94), calls=%async_computation.6 | async-start | bytes 262144 | tf_op jit(solution)/shard_map/all_to_all | solution.py:370
  112.6 0.8 shard_map.95
  113.4 4.6 %collective-permute-start.2 = (f32[8,256]{1,0:T(8,128)S(1)}, f32[8,256]{1,0:T(8,128)S(1)}, u32[]{:S(2)}, u32[]{:S(2)}) collective-permute-start(f32[8,256]{1,0:T(8,128)S(1)} %get-tuple-element.64), channel_id=1, source_target_pairs={{16,0},{32,16},{48,32},{64,48},{80,64},{96,80},{112,96},{128,112},... | collective-permute-start | bytes 24584 | tf_op jit(solution)/shard_map/ppermute | solution.py:362
  118.0 3.7 %collective-permute-done.2.next_ref = f32[8,256]{1,0:T(8,128)S(1)} collective-permute-done((f32[8,256]{1,0:T(8,128)S(1)}, f32[8,256]{1,0:T(8,128)S(1)}, u32[]{:S(2)}, u32[]{:S(2)}) %collective-permute-start.2) | collective-permute-done | bytes 8224 | tf_op jit(solution)/shard_map/ppermute | solution.py:362
  122.3 1.8 %all-to-all-done.6.a = bf16[64,8,128]{2,1,0:T(8,128)(2,1)S(1)} async-done(((bf16[64,8,128]{2,1,0:T(8,128)(2,1)}), bf16[64,8,128]{2,1,0:T(8,128)(2,1)S(1)}, u32[]{:S(2)}, u32[]{:S(2)}) %all-to-all-start.6) | async-done | bytes 131104 | tf_op jit(solution)/shard_map/all_to_all | solution.py:370
  124.2 0.8 shard_map.97
  (19 shorter events, 2.6 us)
Async XLA Ops:
  0.6 30.2 %copy-start = (bf16[1,128,4096]{2,1,0:T(8,128)(2,1)S(1)}, bf16[1,128,4096]{2,1,0:T(8,128)(2,1)}, u32[]{:S(2)}) copy-start(bf16[1,128,4096]{2,1,0:T(8,128)(2,1)} %param.6) | copy-start | bytes 3145732
  2.9 17.4 %copy-start.4 = (bf16[8,4352]{1,0:T(8,128)(2,1)S(1)}, bf16[8,4352]{1,0:T(8,128)(2,1)}, u32[]{:S(2)}) copy-start(bf16[8,4352]{1,0:T(8,128)(2,1)} %get-tuple-element.37) | copy-start | bytes 208900
  3.0 24.0 %copy-start.1 = (f32[232,256]{1,0:T(8,128)S(1)}, f32[232,256]{1,0:T(8,128)}, u32[]{:S(2)}) copy-start(f32[232,256]{1,0:T(8,128)} %get-tuple-element.38.val_ref) | copy-start | bytes 712708
  3.0 24.0 %copy-start.2 = (bf16[128,256]{1,0:T(8,128)(2,1)S(1)}, bf16[128,256]{1,0:T(8,128)(2,1)}, u32[]{:S(2)}) copy-start(bf16[128,256]{1,0:T(8,128)(2,1)} %get-tuple-element.39.grad_ref) | copy-start | bytes 196612
  3.0 27.8 %all-to-all-start = ((bf16[8,32,512]{2,1,0:T(8,128)(2,1)}), bf16[8,32,512]{2,1,0:T(8,128)(2,1)S(1)}, u32[]{:S(2)}, u32[]{:S(2)}) async-start(bf16[8,32,512]{2,1,0:T(8,128)(2,1)} %get-tuple-element.36), calls=%async_computation | async-start | bytes 524288 | tf_op jit(solution)/shard_map/all_to_all | solution.py:370
  20.3 6.6 %collective-permute-start = (bf16[8,4352]{1,0:T(8,128)(2,1)S(1)}, bf16[8,4352]{1,0:T(8,128)(2,1)S(1)}, u32[]{:S(2)}, u32[]{:S(2)}) collective-permute-start(bf16[8,4352]{1,0:T(8,128)(2,1)S(1)} %copy-done.4), channel_id=1, source_target_pairs={{0,16},{16,32},{32,48},{48,64},{64,80},{80,96},{96,112},{112,128},... | collective-permute-start | bytes 208904 | tf_op jit(solution)/shard_map/ppermute | solution.py:362
  51.1 11.6 %collective-permute-start.1 = (bf16[136,2048]{1,0:T(8,128)(2,1)S(1)}, bf16[136,2048]{1,0:T(8,128)(2,1)S(1)}, u32[]{:S(2)}, u32[]{:S(2)}) collective-permute-start(bf16[136,2048]{1,0:T(8,128)(2,1)S(1)} %get-tuple-element.46), channel_id=1, source_target_pairs={{0,16},{16,0},{1,17},{17,1},{2,18},{18,2},{3,19},{19,3},{4,20},{20... | collective-permute-start | bytes 1671176 | tf_op jit(solution)/shard_map/ppermute | solution.py:366
  55.1 13.8 %all-to-all-start.2 = ((bf16[8,40,128]{2,1,0:T(8,128)(2,1)}), bf16[8,40,128]{2,1,0:T(8,128)(2,1)S(1)}, u32[]{:S(2)}, u32[]{:S(2)}) async-start(bf16[8,40,128]{2,1,0:T(8,128)(2,1)} %get-tuple-element.42), calls=%async_computation.2 | async-start | bytes 163840 | tf_op jit(solution)/shard_map/all_to_all | solution.py:370
  81.4 10.7 %all-to-all-start.4 = ((bf16[8,40,128]{2,1,0:T(8,128)(2,1)}), bf16[8,40,128]{2,1,0:T(8,128)(2,1)S(1)}, u32[]{:S(2)}, u32[]{:S(2)}) async-start(bf16[8,40,128]{2,1,0:T(8,128)(2,1)} %get-tuple-element.52), calls=%async_computation.4 | async-start | bytes 163840 | tf_op jit(solution)/shard_map/all_to_all | solution.py:370
  107.3 5.3 %copy-start.3 = (f32[3,256]{1,0:T(4,128)S(1)}, f32[3,256]{1,0:T(4,128)}, u32[]{:S(2)}) copy-start(f32[3,256]{1,0:T(4,128)} %cv_ref.3) | copy-start | bytes 9220
  107.3 16.8 %all-to-all-start.6 = ((bf16[64,8,128]{2,1,0:T(8,128)(2,1)}), bf16[64,8,128]{2,1,0:T(8,128)(2,1)S(1)}, u32[]{:S(2)}, u32[]{:S(2)}) async-start(bf16[64,8,128]{2,1,0:T(8,128)(2,1)} %shard_map.94), calls=%async_computation.6 | async-start | bytes 262144 | tf_op jit(solution)/shard_map/all_to_all | solution.py:370
  113.4 8.3 %collective-permute-start.2 = (f32[8,256]{1,0:T(8,128)S(1)}, f32[8,256]{1,0:T(8,128)S(1)}, u32[]{:S(2)}, u32[]{:S(2)}) collective-permute-start(f32[8,256]{1,0:T(8,128)S(1)} %get-tuple-element.64), channel_id=1, source_target_pairs={{16,0},{32,16},{48,32},{64,48},{80,64},{96,80},{112,96},{128,112},... | collective-permute-start | bytes 24584 | tf_op jit(solution)/shard_map/ppermute | solution.py:362
